TPU v7x, 32 devices: a whole 2x2x4 slice. The times are simulated.
32 devices in a mesh: parts: 2 (over y), slab: 8 (over z, x), sub: 2 (over core).
Axes of the slice: x: 2, y: 2, z: 4, core: 2. Of those that a mesh axis runs over, the one named last changes fastest.
Arguments:
- node_feat: bfloat16 [16384, 512], P(('parts', 'slab', 'sub')), parts along dimension 0, may hold values from -6 to 6
- self_weight: bfloat16 [512, 512], replicated, may hold values from -0.25 to 0.25
- neigh_weight: bfloat16 [512, 512], replicated, may hold values from -0.25 to 0.25
- block_tiles: bfloat16 [128, 3, 6, 128, 128], P(('parts', 'slab', 'sub')), parts along dimension 0, may hold values from -6 to 6
- source_block: int32 [128, 3, 6], P(('parts', 'slab', 'sub')), parts along dimension 0, may hold values from 0 to 7
- edge_counts: int32 [128, 3, 6], P(('parts', 'slab', 'sub')), parts along dimension 0, may hold values from 0 to 128
- normalizer: int32 [16384], P(('parts', 'slab', 'sub')), parts along dimension 0, may hold values from 16 to 64
- cotangent: bfloat16 [16384, 512], P(('parts', 'slab', 'sub')), parts along dimension 0, may hold values from -6 to 6
Outputs:
- node_out: bfloat16 [16384, 512], P(('parts', 'slab', 'sub')), parts along dimension 0
- node_grad: bfloat16 [16384, 512], P(('parts', 'slab', 'sub')), parts along dimension 0
There are 2 independent parts, one for each index of `parts`. A program takes and returns all parts, laid end to end along the dimension named above; an argument that names none is the same for every part. Nothing has to cross between parts.
Inputs may be any that keep to these rules, and one draw needn't show every extreme that they name: `edge_counts`: A slot with edge count 0 adds nothing.
All inputs are finite; a program needn't handle non-finite values.
Results may differ from a plain program's by a relative error of at most 0.01.
Values may be sent and summed in bfloat16 or wider, within the bound.
No kernel may reach another device: no remote copies, remote signals or barrier semaphores. Data moves between devices by JAX's collectives and lax.ppermute only.
A program may use at most 64 MiB of HBM per device.

v0:
```python
import jax
import jax.numpy as jnp
from jax import lax
from jax.sharding import PartitionSpec as P


def shifted(block, axis, distance):
    devices = range(lax.axis_size(axis))
    route = [((i - distance) % len(devices), i) for i in devices]
    return lax.ppermute(block, axis, route)


def weighted_tiles(block_tiles, edge_counts):
    scale = edge_counts.astype(jnp.float32) / block_tiles.shape[-1]
    return (block_tiles.astype(jnp.float32) * scale[..., None, None]).astype(jnp.bfloat16)


def silu_grad(pre_act):
    logistic = jax.nn.sigmoid(pre_act)
    return logistic * (1.0 + pre_act * (1.0 - logistic))


def per_device(
    node_feat,
    self_weight,
    neigh_weight,
    block_tiles,
    source_block,
    edge_counts,
    normalizer,
    cotangent,
):
    row_count = node_feat.shape[0]
    feat_width = node_feat.shape[1]
    block_size = block_tiles.shape[-1]
    slot_count = block_tiles.shape[2]
    local_blocks = row_count // block_size
    weighted = weighted_tiles(block_tiles, edge_counts)
    prev_half = shifted(node_feat, "slab", 1)
    next_half = shifted(node_feat, "slab", -1)
    prev_slab, own_slab, next_slab = (
        lax.all_gather(prev_half, "sub", axis=0, tiled=True),
        lax.all_gather(node_feat, "sub", axis=0, tiled=True),
        lax.all_gather(next_half, "sub", axis=0, tiled=True),
    )
    slab_blocks = own_slab.shape[0] // block_size
    flat_slabs = jnp.concatenate([prev_slab, own_slab, next_slab], axis=0).reshape(
        3 * slab_blocks, block_size, feat_width
    )
    offsets = (jnp.arange(3, dtype=jnp.int32) * slab_blocks)[None, :, None]
    block_index = (source_block + offsets).reshape(local_blocks, 3 * slot_count)
    gathered = jnp.take(flat_slabs, block_index, axis=0)
    flat_tiles = weighted.reshape(local_blocks, 3 * slot_count, block_size, block_size)
    messages = jnp.einsum(
        "bkij,bkjf->bif", flat_tiles, gathered, preferred_element_type=jnp.float32
    )
    scale_rows = normalizer.astype(jnp.float32)[:, None]
    aggregate = (messages.reshape(row_count, feat_width) / scale_rows).astype(jnp.bfloat16)
    pre_act = jnp.dot(node_feat, self_weight, preferred_element_type=jnp.float32) + jnp.dot(
        aggregate, neigh_weight, preferred_element_type=jnp.float32
    )
    node_out = jax.nn.silu(pre_act).astype(jnp.bfloat16)
    pre_grad = (cotangent.astype(jnp.float32) * silu_grad(pre_act)).astype(jnp.bfloat16)
    contract = (((1,), (1,)), ((), ()))
    agg_grad = (
        lax.dot_general(pre_grad, neigh_weight, contract, preferred_element_type=jnp.float32)
        / scale_rows
    ).astype(jnp.bfloat16)
    grad_blocks = agg_grad.reshape(local_blocks, block_size, feat_width)
    block_ids = jnp.arange(slab_blocks, dtype=jnp.int32)
    partials = []
    for offset in range(3):
        spread = jnp.einsum(
            "bkij,bif->bkjf", weighted[:, offset], grad_blocks, preferred_element_type=jnp.float32
        )
        selector = (source_block[:, offset][..., None] == block_ids).astype(jnp.float32)
        placed = jnp.einsum("bkq,bkjf->qjf", selector, spread)
        partials.append(placed.reshape(slab_blocks * block_size, feat_width).astype(jnp.bfloat16))
    to_prev = shifted(partials[0], "slab", -1)
    to_next = shifted(partials[2], "slab", 1)
    summed = (
        partials[1].astype(jnp.float32) + to_prev.astype(jnp.float32) + to_next.astype(jnp.float32)
    )
    returned = lax.psum_scatter(
        summed.astype(jnp.bfloat16), "sub", scatter_dimension=0, tiled=True
    ).astype(jnp.float32)
    own_grad = lax.dot_general(pre_grad, self_weight, contract, preferred_element_type=jnp.float32)
    node_grad = (own_grad + returned).astype(jnp.bfloat16)
    return (node_out, node_grad)


def solution(mesh):
    return jax.shard_map(
        per_device,
        mesh=mesh,
        in_specs=(
            P(("parts", "slab", "sub"), None),
            P(),
            P(),
            P(("parts", "slab", "sub"), None, None, None, None),
            P(("parts", "slab", "sub"), None, None),
            P(("parts", "slab", "sub"), None, None),
            P(("parts", "slab", "sub")),
            P(("parts", "slab", "sub"), None),
        ),
        out_specs=(P(("parts", "slab", "sub"), None), P(("parts", "slab", "sub"), None)),
        check_vma=False,
    )
```

profile of v0, /device:TPU:0, one launch (start us, length us, event | category | flops | bytes accessed | tf_op | source)
XLA Modules:
  0.0 144.7 jit_solution(13847208391205132995)
XLA Ops:
  7.2 0.0 all-gather.6.cloned.1.call-start
  7.2 0.7 all-gather.6.cloned.1.call-update
  7.9 0.0 all-gather.4.cloned.1.call-start
  8.0 3.0 %collective-permute-start = (bf16[512,512]{1,0:T(8,128)(2,1)}, bf16[512,512]{1,0:T(8,128)(2,1)S(1)}, u32[]{:S(2)}, u32[]{:S(2)}) collective-permute-start(bf16[512,512]{1,0:T(8,128)(2,1)} %param.8), channel_id=1, source_target_pairs={{14,0},{0,2},{2,4},{4,6},{6,8},{8,10},{10,12},{12,14},{15,1},{1,3}... | collective-permute-start | bytes 1572872 | tf_op jit(solution)/shard_map/ppermute | solution.py:10
  10.9 15.2 %collective-permute-done = bf16[512,512]{1,0:T(8,128)(2,1)S(1)} collective-permute-done((bf16[512,512]{1,0:T(8,128)(2,1)}, bf16[512,512]{1,0:T(8,128)(2,1)S(1)}, u32[]{:S(2)}, u32[]{:S(2)}) %collective-permute-start) | collective-permute-done | bytes 524320 | tf_op jit(solution)/shard_map/ppermute | solution.py:10
  26.1 0.8 copy-done.3
  26.9 0.0 all-gather.8.cloned.1.call-start
  27.0 1.8 %collective-permute-start.1 = (bf16[512,512]{1,0:T(8,128)(2,1)}, bf16[512,512]{1,0:T(8,128)(2,1)S(1)}, u32[]{:S(2)}, u32[]{:S(2)}) collective-permute-start(bf16[512,512]{1,0:T(8,128)(2,1)} %param.8), channel_id=1, source_target_pairs={{2,0},{4,2},{6,4},{8,6},{10,8},{12,10},{14,12},{0,14},{3,1},{5,3},... | collective-permute-start | bytes 1572872 | tf_op jit(solution)/shard_map/ppermute | solution.py:10
  28.8 0.8 broadcast_add_fusion
  29.6 0.1 reshape.75
  29.6 0.1 reshape.73
  29.7 0.7 convert_multiply_fusion
  30.4 0.1 reshape.81
  30.5 0.7 convert_element_type.70
  31.2 9.2 %collective-permute-done.1 = bf16[512,512]{1,0:T(8,128)(2,1)S(1)} collective-permute-done((bf16[512,512]{1,0:T(8,128)(2,1)}, bf16[512,512]{1,0:T(8,128)(2,1)S(1)}, u32[]{:S(2)}, u32[]{:S(2)}) %collective-permute-start.1) | collective-permute-done | bytes 524320 | tf_op jit(solution)/shard_map/ppermute | solution.py:10
  40.4 0.8 copy-done.4
  41.2 0.0 all-gather.8.cloned.1.call-update
  41.2 0.0 reduce-scatter.2.cloned.1.call-start
  41.2 0.7 slice_bitcast_fusion.7
  42.0 2.7 %fusion.36 = f32[512,512]{1,0:T(8,128)} fusion(bf16[512,512]{1,0:T(8,128)(2,1)} %param.8, bf16[512,512]{1,0:T(8,128)(2,1)} %param.9), kind=kOutput, calls=%fused_computation.55 | convolution fusion | flops 268435456 | bytes 2097152 | tf_op jit(solution)/shard_map/dot_general | solution.py:59
  44.6 2.2 %multiply_convert_fusion = bf16[4,3,6,128,128]{4,3,2,1,0:T(8,128)(2,1)S(1)} fusion(bf16[4,3,6,128,128]{4,3,2,1,0:T(8,128)(2,1)} %param.11, f32[4,3,6]{2,1,0:T(4,128)S(1)} %copy.16), kind=kLoop, calls=%fused_computation.11 | loop fusion | flops 3538944 | bytes 4718880 | tf_op jit(solution)/shard_map/convert_element_type | solution.py:15
  46.8 0.0 all-gather.6.cloned.1.call-done
  46.9 0.0 all-gather.4.cloned.1.call-done
  46.9 4.3 %all-gather.8.cloned.1.call-done = bf16[1024,512]{1,0:T(8,128)(2,1)} async-done(((bf16[512,512]{1,0:T(8,128)(2,1)}), bf16[1024,512]{1,0:T(8,128)(2,1)}) %all-gather.8.cloned.1.call-update) | async-done | bytes 1048592 | tf_op jit(solution)/shard_map/all_gather | solution.py:44
  51.2 3.1 %pad_maximum_fusion = bf16[3072,512]{1,0:T(8,128)(2,1)} fusion(bf16[1024,512]{1,0:T(8,128)(2,1)} %all-gather.8.cloned.1.call-done, bf16[1024,512]{1,0:T(8,128)(2,1)} %all-gather.6.cloned.1.call-done, bf16[1024,512]{1,0:T(8,128)(2,1)} %all-gather.4.cloned.1.call-done), kind=kLoop, calls=%fused_computation.12 | loop fusion | flops 9437184 | bytes 6291456 | tf_op jit(solution)/shard_map/concatenate | solution.py:47
  54.4 7.9 %gather_fusion = bf16[72,128,512]{2,1,0:T(8,128)(2,1)} fusion(bf16[24,128,512]{2,1,0:T(8,128)(2,1)} %bitcast.72, s32[1024]{0:T(1024)S(1)} %pad_clamp_fusion), kind=kCustom, calls=%fused_computation | custom fusion | bytes 18874656 | tf_op jit(solution)/shard_map/jit(_take)/gather | solution.py:52
  62.2 4.8 %fusion = f32[4,128,512,1]{2,1,3,0:T(8,128)S(1)} fusion(bf16[4,18,128,128]{3,2,1,0:T(8,128)(2,1)S(1)} %bitcast.74, bf16[4,18,128,512]{3,2,1,0:T(8,128)(2,1)} %bitcast.73, pred[4,18]{1,0:T(4,128)(4,1)S(1)} %compare_and_fusion), kind=kOutput, calls=%fused_computation.1 | convolution fusion | flops 1212678144 | bytes 12845128 | tf_op jit(solution)/shard_map/bkij,bkjf->bif/dot_general | solution.py:54
  67.1 0.1 fusion.22
  67.2 1.6 %multiply_convert_fusion.1 = (bf16[512,512]{1,0:T(8,128)(2,1)S(1)}, bf16[512,512]{1,0:T(8,128)(2,1)}) fusion(bf16[512,512]{1,0:T(8,128)(2,1)S(1)} %copy-done.5, f32[512,512]{1,0:T(8,128)S(1)} %copy-done.2, bf16[512,512]{1,0:T(8,128)(2,1)S(1)} %fusion.22, bf16[512,512]{1,0:T(8,128)(2,1)S(1)} %copy-done), kind=kOutput, calls=%fused_computation.26 | convolution fusion | flops 271843328 | bytes 3670016 | tf_op jit(solution)/shard_map/dot_general | solution.py:59
  68.8 0.5 fusion.21
  69.3 1.0 fusion.24
  70.3 1.0 fusion.23
  71.4 2.5 %bitcast_convert_fusion.1 = bf16[8,128,512]{2,0,1:T(8,128)(2,1)S(1)} fusion(bf16[4,6,128,512]{3,2,1,0:T(8,128)(2,1)S(1)} %fusion.24, s32[4,6]{1,0:T(4,128)S(1)} %get-tuple-element.4), kind=kOutput, calls=%fused_computation.14 | convolution fusion | flops 25166016 | bytes 4194400 | tf_op jit(solution)/shard_map/bkq,bkjf->qjf/dot_general | solution.py:77
  73.9 0.3 copy.20
  74.2 4.5 %collective-permute-start.2 = (bf16[1024,512]{1,0:T(8,128)(2,1)S(1)}, bf16[1024,512]{1,0:T(8,128)(2,1)S(1)}, u32[]{:S(2)}, u32[]{:S(2)}) collective-permute-start(bf16[1024,512]{1,0:T(8,128)(2,1)S(1)} %bitcast.78), channel_id=1, source_target_pairs={{2,0},{4,2},{6,4},{8,6},{10,8},{12,10},{14,12},{0,14},{3,1},{5,3},... | collective-permute-start | bytes 3145736 | tf_op jit(solution)/shard_map/ppermute | solution.py:10
  78.8 2.5 %bitcast_convert_fusion = bf16[8,128,512]{2,0,1:T(8,128)(2,1)S(1)} fusion(bf16[4,6,128,512]{3,2,1,0:T(8,128)(2,1)S(1)} %fusion.23, s32[4,6]{1,0:T(4,128)S(1)} %get-tuple-element.6), kind=kOutput, calls=%fused_computation.13 | convolution fusion | flops 25166016 | bytes 4194400 | tf_op jit(solution)/shard_map/bkq,bkjf->qjf/dot_general | solution.py:77
  81.3 0.3 copy.21
  81.6 0.2 collective-permute-start.3
  81.9 1.0 fusion.25
  82.9 2.5 %fusion.18 = f32[8,128,512]{2,0,1:T(8,128)S(1)} fusion(bf16[4,6,128,512]{3,2,1,0:T(8,128)(2,1)S(1)} %fusion.25, s32[4,6]{1,0:T(4,128)S(1)} %get-tuple-element.5), kind=kOutput, calls=%fused_computation.19 | convolution fusion | flops 25690304 | bytes 5242976 | tf_op jit(solution)/shard_map/bkq,bkjf->qjf/dot_general | solution.py:77
  85.4 1.2 copy.19
  86.7 35.4 %collective-permute-done.2 = bf16[1024,512]{1,0:T(8,128)(2,1)S(1)} collective-permute-done((bf16[1024,512]{1,0:T(8,128)(2,1)S(1)}, bf16[1024,512]{1,0:T(8,128)(2,1)S(1)}, u32[]{:S(2)}, u32[]{:S(2)}) %collective-permute-start.2) | collective-permute-done | bytes 1048608 | tf_op jit(solution)/shard_map/ppermute | solution.py:10
  122.1 0.2 collective-permute-done.3
  122.3 1.5 %fusion.11 = bf16[1024,512]{1,0:T(8,128)(2,1)} fusion(f32[8,128,512]{2,1,0:T(8,128)S(1)} %copy.19, bf16[1024,512]{1,0:T(8,128)(2,1)S(1)} %collective-permute-done.3, bf16[1024,512]{1,0:T(8,128)(2,1)S(1)} %collective-permute-done.2), kind=kLoop, calls=%fused_computation.17 | loop fusion | flops 2621440 | bytes 5242880 | tf_op jit(solution)/shard_map/convert_element_type | solution.py:85
  123.7 0.0 reduce-scatter.2.cloned.1.call-update
  123.8 0.5 fusion.37
  124.2 12.0 %reduce-scatter.2.cloned.1.call-done = bf16[512,512]{1,0:T(8,128)(2,1)} async-done(((bf16[1024,512]{1,0:T(8,128)(2,1)}), bf16[512,512]{1,0:T(8,128)(2,1)}) %reduce-scatter.2.cloned.1.call-update) | async-done | bytes 524304 | tf_op jit(solution)/shard_map/reduce_scatter | solution.py:84
  136.2 2.0 %add_convert_fusion = bf16[512,512]{1,0:T(8,128)(2,1)} fusion(f32[512,512]{1,0:T(8,128)S(1)} %fusion.37, bf16[512,512]{1,0:T(8,128)(2,1)} %reduce-scatter.2.cloned.1.call-done), kind=kLoop, calls=%fused_computation.25 | loop fusion | flops 786432 | bytes 2097152 | tf_op jit(solution)/shard_map/convert_element_type | solution.py:88
  (17 shorter events, 0.1 us)
Async XLA Ops:
  7.2 60.0 %copy-start = (bf16[512,512]{1,0:T(8,128)(2,1)S(1)}, bf16[512,512]{1,0:T(8,128)(2,1)}, u32[]{:S(2)}) copy-start(bf16[512,512]{1,0:T(8,128)(2,1)} %param.10) | copy-start | bytes 1572868
  7.2 39.7 %all-gather.6.cloned.1.call-start = ((), (), s32[]{:S(2)}) async-start(), calls=%async_computation.2 | async-start | bytes 1572864 | tf_op jit(solution)/shard_map/all_gather | solution.py:43
  7.9 39.0 %all-gather.4.cloned.1.call-start = ((), (), s32[]{:S(2)}) async-start(), calls=%async_computation.1 | async-start | bytes 1572864 | tf_op jit(solution)/shard_map/all_gather | solution.py:42
  8.0 18.2 %collective-permute-start = (bf16[512,512]{1,0:T(8,128)(2,1)}, bf16[512,512]{1,0:T(8,128)(2,1)S(1)}, u32[]{:S(2)}, u32[]{:S(2)}) collective-permute-start(bf16[512,512]{1,0:T(8,128)(2,1)} %param.8), channel_id=1, source_target_pairs={{14,0},{0,2},{2,4},{4,6},{6,8},{8,10},{10,12},{12,14},{15,1},{1,3}... | collective-permute-start | bytes 1572872 | tf_op jit(solution)/shard_map/ppermute | solution.py:10
  26.1 0.8 copy-start.3
  26.9 24.3 %all-gather.8.cloned.1.call-start = ((), (), s32[]{:S(2)}) async-start(), calls=%async_computation.3 | async-start | bytes 1572864 | tf_op jit(solution)/shard_map/all_gather | solution.py:44
  27.0 13.4 %collective-permute-start.1 = (bf16[512,512]{1,0:T(8,128)(2,1)}, bf16[512,512]{1,0:T(8,128)(2,1)S(1)}, u32[]{:S(2)}, u32[]{:S(2)}) collective-permute-start(bf16[512,512]{1,0:T(8,128)(2,1)} %param.8), channel_id=1, source_target_pairs={{2,0},{4,2},{6,4},{8,6},{10,8},{12,10},{14,12},{0,14},{3,1},{5,3},... | collective-permute-start | bytes 1572872 | tf_op jit(solution)/shard_map/ppermute | solution.py:10
  40.4 0.8 copy-start.4
  41.2 95.0 %reduce-scatter.2.cloned.1.call-start = ((), (), s32[]{:S(2)}) async-start(), calls=%async_computation.4 | async-start | bytes 1572864 | tf_op jit(solution)/shard_map/reduce_scatter | solution.py:84
  62.2 5.0 %copy-start.2 = (f32[512,512]{1,0:T(8,128)S(1)}, f32[512,512]{1,0:T(8,128)}, u32[]{:S(2)}) copy-start(f32[512,512]{1,0:T(8,128)} %fusion.36) | copy-start | bytes 3145732
  62.2 5.0 %copy-start.5 = (bf16[512,512]{1,0:T(8,128)(2,1)S(1)}, bf16[512,512]{1,0:T(8,128)(2,1)}, u32[]{:S(2)}) copy-start(bf16[512,512]{1,0:T(8,128)(2,1)} %param.15) | copy-start | bytes 1572868
  74.2 47.9 %collective-permute-start.2 = (bf16[1024,512]{1,0:T(8,128)(2,1)S(1)}, bf16[1024,512]{1,0:T(8,128)(2,1)S(1)}, u32[]{:S(2)}, u32[]{:S(2)}) collective-permute-start(bf16[1024,512]{1,0:T(8,128)(2,1)S(1)} %bitcast.78), channel_id=1, source_target_pairs={{2,0},{4,2},{6,4},{8,6},{10,8},{12,10},{14,12},{0,14},{3,1},{5,3},... | collective-permute-start | bytes 3145736 | tf_op jit(solution)/shard_map/ppermute | solution.py:10
  81.6 40.6 %collective-permute-start.3 = (bf16[1024,512]{1,0:T(8,128)(2,1)S(1)}, bf16[1024,512]{1,0:T(8,128)(2,1)S(1)}, u32[]{:S(2)}, u32[]{:S(2)}) collective-permute-start(bf16[1024,512]{1,0:T(8,128)(2,1)S(1)} %bitcast.79), channel_id=1, source_target_pairs={{14,0},{0,2},{2,4},{4,6},{6,8},{8,10},{10,12},{12,14},{15,1},{1,3}... | collective-permute-start | bytes 3145736 | tf_op jit(solution)/shard_map/ppermute | solution.py:10
  86.7 37.1 %copy-start.1 = (bf16[512,512]{1,0:T(8,128)(2,1)S(1)}, bf16[512,512]{1,0:T(8,128)(2,1)}, u32[]{:S(2)}) copy-start(bf16[512,512]{1,0:T(8,128)(2,1)} %param.9) | copy-start | bytes 1572868
Sparse Core Ops, SparseCore 0:
  9.6 11.7 all-gather.5
  27.1 7.4 all-gather.3
  41.3 9.8 all-gather.7
  123.9 12.2 reduce-scatter.1
where the time goes:
time: 145 us
  waiting for transfers between devices  77 us (53%)
  matrix products  20.7 us (14%)
  between operations  13.9 us (10%)
  local copies, waits for them, and re-layouts  12.4 us (9%)
  other arithmetic  11.1 us (8%)
  starting transfers between devices  9.72 us (7%)
    ppermute x4, waiting for transfers between devices, shifted(): return lax.ppermute(block, axis, route)  59.9 us
    reduce_scatter x1, waiting for transfers between devices, per_device(): lax.psum_scatter(summed.astype(jnp.bfloat16), 'sub', scatter_dimension=0,...  12 us
    ppermute x4, starting transfers between devices, shifted(): return lax.ppermute(block, axis, route)  9.56 us
    gather x1, local copies, waits for them, and re-layouts, per_device(): gathered = jnp.take(flat_slabs, block_index, axis=0)  7.88 us
    dot_general x3, matrix products, per_device(): placed = jnp.einsum('bkq,bkjf->qjf', selector, spread)  7.57 us
    dot_general x1, matrix products, per_device(): jnp.einsum('bkij,bkjf->bif', flat_tiles, gathered, preferred_element_type...  4.81 us
    all_gather x1, waiting for transfers between devices, per_device(): lax.all_gather(next_half, 'sub', axis=0, tiled=True)  4.34 us
    concatenate x1, other arithmetic, per_device(): jnp.concatenate([prev_slab, own_slab, next_slab], axis=0)  3.13 us
  transfers between devices with their start and end apart: 8, of which 6 were waited for; matrix products, arithmetic and copies ran while one was open for 11% of the time, Pallas kernels for 0%

commit v1 on v0

v1 whole, which is shorter than its diff:
```python
import jax
import jax.numpy as jnp
from jax import lax
from jax.experimental import pallas as pl
from jax.experimental.pallas import tpu as pltpu
from jax.sharding import PartitionSpec as P

ROWS = ("parts", "slab", "sub")


def dense_kernel(info, sources, counts, tiles, fwd, mine, other, total):
    i = pl.program_id(0)
    j, u = info[0], info[1]
    slots, size = tiles.shape[2], tiles.shape[3]
    blocks = total.shape[0]
    half = blocks // 2
    total[...] = jnp.zeros_like(total)
    for k in range(slots):
        at = (i * 3 + j) * slots + k
        b = sources[at]
        place = jnp.bitwise_xor(b // half, u) * half + b % half
        scale = counts[at].astype(jnp.float32) * (1.0 / size)
        total[place] += tiles[0, 0, k].astype(jnp.float32) * scale
    for b in range(blocks):
        block = total[b]
        fwd[:, b * size:(b + 1) * size] = block.astype(fwd.dtype)
        turned = block.T.astype(fwd.dtype)
        if b < half:
            mine[b * size:(b + 1) * size, :] = turned
        else:
            other[(b - half) * size:(b - half + 1) * size, :] = turned


def dense(info, sources, counts, tiles):
    local, _, slots, size, _ = tiles.shape
    rows = local * size
    kind = tiles.dtype
    return pl.pallas_call(
        dense_kernel,
        grid_spec=pltpu.PrefetchScalarGridSpec(
            num_scalar_prefetch=3,
            grid=(local,),
            in_specs=[
                pl.BlockSpec((1, 1, slots, size, size), lambda i, n, s, c: (i, n[0], 0, 0, 0)),
            ],
            out_specs=[
                pl.BlockSpec((size, 2 * rows), lambda i, n, s, c: (i, 0)),
                pl.BlockSpec((rows, size), lambda i, n, s, c: (0, i)),
                pl.BlockSpec((rows, size), lambda i, n, s, c: (0, i)),
            ],
            scratch_shapes=[pltpu.VMEM((2 * local, size, size), jnp.float32)],
        ),
        out_shape=[
            jax.ShapeDtypeStruct((rows, 2 * rows), kind),
            jax.ShapeDtypeStruct((rows, rows), kind),
            jax.ShapeDtypeStruct((rows, rows), kind),
        ],
        compiler_params=pltpu.CompilerParams(vmem_limit_bytes=16 << 20),
        cost_estimate=pl.CostEstimate(
            flops=4 * local * slots * size * size,
            bytes_accessed=2 * local * (slots + 4 * local) * size * size,
            transcendentals=0,
        ),
    )(info, sources, counts, tiles)


def mm(a, b):
    return jnp.dot(a, b, preferred_element_type=jnp.float32)


def mmt(a, b):
    return lax.dot_general(a, b, (((1,), (1,)), ((), ())), preferred_element_type=jnp.float32)


def after(value, *earlier):
    return lax.optimization_barrier((value, *earlier))[0]


def per_device(x, w_self, w_neigh, tiles, source_block, edge_counts, normalizer, cotangent):
    n_slab = lax.axis_size("slab")
    ring = range(n_slab)
    pair = [(i, i ^ 1) for i in ring]
    diag = [(i, (i + (1 if i % 2 else -1)) % n_slab) for i in ring]
    hop = [(i, (i + (-2 if i % 2 else 2)) % n_slab) for i in ring]
    back = [(b, a) for a, b in hop]
    swap = [(0, 1), (1, 0)]

    def slab(v, route):
        return lax.ppermute(v, "slab", route)

    def sub(v):
        return lax.ppermute(v, "sub", swap)

    rows, width = x.shape
    cut = rows // 2
    odd = lax.axis_index("slab") % 2
    u = lax.axis_index("sub")
    kind = x.dtype
    sources = source_block.reshape(-1)
    counts = edge_counts.reshape(-1)

    def build(j):
        return dense(jnp.stack([j, u]).astype(jnp.int32), sources, counts, tiles)

    xa = slab(x[:cut], pair)
    x_sib = sub(x)
    fx, mx, ox = build(2 - 2 * odd)
    xb = slab(after(x[cut:], fx), pair)
    zb = slab(after(x[cut:], fx), diag)
    za = slab(xa, hop)
    fz, mz, oz = build(2 * odd)
    fo, mo, oo = build(jnp.ones_like(odd))
    mx2, mz2, mo2 = sub(ox), sub(oz), sub(oo)
    xa_sib, za_sib, xb_sib, zb_sib = sub(xa), sub(za), sub(xb), sub(zb)
    own = mm(x, w_self)
    messages = mm(fo[:, :rows], x) + mm(fo[:, rows:], x_sib)
    c0, c1, c2, c3, c4 = (k * cut for k in range(5))
    messages += mm(fx[:, c0:c1], xa) + mm(fx[:, c2:c3], xa_sib)
    messages += mm(fz[:, c0:c1], za) + mm(fz[:, c2:c3], za_sib)
    messages += mm(fx[:, c1:c2], xb) + mm(fz[:, c1:c2], zb)
    messages += mm(fx[:, c3:c4], xb_sib) + mm(fz[:, c3:c4], zb_sib)

    norm = normalizer.astype(jnp.float32)[:, None]
    aggregate = (messages / norm).astype(kind)
    pre = own + mm(aggregate, w_neigh)
    q = jax.nn.sigmoid(pre)
    node_out = (pre * q).astype(kind)
    pre_grad = (cotangent.astype(jnp.float32) * (q * (1.0 + pre * (1.0 - q)))).astype(kind)
    g = (mmt(pre_grad, w_neigh) / norm).astype(kind)
    g_sib = sub(g)

    pz = (mm(mz, g) + mm(mz2, g_sib)).astype(kind)
    ra = slab(pz[:cut], back)
    px = mm(mx, g) + mm(mx2, g_sib)
    rzb = slab(pz[cut:], diag)
    rxb = slab(px[cut:].astype(kind), pair)
    own_grad = mmt(pre_grad, w_self) + mm(mo, g) + mm(mo2, g_sib)
    rxa = slab((px[:cut] + ra.astype(jnp.float32)).astype(kind), pair)
    low = own_grad[:cut] + rxa.astype(jnp.float32)
    high = own_grad[cut:] + rxb.astype(jnp.float32) + rzb.astype(jnp.float32)
    node_grad = jnp.concatenate([low, high], axis=0).astype(kind)
    return (node_out, node_grad)


def solution(mesh):
    whole = P(None, None)
    return jax.shard_map(
        per_device,
        mesh=mesh,
        in_specs=(
            P(ROWS, None),
            whole,
            whole,
            P(ROWS, None, None, None, None),
            P(ROWS, None, None),
            P(ROWS, None, None),
            P(ROWS),
            P(ROWS, None),
        ),
        out_specs=(P(ROWS, None), P(ROWS, None)),
        check_vma=False,
    )
```

time: 145 us -> 82.4 us (0.57)
  waiting for transfers between devices: 77 us -> 33.6 us
  between operations: 13.9 us -> 0.84 us
  other arithmetic: 11.1 us -> 1.24 us
  Pallas kernels: 0 us -> 7.98 us
  local copies, waits for them, and re-layouts: 12.4 us -> 5.1 us
  starting transfers between devices: 9.72 us -> 14 us
  matrix products: 20.7 us -> 19.1 us
    ppermute x4 -> x17, waiting for transfers between devices: 59.9 us -> 33.6 us  [the longest x8 32 us: slab(): return lax.ppermute(v, 'slab', route)]
    reduce_scatter x1 -> x0, waiting for transfers between devices: 12 us -> none  [per_device(): lax.psum_scatter(summed.astype(jnp.bfloat16), 'sub', scatter_dimension=0,...]
    pallas_call x0 -> x3, Pallas kernels: none -> 7.98 us  [dense(): pl.pallas_call(dense_kernel, grid_spec=pltpu.PrefetchScalarGridSpec(num_s...]
    gather x1 -> x0, local copies, waits for them, and re-layouts: 7.88 us -> none  [per_device(): gathered = jnp.take(flat_slabs, block_index, axis=0)]
    convert_element_type x5 -> x2, other arithmetic: 6.47 us -> 0.07 us  [the longest x1 0.07 us: per_device(): rxa = slab((px[:cut] + ra.astype(jnp.float32)).astype(kind), pair)]
    ppermute x4 -> x17, starting transfers between devices: 9.56 us -> 14 us  [the longest x8 11.4 us: slab(): return lax.ppermute(v, 'slab', route)]
    all_gather x3 -> x0, waiting for transfers between devices: 4.37 us -> none  [the longest x1 4.34 us: per_device(): lax.all_gather(next_half, 'sub', axis=0, tiled=True)]
    concatenate x1, other arithmetic: 3.13 us -> 0.83 us  [per_device(): node_grad = jnp.concatenate([low, high], axis=0).astype(kind)]
  transfers between devices with their start and end apart: 8 -> 17, of which waited for: 6 -> 8; matrix products, arithmetic and copies ran while one was open for 11% -> 28% of each run, Pallas kernels for 0% -> 10%
where the time goes in v1:
time: 82.4 us; the launch traced here: 81.9 us
  waiting for transfers between devices  33.6 us (41%)
  matrix products  19.1 us (23%)
  starting transfers between devices  14 us (17%)
  Pallas kernels  7.98 us (10%)
  local copies, waits for them, and re-layouts  5.1 us (6%)
  other arithmetic  1.24 us (2%)
  between operations  0.84 us (1%)
    ppermute x8, waiting for transfers between devices, slab(): return lax.ppermute(v, 'slab', route)  32 us
    dot_general x17, matrix products, mm(): return jnp.dot(a, b, preferred_element_type=jnp.float32)  17 us
    ppermute x8, starting transfers between devices, slab(): return lax.ppermute(v, 'slab', route)  11.4 us
    pallas_call x3, Pallas kernels, dense(): pl.pallas_call(dense_kernel, grid_spec=pltpu.PrefetchScalarGridSpec(num_s...  7.98 us
    unnamed x18, local copies, waits for them, and re-layouts  3.09 us
    ppermute x9, starting transfers between devices, sub(): return lax.ppermute(v, 'sub', swap)  2.61 us
    dot_general x2, matrix products, mmt(): lax.dot_general(a, b, (((1,), (1,)), ((), ())), preferred_element_type=jn...  2.07 us
    slice x1, local copies, waits for them, and re-layouts, per_device(): xa = slab(x[:cut], pair)  1.76 us
  transfers between devices with their start and end apart: 17, of which 8 were waited for; matrix products, arithmetic and copies ran while one was open for 28% of the time, Pallas kernels for 10%

profile of v1, /device:TPU:0, one launch (start us, length us, event | category | flops | bytes accessed | tf_op | source)
XLA Modules:
  0.0 81.9 jit_solution(12059026737254660244)
XLA Ops:
  0.6 0.5 collective-permute-start
  1.2 1.8 %fusion.30 = (bf16[256,512]{1,0:T(8,128)(2,1)}, bf16[256,512]{1,0:T(8,128)(2,1)S(1)}) fusion(bf16[512,512]{1,0:T(8,128)(2,1)} %param.8), kind=kLoop, calls=%fused_computation.51 | loop fusion | bytes 1048576 | tf_op jit(solution)/shard_map/slice | solution.py:105
  2.9 0.7 copy.12
  3.6 0.1 reshape.11.sources
  3.7 0.7 copy.13
  4.6 1.7 %copy-done.1 = bf16[4,3,6,128,128]{4,3,2,1,0:T(8,128)(2,1)S(1)} copy-done((bf16[4,3,6,128,128]{4,3,2,1,0:T(8,128)(2,1)S(1)}, bf16[4,3,6,128,128]{4,3,2,1,0:T(8,128)(2,1)}, u32[]{:S(2)}) %copy-start.1) | copy-done | bytes 2359320
  6.2 2.7 %shard_map.96 = (bf16[512,1024]{1,0:T(8,128)(2,1)S(1)}, bf16[512,512]{1,0:T(8,128)(2,1)S(1)}, bf16[512,512]{1,0:T(8,128)(2,1)}) custom-call(s32[2]{0:T(128)S(1)} %get-tuple-element.31.info, s32[72]{0:T(128)S(1)} %reshape.11.sources, s32[72]{0:T(128)S(1)} %reshape.12.counts, bf16[4,3,6,128,128]{4,3,2,1,0:T(8,128)(2,1)S(1)} %copy-done.1), custom_call_target="tpu_custom_call" | custom-call | flops 1572864 | bytes 2883584 | tf_op jit(solution)/shard_map/pallas_call | solution.py:38
  8.9 5.6 %collective-permute-start.6 = (bf16[256,512]{1,0:T(8,128)(2,1)S(1)}, bf16[256,512]{1,0:T(8,128)(2,1)S(1)}, u32[]{:S(2)}, u32[]{:S(2)}) collective-permute-start(bf16[256,512]{1,0:T(8,128)(2,1)S(1)} %get-tuple-element.15), channel_id=1, source_target_pairs={{0,14},{2,4},{4,2},{6,8},{8,6},{10,12},{12,10},{14,0},{1,15},{3,5}... | collective-permute-start | bytes 786440 | tf_op jit(solution)/shard_map/ppermute | solution.py:89
  14.5 2.0 %collective-permute-start.1 = (bf16[256,512]{1,0:T(8,128)(2,1)}, bf16[256,512]{1,0:T(8,128)(2,1)S(1)}, u32[]{:S(2)}, u32[]{:S(2)}) collective-permute-start(bf16[256,512]{1,0:T(8,128)(2,1)} %get-tuple-element.28), channel_id=1, source_target_pairs={{0,2},{2,0},{4,6},{6,4},{8,10},{10,8},{12,14},{14,12},{1,3},{3,1},... | collective-permute-start | bytes 786440 | tf_op jit(solution)/shard_map/ppermute | solution.py:89
  16.7 2.6 %shard_map.97 = (bf16[512,1024]{1,0:T(8,128)(2,1)S(1)}, bf16[512,512]{1,0:T(8,128)(2,1)S(1)}, bf16[512,512]{1,0:T(8,128)(2,1)}) custom-call(s32[2]{0:T(128)S(1)} %pad_add_fusion.2.info, s32[72]{0:T(128)S(1)} %reshape.11.sources, s32[72]{0:T(128)S(1)} %reshape.12.counts, bf16[4,3,6,128,128]{4,3,2,1,0:T(8,128)(2,1)S(1)} %copy-done.2), custom_call_target="tpu_custom_call" | custom-call | flops 1572864 | bytes 2883584 | tf_op jit(solution)/shard_map/pallas_call | solution.py:38
  19.3 2.7 %shard_map.95 = (bf16[512,1024]{1,0:T(8,128)(2,1)S(1)}, bf16[512,512]{1,0:T(8,128)(2,1)S(1)}, bf16[512,512]{1,0:T(8,128)(2,1)}) custom-call(s32[2]{0:T(128)S(1)} %get-tuple-element.30.info, s32[72]{0:T(128)S(1)} %reshape.11.sources, s32[72]{0:T(128)S(1)} %reshape.12.counts, bf16[4,3,6,128,128]{4,3,2,1,0:T(8,128)(2,1)S(1)} %copy-done.2), custom_call_target="tpu_custom_call" | custom-call | flops 1572864 | bytes 2883584 | tf_op jit(solution)/shard_map/pallas_call | solution.py:38
  22.0 0.4 fusion.14
  22.4 1.4 %fusion.33 = f32[512,512]{1,0:T(8,128)} fusion(bf16[512,512]{1,0:T(8,128)(2,1)S(1)} %copy-done.3, bf16[512,512]{1,0:T(8,128)(2,1)S(1)} %copy-done.4), kind=kOutput, calls=%fused_computation.52 | convolution fusion | flops 268435456 | bytes 2097152 | tf_op jit(solution)/shard_map/dot_general | solution.py:68
  23.9 0.5 collective-permute-start.11
  24.4 0.3 fusion.20
  24.7 8.0 %collective-permute-done.1 = bf16[256,512]{1,0:T(8,128)(2,1)S(1)} collective-permute-done((bf16[256,512]{1,0:T(8,128)(2,1)}, bf16[256,512]{1,0:T(8,128)(2,1)S(1)}, u32[]{:S(2)}, u32[]{:S(2)}) %collective-permute-start.1) | collective-permute-done | bytes 262176 | tf_op jit(solution)/shard_map/ppermute | solution.py:89
  32.7 0.5 collective-permute-start.2
  33.2 0.3 convolution_add_fusion.7
  33.5 0.3 fusion.27
  33.8 1.2 %collective-permute-done.2 = bf16[256,512]{1,0:T(8,128)(2,1)S(1)} collective-permute-done((bf16[256,512]{1,0:T(8,128)(2,1)S(1)}, bf16[256,512]{1,0:T(8,128)(2,1)S(1)}, u32[]{:S(2)}, u32[]{:S(2)}) %collective-permute-start.2) | collective-permute-done | bytes 262176 | tf_op jit(solution)/shard_map/ppermute | solution.py:92
  35.0 0.3 convolution_add_fusion.9
  35.3 0.2 collective-permute-start.8
  35.5 1.5 %fusion = f32[512,512]{1,0:T(8,128)S(1)} fusion(f32[512,512]{1,0:T(8,128)S(1)} %convolution_add_fusion.9, f32[512,512]{1,0:T(8,128)S(1)} %fusion.14, bf16[512,512]{1,0:T(8,128)(2,1)} %collective-permute-done, bf16[512,1024]{1,0:T(8,128)(2,1)S(1)} %get-tuple-element.12), kind=kOutput, calls=%fused_computation.7 | convolution fusion | flops 268959744 | bytes 4194304 | tf_op jit(solution)/shard_map/dot_general | solution.py:68
  37.0 8.1 %collective-permute-done.3 = bf16[256,512]{1,0:T(8,128)(2,1)S(1)} collective-permute-done((bf16[256,512]{1,0:T(8,128)(2,1)S(1)}, bf16[256,512]{1,0:T(8,128)(2,1)S(1)}, u32[]{:S(2)}, u32[]{:S(2)}) %collective-permute-start.3) | collective-permute-done | bytes 262176 | tf_op jit(solution)/shard_map/ppermute | solution.py:89
  45.1 0.3 fusion.24
  45.4 0.6 collective-permute-start.4
  46.0 1.3 %fusion.16 = f32[512,512]{1,0:T(8,128)} fusion(bf16[256,512]{1,0:T(8,128)(2,1)S(1)} %collective-permute-done.8, bf16[512,1024]{1,0:T(8,128)(2,1)S(1)} %get-tuple-element.14), kind=kOutput, calls=%fused_computation.35 | convolution fusion | flops 134217728 | bytes 1572864 | tf_op jit(solution)/shard_map/dot_general | solution.py:68
  47.3 1.3 %fusion.3 = f32[512,512]{1,0:T(8,128)} fusion(f32[512,512]{1,0:T(8,128)S(1)} %convolution_add_fusion.7, f32[512,512]{1,0:T(8,128)S(1)} %fusion, f32[512,512]{1,0:T(8,128)S(1)} %fusion.24, bf16[256,512]{1,0:T(8,128)(2,1)S(1)} %collective-permute-done.4, bf16[512,1024]{1,0:T(8,128)(2,1)S(1)} %get-tuple-element.14), kind=kOutput, calls=%fused_computation.14 | convolution fusion | flops 135004160 | bytes 4718592 | tf_op jit(solution)/shard_map/dot_general | solution.py:68
  48.6 3.9 %multiply_convert_fusion = (bf16[512,512]{1,0:T(8,128)(2,1)}, bf16[512,512]{1,0:T(8,128)(2,1)}) fusion(bf16[512,512]{1,0:T(8,128)(2,1)} %param.15, f32[512,512]{1,0:T(8,128)} %fusion.33, bf16[512,512]{1,0:T(8,128)(2,1)S(1)} %copy-done, f32[512,512]{1,0:T(8,128)} %fusion.3, f32[512,512]{1,0:T(8,128)} %fusion.16, ...), kind=kOutput, calls=%fused_computation.19 | convolution fusion | flops 407109632 | bytes 5769216 | tf_op jit(solution)/shard_map/dot_general | solution.py:68
  52.5 1.6 %fusion.6 = bf16[512,512]{1,0:T(8,128)(2,1)S(1)} fusion(bf16[512,512]{1,0:T(8,128)(2,1)} %get-tuple-element.24, bf16[512,512]{1,0:T(8,128)(2,1)S(1)} %copy-done, f32[512]{0:T(512)S(1)} %convert_element_type.38), kind=kOutput, calls=%fused_computation.17 | convolution fusion | flops 268959744 | bytes 1574912 | tf_op jit(solution)/shard_map/dot_general | solution.py:72
  54.1 0.5 fusion.34
  54.6 0.3 collective-permute-start.10
  54.9 0.4 fusion.36
  55.3 0.4 fusion.35
  55.8 0.4 convolution_add_fusion.3
  56.2 0.3 collective-permute-done.10
  56.6 1.5 %fusion.7 = bf16[512,512]{1,0:T(8,128)(2,1)S(1)} fusion(f32[512,512]{1,0:T(8,128)S(1)} %fusion.36, bf16[512,512]{1,0:T(8,128)(2,1)} %collective-permute-done.12, bf16[512,512]{1,0:T(8,128)(2,1)S(1)} %collective-permute-done.10), kind=kOutput, calls=%fused_computation.18 | convolution fusion | flops 268959744 | bytes 2621440 | tf_op jit(solution)/shard_map/dot_general | solution.py:68
  58.2 1.7 %collective-permute-start.16 = (bf16[256,512]{1,0:T(8,128)(2,1)S(1)}, bf16[256,512]{1,0:T(8,128)(2,1)S(1)}, u32[]{:S(2)}, u32[]{:S(2)}) collective-permute-start(bf16[256,512]{1,0:T(8,128)(2,1)S(1)} %get-tuple-element.27), channel_id=1, source_target_pairs={{0,14},{2,4},{4,2},{6,8},{8,6},{10,12},{12,10},{14,0},{1,15},{3,5}... | collective-permute-start | bytes 786440 | tf_op jit(solution)/shard_map/ppermute | solution.py:89
  59.9 1.5 %convolution_add_fusion.1 = f32[512,512]{1,0:T(8,128)S(1)} fusion(f32[512,512]{1,0:T(8,128)S(1)} %fusion.35, bf16[512,512]{1,0:T(8,128)(2,1)} %collective-permute-done.11, bf16[512,512]{1,0:T(8,128)(2,1)S(1)} %collective-permute-done.10), kind=kOutput, calls=%fused_computation.1 | convolution fusion | flops 268697600 | bytes 3145728 | tf_op jit(solution)/shard_map/dot_general | solution.py:68
  61.4 1.8 %collective-permute-start.15 = (bf16[256,512]{1,0:T(8,128)(2,1)S(1)}, bf16[256,512]{1,0:T(8,128)(2,1)S(1)}, u32[]{:S(2)}, u32[]{:S(2)}) collective-permute-start(bf16[256,512]{1,0:T(8,128)(2,1)S(1)} %slice.113), channel_id=1, source_target_pairs={{0,2},{2,0},{4,6},{6,4},{8,10},{10,8},{12,14},{14,12},{1,3},{3,1},... | collective-permute-start | bytes 786440 | tf_op jit(solution)/shard_map/ppermute | solution.py:89
  63.3 4.1 %collective-permute-done.13 = bf16[256,512]{1,0:T(8,128)(2,1)S(1)} collective-permute-done((bf16[256,512]{1,0:T(8,128)(2,1)S(1)}, bf16[256,512]{1,0:T(8,128)(2,1)S(1)}, u32[]{:S(2)}, u32[]{:S(2)}) %collective-permute-start.13) | collective-permute-done | bytes 262176 | tf_op jit(solution)/shard_map/ppermute | solution.py:89
  67.4 0.2 collective-permute-start.14
  67.6 1.5 %convolution_add_fusion.2 = f32[512,512]{1,0:T(8,128)S(1)} fusion(f32[512,512]{1,0:T(8,128)S(1)} %convolution_add_fusion.3, bf16[512,512]{1,0:T(8,128)(2,1)} %collective-permute-done.9, bf16[512,512]{1,0:T(8,128)(2,1)S(1)} %collective-permute-done.10), kind=kOutput, calls=%fused_computation.2 | convolution fusion | flops 268697600 | bytes 3145728 | tf_op jit(solution)/shard_map/dot_general | solution.py:68
  69.1 3.2 %collective-permute-done.16 = bf16[256,512]{1,0:T(8,128)(2,1)S(1)} collective-permute-done((bf16[256,512]{1,0:T(8,128)(2,1)S(1)}, bf16[256,512]{1,0:T(8,128)(2,1)S(1)}, u32[]{:S(2)}, u32[]{:S(2)}) %collective-permute-start.16) | collective-permute-done | bytes 262176 | tf_op jit(solution)/shard_map/ppermute | solution.py:89
  72.2 4.0 %collective-permute-done.15 = bf16[256,512]{1,0:T(8,128)(2,1)S(1)} collective-permute-done((bf16[256,512]{1,0:T(8,128)(2,1)S(1)}, bf16[256,512]{1,0:T(8,128)(2,1)S(1)}, u32[]{:S(2)}, u32[]{:S(2)}) %collective-permute-start.15) | collective-permute-done | bytes 262176 | tf_op jit(solution)/shard_map/ppermute | solution.py:89
  76.3 4.6 %collective-permute-done.14 = bf16[256,512]{1,0:T(8,128)(2,1)S(1)} collective-permute-done((bf16[256,512]{1,0:T(8,128)(2,1)S(1)}, bf16[256,512]{1,0:T(8,128)(2,1)S(1)}, u32[]{:S(2)}, u32[]{:S(2)}) %collective-permute-start.14) | collective-permute-done | bytes 262176 | tf_op jit(solution)/shard_map/ppermute | solution.py:89
  80.9 0.2 fusion.11
  81.1 0.8 %pad_maximum_fusion = bf16[512,512]{1,0:T(8,128)(2,1)} fusion(bf16[256,512]{1,0:T(8,128)(2,1)S(1)} %get-tuple-element.23, bf16[256,512]{1,0:T(8,128)(2,1)S(1)} %get-tuple-element.22), kind=kLoop, calls=%fused_computation.30 | loop fusion | flops 1048576 | bytes 1048576 | tf_op jit(solution)/shard_map/concatenate | solution.py:141
  (37 shorter events, 0.5 us)
Async XLA Ops:
  0.6 48.0 %copy-start = (bf16[512,512]{1,0:T(8,128)(2,1)S(1)}, bf16[512,512]{1,0:T(8,128)(2,1)}, u32[]{:S(2)}) copy-start(bf16[512,512]{1,0:T(8,128)(2,1)} %param.10) | copy-start | bytes 1572868
  0.6 34.6 %collective-permute-start = (bf16[512,512]{1,0:T(8,128)(2,1)}, bf16[512,512]{1,0:T(8,128)(2,1)}, u32[]{:S(2)}, u32[]{:S(2)}) collective-permute-start(bf16[512,512]{1,0:T(8,128)(2,1)} %param.8), channel_id=1, source_target_pairs={{0,1},{1,0},{2,3},{3,2},{4,5},{5,4},{6,7},{7,6},{8,9},{9,8},{10,11... | collective-permute-start | bytes 1572872 | tf_op jit(solution)/shard_map/ppermute | solution.py:92
  4.6 1.7 %copy-start.1 = (bf16[4,3,6,128,128]{4,3,2,1,0:T(8,128)(2,1)S(1)}, bf16[4,3,6,128,128]{4,3,2,1,0:T(8,128)(2,1)}, u32[]{:S(2)}) copy-start(bf16[4,3,6,128,128]{4,3,2,1,0:T(8,128)(2,1)} %tiles.5) | copy-start | bytes 7077892
  6.2 10.4 %copy-start.2 = (bf16[4,3,6,128,128]{4,3,2,1,0:T(8,128)(2,1)S(1)}, bf16[4,3,6,128,128]{4,3,2,1,0:T(8,128)(2,1)}, u32[]{:S(2)}) copy-start(bf16[4,3,6,128,128]{4,3,2,1,0:T(8,128)(2,1)} %tiles.5) | copy-start | bytes 7077892
  8.9 14.9 %collective-permute-start.6 = (bf16[256,512]{1,0:T(8,128)(2,1)S(1)}, bf16[256,512]{1,0:T(8,128)(2,1)S(1)}, u32[]{:S(2)}, u32[]{:S(2)}) collective-permute-start(bf16[256,512]{1,0:T(8,128)(2,1)S(1)} %get-tuple-element.15), channel_id=1, source_target_pairs={{0,14},{2,4},{4,2},{6,8},{8,6},{10,12},{12,10},{14,0},{1,15},{3,5}... | collective-permute-start | bytes 786440 | tf_op jit(solution)/shard_map/ppermute | solution.py:89
  14.5 18.2 %collective-permute-start.5 = (bf16[256,512]{1,0:T(8,128)(2,1)S(1)}, bf16[256,512]{1,0:T(8,128)(2,1)S(1)}, u32[]{:S(2)}, u32[]{:S(2)}) collective-permute-start(bf16[256,512]{1,0:T(8,128)(2,1)S(1)} %get-tuple-element.15), channel_id=1, source_target_pairs={{0,2},{2,0},{4,6},{6,4},{8,10},{10,8},{12,14},{14,12},{1,3},{3,1},... | collective-permute-start | bytes 786440 | tf_op jit(solution)/shard_map/ppermute | solution.py:89
  14.5 18.1 %collective-permute-start.1 = (bf16[256,512]{1,0:T(8,128)(2,1)}, bf16[256,512]{1,0:T(8,128)(2,1)S(1)}, u32[]{:S(2)}, u32[]{:S(2)}) collective-permute-start(bf16[256,512]{1,0:T(8,128)(2,1)} %get-tuple-element.28), channel_id=1, source_target_pairs={{0,2},{2,0},{4,6},{6,4},{8,10},{10,8},{12,14},{14,12},{1,3},{3,1},... | collective-permute-start | bytes 786440 | tf_op jit(solution)/shard_map/ppermute | solution.py:89
  16.6 5.3 %copy-start.3 = (bf16[512,512]{1,0:T(8,128)(2,1)S(1)}, bf16[512,512]{1,0:T(8,128)(2,1)}, u32[]{:S(2)}) copy-start(bf16[512,512]{1,0:T(8,128)(2,1)} %param.8) | copy-start | bytes 1572868
  19.3 3.1 %copy-start.7 = (s32[512]{0:T(512)S(1)}, s32[512]{0:T(512)}, u32[]{:S(2)}) copy-start(s32[512]{0:T(512)} %param.14) | copy-start | bytes 6148
  19.3 3.1 %copy-start.4 = (bf16[512,512]{1,0:T(8,128)(2,1)S(1)}, bf16[512,512]{1,0:T(8,128)(2,1)}, u32[]{:S(2)}) copy-start(bf16[512,512]{1,0:T(8,128)(2,1)} %param.9) | copy-start | bytes 1572868
  19.3 36.9 %collective-permute-start.12 = (bf16[512,512]{1,0:T(8,128)(2,1)}, bf16[512,512]{1,0:T(8,128)(2,1)}, u32[]{:S(2)}, u32[]{:S(2)}) collective-permute-start(bf16[512,512]{1,0:T(8,128)(2,1)} %get-tuple-element.21), channel_id=1, source_target_pairs={{0,1},{1,0},{2,3},{3,2},{4,5},{5,4},{6,7},{7,6},{8,9},{9,8},{10,11... | collective-permute-start | bytes 1572872 | tf_op jit(solution)/shard_map/ppermute | solution.py:92
  23.9 36.0 %collective-permute-start.11 = (bf16[512,512]{1,0:T(8,128)(2,1)}, bf16[512,512]{1,0:T(8,128)(2,1)}, u32[]{:S(2)}, u32[]{:S(2)}) collective-permute-start(bf16[512,512]{1,0:T(8,128)(2,1)} %get-tuple-element.19), channel_id=1, source_target_pairs={{0,1},{1,0},{2,3},{3,2},{4,5},{5,4},{6,7},{7,6},{8,9},{9,8},{10,11... | collective-permute-start | bytes 1572872 | tf_op jit(solution)/shard_map/ppermute | solution.py:92
  32.7 34.9 %collective-permute-start.9 = (bf16[512,512]{1,0:T(8,128)(2,1)}, bf16[512,512]{1,0:T(8,128)(2,1)}, u32[]{:S(2)}, u32[]{:S(2)}) collective-permute-start(bf16[512,512]{1,0:T(8,128)(2,1)} %get-tuple-element.17), channel_id=1, source_target_pairs={{0,1},{1,0},{2,3},{3,2},{4,5},{5,4},{6,7},{7,6},{8,9},{9,8},{10,11... | collective-permute-start | bytes 1572872 | tf_op jit(solution)/shard_map/ppermute | solution.py:92
  32.7 2.2 %collective-permute-start.2 = (bf16[256,512]{1,0:T(8,128)(2,1)S(1)}, bf16[256,512]{1,0:T(8,128)(2,1)S(1)}, u32[]{:S(2)}, u32[]{:S(2)}) collective-permute-start(bf16[256,512]{1,0:T(8,128)(2,1)S(1)} %collective-permute-done.1), channel_id=1, source_target_pairs={{0,1},{1,0},{2,3},{3,2},{4,5},{5,4},{6,7},{7,6},{8,9},{9,8},{10,11... | collective-permute-start | bytes 786440 | tf_op jit(solution)/shard_map/ppermute | solution.py:92
  35.0 10.1 %collective-permute-start.3 = (bf16[256,512]{1,0:T(8,128)(2,1)S(1)}, bf16[256,512]{1,0:T(8,128)(2,1)S(1)}, u32[]{:S(2)}, u32[]{:S(2)}) collective-permute-start(bf16[256,512]{1,0:T(8,128)(2,1)S(1)} %collective-permute-done.1), channel_id=1, source_target_pairs={{0,4},{2,14},{4,8},{6,2},{8,12},{10,6},{12,0},{14,10},{1,5},{3,15}... | collective-permute-start | bytes 786440 | tf_op jit(solution)/shard_map/ppermute | solution.py:89
  35.3 10.1 %collective-permute-start.8 = (bf16[256,512]{1,0:T(8,128)(2,1)S(1)}, bf16[256,512]{1,0:T(8,128)(2,1)S(1)}, u32[]{:S(2)}, u32[]{:S(2)}) collective-permute-start(bf16[256,512]{1,0:T(8,128)(2,1)S(1)} %collective-permute-done.6), channel_id=1, source_target_pairs={{0,1},{1,0},{2,3},{3,2},{4,5},{5,4},{6,7},{7,6},{8,9},{9,8},{10,11... | collective-permute-start | bytes 786440 | tf_op jit(solution)/shard_map/ppermute | solution.py:92
  45.1 3.5 %collective-permute-start.7 = (bf16[256,512]{1,0:T(8,128)(2,1)S(1)}, bf16[256,512]{1,0:T(8,128)(2,1)S(1)}, u32[]{:S(2)}, u32[]{:S(2)}) collective-permute-start(bf16[256,512]{1,0:T(8,128)(2,1)S(1)} %collective-permute-done.5), channel_id=1, source_target_pairs={{0,1},{1,0},{2,3},{3,2},{4,5},{5,4},{6,7},{7,6},{8,9},{9,8},{10,11... | collective-permute-start | bytes 786440 | tf_op jit(solution)/shard_map/ppermute | solution.py:92
  45.4 1.9 %collective-permute-start.4 = (bf16[256,512]{1,0:T(8,128)(2,1)S(1)}, bf16[256,512]{1,0:T(8,128)(2,1)S(1)}, u32[]{:S(2)}, u32[]{:S(2)}) collective-permute-start(bf16[256,512]{1,0:T(8,128)(2,1)S(1)} %collective-permute-done.3), channel_id=1, source_target_pairs={{0,1},{1,0},{2,3},{3,2},{4,5},{5,4},{6,7},{7,6},{8,9},{9,8},{10,11... | collective-permute-start | bytes 786440 | tf_op jit(solution)/shard_map/ppermute | solution.py:92
  52.5 1.6 %copy-start.5 = (bf16[512,512]{1,0:T(8,128)(2,1)S(1)}, bf16[512,512]{1,0:T(8,128)(2,1)}, u32[]{:S(2)}) copy-start(bf16[512,512]{1,0:T(8,128)(2,1)} %param.9) | copy-start | bytes 1572868
  52.5 1.6 %copy-start.6 = (bf16[512,512]{1,0:T(8,128)(2,1)S(1)}, bf16[512,512]{1,0:T(8,128)(2,1)}, u32[]{:S(2)}) copy-start(bf16[512,512]{1,0:T(8,128)(2,1)} %get-tuple-element.24) | copy-start | bytes 1572868
  54.6 2.0 %collective-permute-start.10 = (bf16[512,512]{1,0:T(8,128)(2,1)S(1)}, bf16[512,512]{1,0:T(8,128)(2,1)S(1)}, u32[]{:S(2)}, u32[]{:S(2)}) collective-permute-start(bf16[512,512]{1,0:T(8,128)(2,1)S(1)} %fusion.6), channel_id=1, source_target_pairs={{0,1},{1,0},{2,3},{3,2},{4,5},{5,4},{6,7},{7,6},{8,9},{9,8},{10,11... | collective-permute-start | bytes 1572872 | tf_op jit(solution)/shard_map/ppermute | solution.py:92
  58.1 9.2 %collective-permute-start.13 = (bf16[256,512]{1,0:T(8,128)(2,1)S(1)}, bf16[256,512]{1,0:T(8,128)(2,1)S(1)}, u32[]{:S(2)}, u32[]{:S(2)}) collective-permute-start(bf16[256,512]{1,0:T(8,128)(2,1)S(1)} %get-tuple-element.26), channel_id=1, source_target_pairs={{4,0},{14,2},{8,4},{2,6},{12,8},{6,10},{0,12},{10,14},{5,1},{15,3}... | collective-permute-start | bytes 786440 | tf_op jit(solution)/shard_map/ppermute | solution.py:89
  58.2 14.1 %collective-permute-start.16 = (bf16[256,512]{1,0:T(8,128)(2,1)S(1)}, bf16[256,512]{1,0:T(8,128)(2,1)S(1)}, u32[]{:S(2)}, u32[]{:S(2)}) collective-permute-start(bf16[256,512]{1,0:T(8,128)(2,1)S(1)} %get-tuple-element.27), channel_id=1, source_target_pairs={{0,14},{2,4},{4,2},{6,8},{8,6},{10,12},{12,10},{14,0},{1,15},{3,5}... | collective-permute-start | bytes 786440 | tf_op jit(solution)/shard_map/ppermute | solution.py:89
  61.4 14.9 %collective-permute-start.15 = (bf16[256,512]{1,0:T(8,128)(2,1)S(1)}, bf16[256,512]{1,0:T(8,128)(2,1)S(1)}, u32[]{:S(2)}, u32[]{:S(2)}) collective-permute-start(bf16[256,512]{1,0:T(8,128)(2,1)S(1)} %slice.113), channel_id=1, source_target_pairs={{0,2},{2,0},{4,6},{6,4},{8,10},{10,8},{12,14},{14,12},{1,3},{3,1},... | collective-permute-start | bytes 786440 | tf_op jit(solution)/shard_map/ppermute | solution.py:89
  67.4 13.5 %collective-permute-start.14 = (bf16[256,512]{1,0:T(8,128)(2,1)S(1)}, bf16[256,512]{1,0:T(8,128)(2,1)S(1)}, u32[]{:S(2)}, u32[]{:S(2)}) collective-permute-start(bf16[256,512]{1,0:T(8,128)(2,1)S(1)} %fusion.10), channel_id=1, source_target_pairs={{0,2},{2,0},{4,6},{6,4},{8,10},{10,8},{12,14},{14,12},{1,3},{3,1},... | collective-permute-start | bytes 786440 | tf_op jit(solution)/shard_map/ppermute | solution.py:89

commit v2 on v1

v2 whole, which is shorter than its diff:
```python
import functools

import jax
import jax.numpy as jnp
from jax import lax
from jax.experimental import pallas as pl
from jax.experimental.pallas import tpu as pltpu
from jax.sharding import PartitionSpec as P

ROWS = ("parts", "slab", "sub")
VMEM = pl.BlockSpec(memory_space=pltpu.VMEM)
SMEM = pl.BlockSpec(memory_space=pltpu.SMEM)
ANY = pl.BlockSpec(memory_space=pl.ANY)


def dot(a, b):
    return jnp.dot(a, b, preferred_element_type=jnp.float32)


def dot_t(a, b):
    return lax.dot_general(a, b, (((1,), (1,)), ((), ())), preferred_element_type=jnp.float32)


def call(kernel, outs, *args, specs=None, out_specs=None, scratch=(), flops=1 << 26, name=None):
    single = not isinstance(outs, list)
    return pl.pallas_call(
        kernel,
        in_specs=specs or [VMEM] * len(args),
        out_specs=out_specs or (VMEM if single else [VMEM] * len(outs)),
        out_shape=outs,
        scratch_shapes=scratch,
        compiler_params=pltpu.CompilerParams(vmem_limit_bytes=12 << 20),
        cost_estimate=pl.CostEstimate(flops=1 << 36, bytes_accessed=1 << 30, transcendentals=0),
        name=name,
    )(*args)


OFFSET = {
    "own": lambda odd: 1,
    "pair": lambda odd: 2 - 2 * odd,
    "across": lambda odd: 2 * odd,
}


def dense_kernel(roles, known, info, sources, counts, tiles, *refs):
    count = len(roles)
    fwds, refs = refs[:known], refs[known:]
    outs, refs = refs[:count], refs[count:]
    last = len(refs) > 3
    if last:
        mine, send, buffer, total, in_sem, turned, out_sem = refs
    else:
        buffer, total, in_sem = refs
    local, slots, size = buffer.shape[1], buffer.shape[2], buffer.shape[3]
    rows = local * size
    u = info[1]
    offsets = [OFFSET[role](info[0]) for role in roles]

    def load(r, i):
        return pltpu.make_async_copy(tiles.at[i, offsets[r]], buffer.at[r, i], in_sem.at[r, i])

    def place_of(b):
        at = (b % local) * size
        return b // local, slice(at, at + size)

    stores = []

    def hand_out(n):
        for h, out in enumerate((mine, send)):
            part = pl.ds(n * rows, rows)
            store = pltpu.make_async_copy(turned.at[h, part], out.at[part], out_sem.at[h, n])
            store.start()
            stores.append(store)

    for r in range(count):
        for i in range(local):
            load(r, i).start()
    if last:
        for n, fwd in enumerate(fwds):
            for i in range(local):
                rows_i = slice(i * size, (i + 1) * size)
                for b in range(2 * local):
                    h, at = place_of(b)
                    block = fwd[rows_i, b * size:(b + 1) * size]
                    turned[h, n * rows + at.start:n * rows + at.stop, rows_i] = block.T
            hand_out(n)
    for r in range(count):
        n = known + r
        for i in range(local):
            load(r, i).wait()
            total[...] = jnp.zeros_like(total)
            for k in range(slots):
                b = sources[offsets[r], i, k]
                place = jnp.bitwise_xor(b // local, u) * local + b % local
                scale = counts[offsets[r], i, k].astype(jnp.float32) * (1.0 / size)
                total[place] += buffer[r, i, k].astype(jnp.float32) * scale
            rows_i = slice(i * size, (i + 1) * size)
            for b in range(2 * local):
                block = total[b].astype(outs[r].dtype)
                outs[r][rows_i, b * size:(b + 1) * size] = block
                if last:
                    h, at = place_of(b)
                    turned[h, n * rows + at.start:n * rows + at.stop, rows_i] = block.T
        if last:
            hand_out(n)
    for store in stores:
        store.wait()


def dense(roles, built, last, info, sources, counts, tiles):
    local, _, slots, size, _ = tiles.shape
    rows = local * size
    count, every = len(roles), len(roles) + len(built)
    kind = tiles.dtype
    hbm = pl.BlockSpec(memory_space=pltpu.HBM)
    outs = [jax.ShapeDtypeStruct((rows, 2 * rows), kind)] * count
    out_specs = [VMEM] * count
    scratch = [
        pltpu.VMEM((count, local, slots, size, size), kind),
        pltpu.VMEM((2 * local, size, size), jnp.float32),
        pltpu.SemaphoreType.DMA((count, local)),
    ]
    if last:
        outs += [pltpu.HBM((every * rows, rows), kind)] * 2
        out_specs += [hbm] * 2
        scratch += [
            pltpu.VMEM((2, every * rows, rows), kind),
            pltpu.SemaphoreType.DMA((2, every)),
        ]
    return call(
        functools.partial(dense_kernel, roles, len(built)),
        outs,
        info, sources, counts, tiles, *built,
        specs=[SMEM, SMEM, SMEM, hbm] + [VMEM] * len(built),
        out_specs=out_specs,
        scratch=scratch,
        flops=count << 28,
        name="dense_" + roles[0],
    )


def local_kernel(adj, x, x_sib, messages):
    rows = x.shape[0]
    messages[...] = dot(adj[:, :rows], x[...]) + dot(adj[:, rows:], x_sib[...])


def self_kernel(x, w_self, own):
    own[...] = dot(x[...], w_self[...])


def gather_kernel(starts, messages, *refs):
    count = len(starts)
    adjs, feats, out = refs[:count], refs[count:2 * count], refs[2 * count]
    total = messages[...]
    for start, adj, feat in zip(starts, adjs, feats):
        total += dot(adj[:, start:start + feat.shape[0]], feat[...])
    out[...] = total


def gather(messages, starts, adjs, feats):
    out = jax.ShapeDtypeStruct(messages.shape, jnp.float32)
    return call(functools.partial(gather_kernel, starts), out, messages, *adjs, *feats, name="gather")


def middle_kernel(
    start, messages, own, adj_x, adj_z, xb, zb, norm, w_neigh, cotangent,
    out, pre_grad, grad, out_buffer, sem,
):
    kind = out.dtype
    inverse = 1.0 / norm[...]
    total = messages[...] + dot(adj_x[:, start:], xb[...]) + dot(adj_z[:, start:], zb[...])
    aggregate = (total * inverse).astype(kind)
    v = own[...] + dot(aggregate, w_neigh[...])
    q = 1.0 / (1.0 + jnp.exp(-v))
    out_buffer[...] = (v * q).astype(kind)
    store = pltpu.make_async_copy(out_buffer, out, sem)
    store.start()
    p = (cotangent[...].astype(jnp.float32) * (q * (1.0 + v * (1.0 - q)))).astype(kind)
    pre_grad[...] = p
    grad[...] = (dot_t(p, w_neigh[...]) * inverse).astype(kind)
    store.wait()


def first_kernel(mine, g, tx, tz):
    rows = tz.shape[0]
    tx[...] = dot(mine[:rows, :], g[...])
    tz[...] = dot(mine[rows:2 * rows, :], g[...])


def second_kernel(theirs, g_sib, tx, tz, xa, xb, za, zb):
    cut, rows = za.shape[0], tz.shape[0]
    z = (tz[...] + dot(theirs[rows:2 * rows, :], g_sib[...])).astype(za.dtype)
    za[...] = z[:cut]
    zb[...] = z[cut:]
    x = tx[...] + dot(theirs[:rows, :], g_sib[...])
    xa[...] = x[:cut]
    xb[...] = x[cut:].astype(xb.dtype)


def add_kernel(a, b, out):
    out[...] = (a[...] + b[...].astype(jnp.float32)).astype(out.dtype)


def own_kernel(mine, theirs, g, g_sib, pre_grad, w_self, out):
    rows = out.shape[0]
    out[...] = (
        dot_t(pre_grad[...], w_self[...])
        + dot(mine[2 * rows:, :], g[...])
        + dot(theirs[2 * rows:, :], g_sib[...])
    )


def last_kernel(own, xa, xb, zb, out, buffer, sem):
    cut = xa.shape[0]
    high = own[cut:, :] + xb[...].astype(jnp.float32) + zb[...].astype(jnp.float32)
    buffer[cut:, :] = high.astype(out.dtype)
    upper = pltpu.make_async_copy(buffer.at[cut:], out.at[cut:], sem.at[0])
    upper.start()
    buffer[:cut, :] = (own[:cut, :] + xa[...].astype(jnp.float32)).astype(out.dtype)
    lower = pltpu.make_async_copy(buffer.at[:cut], out.at[:cut], sem.at[1])
    lower.start()
    upper.wait()
    lower.wait()


def after(value, *earlier):
    return lax.optimization_barrier((value, *earlier))[0]


def per_device(x, w_self, w_neigh, tiles, source_block, edge_counts, normalizer, cotangent):
    n_slab = lax.axis_size("slab")
    ring = range(n_slab)
    pair = [(i, i ^ 1) for i in ring]
    diag = [(i, (i + (1 if i % 2 else -1)) % n_slab) for i in ring]
    hop = [(i, (i + (-2 if i % 2 else 2)) % n_slab) for i in ring]
    back = [(b, a) for a, b in hop]
    swap = [(0, 1), (1, 0)]

    def slab(v, route):
        return lax.ppermute(v, "slab", route)

    def sub(v):
        return lax.ppermute(v, "sub", swap)

    rows, width = x.shape
    cut = rows // 2
    kind = x.dtype
    tiles = pltpu.with_memory_space_constraint(tiles, pltpu.HBM)
    odd = lax.bitwise_and(lax.axis_index("slab"), 1)
    norm = normalizer.astype(jnp.float32)[:, None]
    info = jnp.stack([odd, lax.axis_index("sub")]).astype(jnp.int32)
    sources = source_block.transpose(1, 0, 2)
    counts = edge_counts.transpose(1, 0, 2)
    wide = jax.ShapeDtypeStruct((rows, width), jnp.float32)
    narrow = jax.ShapeDtypeStruct((rows, width), kind)
    half = jax.ShapeDtypeStruct((cut, width), kind)
    half_wide = jax.ShapeDtypeStruct((cut, width), jnp.float32)

    xa = slab(x[:cut], pair)
    x_sib = sub(x)
    high = x[cut:]
    xb = slab(high, pair)
    (fx,) = dense(("pair",), (), False, after(info, high, norm, x_sib), sources, counts, tiles)
    zb = slab(after(high, fx), diag)
    xa = after(xa, fx)
    za = slab(xa, hop)
    xa_sib = sub(xa)
    fz, fo, mine, send = dense(
        ("across", "own"), (fx,), True, after(info, xa), sources, counts, tiles
    )
    theirs = sub(send)
    messages = call(local_kernel, wide, fo, x, x_sib, name="local")
    za = after(za, messages)
    za_sib = sub(za)
    messages = gather(messages, (0, rows), (fx, fx), (xa, xa_sib))
    xb, zb, theirs = lax.optimization_barrier((xb, zb, theirs, messages))[:3]
    xb_sib, zb_sib = sub(xb), sub(zb)
    messages = gather(messages, (0, rows, cut, cut), (fz, fz, fx, fz), (za, za_sib, xb, zb))
    own = call(self_kernel, wide, after(x, messages), w_self, name="self")
    node_out, pre_grad, g = call(
        functools.partial(middle_kernel, rows + cut),
        [narrow, narrow, narrow],
        messages, own, fx, fz, xb_sib, zb_sib, norm, w_neigh, cotangent,
        out_specs=[ANY, VMEM, VMEM],
        scratch=[pltpu.VMEM((rows, width), kind), pltpu.SemaphoreType.DMA],
        name="middle",
    )
    g_sib = sub(g)

    tx, tz = call(first_kernel, [wide, wide], mine, g, name="first")
    pxa, pxb, pza, pzb = call(
        second_kernel, [half_wide, half, half, half], theirs, g_sib, tx, tz, name="second"
    )
    ra = slab(pza, back)
    rxb = slab(pxb, pair)
    own_grad = call(own_kernel, wide, mine, theirs, g, g_sib, after(pre_grad, pxb), w_self, name="own")
    rzb = slab(after(pzb, own_grad), diag)
    rxa = slab(call(add_kernel, half, pxa, after(ra, own_grad), name="add"), pair)
    node_grad = call(
        last_kernel, narrow, own_grad, rxa, rxb, rzb,
        out_specs=ANY,
        scratch=[pltpu.VMEM((rows, width), kind), pltpu.SemaphoreType.DMA((2,))],
        name="last",
    )
    return (node_out, node_grad)


def solution(mesh):
    whole = P(None, None)
    return jax.shard_map(
        per_device,
        mesh=mesh,
        in_specs=(
            P(ROWS, None),
            whole,
            whole,
            P(ROWS, None, None, None, None),
            P(ROWS, None, None),
            P(ROWS, None, None),
            P(ROWS),
            P(ROWS, None),
        ),
        out_specs=(P(ROWS, None), P(ROWS, None)),
        check_vma=False,
    )
```

time: 82.4 us -> 62 us (0.75)
  matrix products: 19.1 us -> 0 us
  waiting for transfers between devices: 33.6 us -> 21.4 us
  Pallas kernels: 7.98 us -> 15.3 us
  starting transfers between devices: 14 us -> 18.2 us
    dot_general x19 -> x0, matrix products: 19.1 us -> none  [the longest x17 17 us: mm(): return jnp.dot(a, b, preferred_element_type=jnp.float32)]
    ppermute x8, waiting for transfers between devices: 32 us -> 20.2 us  [slab(): return lax.ppermute(v, 'slab', route)]
    pallas_call x3 -> x12, Pallas kernels: 7.98 us -> 15.3 us  [call(): pl.pallas_call(kernel, in_specs=specs or [VMEM] * len(args), out_specs=ou...]
    ppermute x8, starting transfers between devices: 11.4 us -> 16.8 us  [slab(): return lax.ppermute(v, 'slab', route)]
    ppermute x9 -> x7, starting transfers between devices: 2.61 us -> 1.46 us  [sub(): return lax.ppermute(v, 'sub', swap)]
    concatenate x1 -> x0, other arithmetic: 0.83 us -> none  [per_device(): node_grad = jnp.concatenate([low, high], axis=0).astype(kind)]
    unnamed x18 -> x20, local copies, waits for them, and re-layouts: 3.09 us -> 3.27 us
    slice x3 -> x1, local copies, waits for them, and re-layouts: 1.83 us -> 1.76 us  [per_device(): high = x[cut:]]
  transfers between devices with their start and end apart: 17 -> 15, of which waited for: 8 -> 7; matrix products, arithmetic and copies ran while one was open for 28% -> 4% of each run, Pallas kernels for 10% -> 19%
where the time goes in v2:
time: 62 us; the launch traced here: 61.7 us
  waiting for transfers between devices  21.4 us (35%)
  starting transfers between devices  18.2 us (29%)
  Pallas kernels  15.3 us (25%)
  local copies, waits for them, and re-layouts  5.18 us (8%)
  between operations  0.79 us (1%)
  other arithmetic  0.76 us (1%)
    ppermute x8, waiting for transfers between devices, slab(): return lax.ppermute(v, 'slab', route)  20.2 us
    ppermute x8, starting transfers between devices, slab(): return lax.ppermute(v, 'slab', route)  16.8 us
    pallas_call x12, Pallas kernels, call(): pl.pallas_call(kernel, in_specs=specs or [VMEM] * len(args), out_specs=ou...  15.3 us
    unnamed x20, local copies, waits for them, and re-layouts  3.27 us
    slice x1, local copies, waits for them, and re-layouts, per_device(): high = x[cut:]  1.76 us
    ppermute x7, starting transfers between devices, sub(): return lax.ppermute(v, 'sub', swap)  1.46 us
  transfers between devices with their start and end apart: 15, of which 7 were waited for; matrix products, arithmetic and copies ran while one was open for 4% of the time, Pallas kernels for 19%

profile of v2, /device:TPU:0, one launch (start us, length us, event | category | flops | bytes accessed | tf_op | source)
XLA Modules:
  0.0 61.7 jit_solution(6379100321277097953)
XLA Ops:
  0.6 0.5 collective-permute-start.1
  1.1 1.8 %fusion = (bf16[256,512]{1,0:T(8,128)(2,1)}, bf16[256,512]{1,0:T(8,128)(2,1)S(1)}) fusion(bf16[512,512]{1,0:T(8,128)(2,1)} %x.2), kind=kLoop, calls=%fused_computation.1 | loop fusion | bytes 1048576 | tf_op jit(solution)/shard_map/slice | solution.py:261
  2.9 2.5 %collective-permute-start = (bf16[256,512]{1,0:T(8,128)(2,1)S(1)}, bf16[256,512]{1,0:T(8,128)(2,1)S(1)}, u32[]{:S(2)}, u32[]{:S(2)}) collective-permute-start(bf16[256,512]{1,0:T(8,128)(2,1)S(1)} %get-tuple-element.53), channel_id=1, source_target_pairs={{0,2},{2,0},{4,6},{6,4},{8,10},{10,8},{12,14},{14,12},{1,3},{3,1},... | collective-permute-start | bytes 786440 | tf_op jit(solution)/shard_map/ppermute | solution.py:240
  5.4 0.0 collective-permute-start.5
  5.5 0.7 %convert_element_type.3 = f32[512]{0:T(512)S(1)} convert(s32[512]{0:T(512)} %param.14) | non-fusion elementwise | flops 512 | bytes 4096 | tf_op jit(solution)/shard_map/convert_element_type | solution.py:250
  6.1 0.1 copy.10.norm
  6.3 0.1 pad_add_fusion.info
  6.4 0.0 collective-permute-done.1.x_sib
  6.4 0.7 %copy-done.7 = s32[4,3,6]{2,0,1:T(4,128)S(1)} copy-done((s32[4,3,6]{2,0,1:T(4,128)S(1)}, s32[4,3,6]{2,0,1:T(4,128)}, u32[]{:S(2)}) %copy-start.7) | copy-done | bytes 312
  7.1 0.7 %copy-done.8 = s32[4,3,6]{2,0,1:T(4,128)S(1)} copy-done((s32[4,3,6]{2,0,1:T(4,128)S(1)}, s32[4,3,6]{2,0,1:T(4,128)}, u32[]{:S(2)}) %copy-start.8) | copy-done | bytes 312
  7.8 2.3 %dense_pair.1.refs_0_.refs_1_.refs_2_.adj_x = bf16[512,1024]{1,0:T(8,128)(2,1)S(1)} custom-call(s32[2]{0:T(128)S(1)} %pad_add_fusion.info, s32[3,4,6]{2,1,0:T(4,128)S(1)} %bitcast.5, s32[3,4,6]{2,1,0:T(4,128)S(1)} %bitcast.7, bf16[4,3,6,128,128]{4,3,2,1,0:T(8,128)(2,1)} %tiles.3), custom_call_target="tpu_custom_call" | custom-call | flops 68719476736 | bytes 1073741824 | tf_op jit(solution)/shard_map/dense_pair/pallas_call | solution.py:26
  10.0 0.0 copy-start
  10.0 2.5 %collective-permute-done.refs_2_ = bf16[256,512]{1,0:T(8,128)(2,1)S(1)} collective-permute-done((bf16[256,512]{1,0:T(8,128)(2,1)S(1)}, bf16[256,512]{1,0:T(8,128)(2,1)S(1)}, u32[]{:S(2)}, u32[]{:S(2)}) %collective-permute-start) | collective-permute-done | bytes 262176 | tf_op jit(solution)/shard_map/ppermute | solution.py:240
  12.6 2.0 %collective-permute-start.3 = (bf16[256,512]{1,0:T(8,128)(2,1)S(1)}, bf16[256,512]{1,0:T(8,128)(2,1)S(1)}, u32[]{:S(2)}, u32[]{:S(2)}) collective-permute-start(bf16[256,512]{1,0:T(8,128)(2,1)S(1)} %collective-permute-done.refs_2_), channel_id=1, source_target_pairs={{0,4},{2,14},{4,8},{6,2},{8,12},{10,6},{12,0},{14,10},{1,5},{3,15}... | collective-permute-start | bytes 786440 | tf_op jit(solution)/shard_map/ppermute | solution.py:240
  14.6 0.0 collective-permute-start.2
  14.6 3.4 %collective-permute-start.6 = (bf16[256,512]{1,0:T(8,128)(2,1)}, bf16[256,512]{1,0:T(8,128)(2,1)}, u32[]{:S(2)}, u32[]{:S(2)}) collective-permute-start(bf16[256,512]{1,0:T(8,128)(2,1)} %get-tuple-element.33), channel_id=1, source_target_pairs={{0,14},{2,4},{4,2},{6,8},{8,6},{10,12},{12,10},{14,0},{1,15},{3,5}... | collective-permute-start | bytes 786440 | tf_op jit(solution)/shard_map/ppermute | solution.py:240
  18.0 4.5 %dense_across.1 = (bf16[512,1024]{1,0:T(8,128)(2,1)S(1)}, bf16[512,1024]{1,0:T(8,128)(2,1)S(1)}, bf16[1536,512]{1,0:T(8,128)(2,1)}, bf16[1536,512]{1,0:T(8,128)(2,1)}) custom-call(s32[2]{0:T(128)S(1)} %pad_add_fusion.info, s32[3,4,6]{2,1,0:T(4,128)S(1)} %bitcast.6, s32[3,4,6]{2,1,0:T(4,128)S(1)} %bitcast.8, bf16[4,3,6,128,128]{4,3,2,1,0:T(8,128)(2,1)} %tiles.3, ...), custom_call_target="tpu_custom_call" | custom-call | flops 68719476736 | bytes 1073741824 | tf_op jit(solution)/shard_map/dense_across/pallas_call | solution.py:26
  22.6 0.3 collective-permute-start.7
  22.9 0.7 %local.1.messages = f32[512,512]{1,0:T(8,128)S(1)} custom-call(bf16[512,1024]{1,0:T(8,128)(2,1)S(1)} %get-tuple-element.30.adj, bf16[512,512]{1,0:T(8,128)(2,1)S(1)} %copy-done, bf16[512,512]{1,0:T(8,128)(2,1)S(1)} %collective-permute-done.1.x_sib), custom_call_target="tpu_custom_call" | custom-call | flops 68719476736 | bytes 1073741824 | tf_op jit(solution)/shard_map/local/pallas_call | solution.py:26
  23.6 0.3 collective-permute-done.3.refs_4_
  23.9 0.0 collective-permute-start.4
  23.9 0.4 gather.2.messages
  24.4 0.0 collective-permute-done.5.refs_6_
  24.4 4.8 %collective-permute-done.6.refs_7_ = bf16[256,512]{1,0:T(8,128)(2,1)} collective-permute-done((bf16[256,512]{1,0:T(8,128)(2,1)}, bf16[256,512]{1,0:T(8,128)(2,1)}, u32[]{:S(2)}, u32[]{:S(2)}) %collective-permute-start.6) | collective-permute-done | bytes 262176 | tf_op jit(solution)/shard_map/ppermute | solution.py:240
  29.2 1.1 %copy-done.1 = bf16[1536,512]{1,0:T(8,128)(2,1)} copy-done((bf16[1536,512]{1,0:T(8,128)(2,1)}, bf16[1536,512]{1,0:T(8,128)(2,1)S(1)}, u32[]{:S(2)}) %copy-start.1) | copy-done | bytes 1572888
  30.4 0.0 collective-permute-start.8
  30.4 0.5 collective-permute-start.9
  30.9 0.0 collective-permute-done.4.refs_5_
  30.9 1.8 %gather.3.messages = f32[512,512]{1,0:T(8,128)S(1)} custom-call(f32[512,512]{1,0:T(8,128)S(1)} %gather.2.messages, bf16[512,1024]{1,0:T(8,128)(2,1)S(1)} %get-tuple-element.31.refs_0_.refs_1_.refs_3_.adj_z, bf16[512,1024]{1,0:T(8,128)(2,1)S(1)} %get-tuple-element.31.refs_0_.refs_1_.refs_3_.adj_z, ...), custom_call_target="tpu_custom_call" | custom-call | flops 68719476736 | bytes 1073741824 | tf_op jit(solution)/shard_map/gather/pallas_call | solution.py:26
  32.7 0.0 copy-start.3
  32.7 0.0 copy-start.4
  32.7 0.4 self.1.own
  33.2 0.6 copy-done.3
  33.7 0.2 copy-done.4
  33.9 1.8 %middle.1 = (bf16[512,512]{1,0:T(8,128)(2,1)}, bf16[512,512]{1,0:T(8,128)(2,1)S(1)}, bf16[512,512]{1,0:T(8,128)(2,1)S(1)}) custom-call(f32[512,512]{1,0:T(8,128)S(1)} %gather.3.messages, f32[512,512]{1,0:T(8,128)S(1)} %self.1.own, bf16[512,1024]{1,0:T(8,128)(2,1)S(1)} %dense_pair.1.refs_0_.refs_1_.refs_2_.adj_x, ...), custom_call_target="tpu_custom_call" | custom-call | flops 68719476736 | bytes 1073741824 | tf_op jit(solution)/shard_map/middle/pallas_call | solution.py:26
  35.8 0.1 collective-permute-start.10
  35.9 0.7 %first.1 = (f32[512,512]{1,0:T(8,128)S(1)}, f32[512,512]{1,0:T(8,128)S(1)}) custom-call(bf16[1536,512]{1,0:T(8,128)(2,1)S(1)} %copy-done.9, bf16[512,512]{1,0:T(8,128)(2,1)S(1)} %get-tuple-element.41.g), custom_call_target="tpu_custom_call" | custom-call | flops 68719476736 | bytes 1073741824 | tf_op jit(solution)/shard_map/first/pallas_call | solution.py:26
  36.6 1.2 %collective-permute-done.10.g_sib = bf16[512,512]{1,0:T(8,128)(2,1)S(1)} collective-permute-done((bf16[512,512]{1,0:T(8,128)(2,1)S(1)}, bf16[512,512]{1,0:T(8,128)(2,1)S(1)}, u32[]{:S(2)}, u32[]{:S(2)}) %collective-permute-start.10) | collective-permute-done | bytes 524320 | tf_op jit(solution)/shard_map/ppermute | solution.py:243
  37.7 0.7 %second.1 = (f32[256,512]{1,0:T(8,128)S(1)}, bf16[256,512]{1,0:T(8,128)(2,1)S(1)}, bf16[256,512]{1,0:T(8,128)(2,1)S(1)}, bf16[256,512]{1,0:T(8,128)(2,1)S(1)}) custom-call(bf16[1536,512]{1,0:T(8,128)(2,1)S(1)} %copy-done.2, bf16[512,512]{1,0:T(8,128)(2,1)S(1)} %collective-permute-done.10.g_sib, f32[512,512]{1,0:T(8,128)S(1)} %get-tuple-element.43.tx, ...), custom_call_target="tpu_custom_call" | custom-call | flops 68719476736 | bytes 1073741824 | tf_op jit(solution)/shard_map/second/pallas_call | solution.py:26
  38.5 0.5 collective-permute-start.13
  39.0 2.6 %collective-permute-start.11 = (bf16[256,512]{1,0:T(8,128)(2,1)S(1)}, bf16[256,512]{1,0:T(8,128)(2,1)S(1)}, u32[]{:S(2)}, u32[]{:S(2)}) collective-permute-start(bf16[256,512]{1,0:T(8,128)(2,1)S(1)} %get-tuple-element.48), channel_id=1, source_target_pairs={{4,0},{14,2},{8,4},{2,6},{12,8},{6,10},{0,12},{10,14},{5,1},{15,3}... | collective-permute-start | bytes 786440 | tf_op jit(solution)/shard_map/ppermute | solution.py:240
  41.5 1.0 %own.1 = f32[512,512]{1,0:T(8,128)S(1)} custom-call(bf16[1536,512]{1,0:T(8,128)(2,1)S(1)} %copy-done.9, bf16[1536,512]{1,0:T(8,128)(2,1)S(1)} %copy-done.2, bf16[512,512]{1,0:T(8,128)(2,1)S(1)} %get-tuple-element.41.g, bf16[512,512]{1,0:T(8,128)(2,1)S(1)} %collective-permute-done.10.g_sib, bf16[512,512]{1,0:T(8,128)(2,1)S(1)} %get-tuple-element.46.pre_grad, ...), custom_call_target="tpu_custom_call" | custom-call | flops 68719476736 | bytes 1073741824 | tf_op jit(solution)/shard_map/own/pallas_call | solution.py:26
  42.5 2.3 %collective-permute-start.14 = (bf16[256,512]{1,0:T(8,128)(2,1)S(1)}, bf16[256,512]{1,0:T(8,128)(2,1)S(1)}, u32[]{:S(2)}, u32[]{:S(2)}) collective-permute-start(bf16[256,512]{1,0:T(8,128)(2,1)S(1)} %get-tuple-element.51), channel_id=1, source_target_pairs={{0,14},{2,4},{4,2},{6,8},{8,6},{10,12},{12,10},{14,0},{1,15},{3,5}... | collective-permute-start | bytes 786440 | tf_op jit(solution)/shard_map/ppermute | solution.py:240
  44.8 3.4 %collective-permute-done.11.b = bf16[256,512]{1,0:T(8,128)(2,1)S(1)} collective-permute-done((bf16[256,512]{1,0:T(8,128)(2,1)S(1)}, bf16[256,512]{1,0:T(8,128)(2,1)S(1)}, u32[]{:S(2)}, u32[]{:S(2)}) %collective-permute-start.11) | collective-permute-done | bytes 262176 | tf_op jit(solution)/shard_map/ppermute | solution.py:240
  48.3 3.4 %collective-permute-start.12 = (bf16[256,512]{1,0:T(8,128)(2,1)S(1)}, bf16[256,512]{1,0:T(8,128)(2,1)S(1)}, u32[]{:S(2)}, u32[]{:S(2)}) collective-permute-start(bf16[256,512]{1,0:T(8,128)(2,1)S(1)} %add.3), channel_id=1, source_target_pairs={{0,2},{2,0},{4,6},{6,4},{8,10},{10,8},{12,14},{14,12},{1,3},{3,1},... | collective-permute-start | bytes 786440 | tf_op jit(solution)/shard_map/ppermute | solution.py:240
  51.6 3.9 %collective-permute-done.14.zb = bf16[256,512]{1,0:T(8,128)(2,1)S(1)} collective-permute-done((bf16[256,512]{1,0:T(8,128)(2,1)S(1)}, bf16[256,512]{1,0:T(8,128)(2,1)S(1)}, u32[]{:S(2)}, u32[]{:S(2)}) %collective-permute-start.14) | collective-permute-done | bytes 262176 | tf_op jit(solution)/shard_map/ppermute | solution.py:240
  55.6 5.2 %collective-permute-done.12.xa = bf16[256,512]{1,0:T(8,128)(2,1)S(1)} collective-permute-done((bf16[256,512]{1,0:T(8,128)(2,1)S(1)}, bf16[256,512]{1,0:T(8,128)(2,1)S(1)}, u32[]{:S(2)}, u32[]{:S(2)}) %collective-permute-start.12) | collective-permute-done | bytes 262176 | tf_op jit(solution)/shard_map/ppermute | solution.py:240
  60.8 0.9 %last.1 = bf16[512,512]{1,0:T(8,128)(2,1)} custom-call(f32[512,512]{1,0:T(8,128)S(1)} %own.1, bf16[256,512]{1,0:T(8,128)(2,1)S(1)} %collective-permute-done.12.xa, bf16[256,512]{1,0:T(8,128)(2,1)S(1)} %collective-permute-done.13.xb, bf16[256,512]{1,0:T(8,128)(2,1)S(1)} %collective-permute-done.14.zb), custom_call_target="tpu_custom_call" | custom-call | flops 68719476736 | bytes 1073741824 | tf_op jit(solution)/shard_map/last/pallas_call | solution.py:26
  (18 shorter events, 0.1 us)
Async XLA Ops:
  0.6 5.7 %collective-permute-start.1 = (bf16[512,512]{1,0:T(8,128)(2,1)}, bf16[512,512]{1,0:T(8,128)(2,1)S(1)}, u32[]{:S(2)}, u32[]{:S(2)}) collective-permute-start(bf16[512,512]{1,0:T(8,128)(2,1)} %x.2), channel_id=1, source_target_pairs={{0,1},{1,0},{2,3},{3,2},{4,5},{5,4},{6,7},{7,6},{8,9},{9,8},{10,11... | collective-permute-start | bytes 1572872 | tf_op jit(solution)/shard_map/ppermute | solution.py:243
  2.9 9.7 %collective-permute-start = (bf16[256,512]{1,0:T(8,128)(2,1)S(1)}, bf16[256,512]{1,0:T(8,128)(2,1)S(1)}, u32[]{:S(2)}, u32[]{:S(2)}) collective-permute-start(bf16[256,512]{1,0:T(8,128)(2,1)S(1)} %get-tuple-element.53), channel_id=1, source_target_pairs={{0,2},{2,0},{4,6},{6,4},{8,10},{10,8},{12,14},{14,12},{1,3},{3,1},... | collective-permute-start | bytes 786440 | tf_op jit(solution)/shard_map/ppermute | solution.py:240
  5.4 19.0 %collective-permute-start.5 = (bf16[256,512]{1,0:T(8,128)(2,1)}, bf16[256,512]{1,0:T(8,128)(2,1)}, u32[]{:S(2)}, u32[]{:S(2)}) collective-permute-start(bf16[256,512]{1,0:T(8,128)(2,1)} %get-tuple-element.33), channel_id=1, source_target_pairs={{0,2},{2,0},{4,6},{6,4},{8,10},{10,8},{12,14},{14,12},{1,3},{3,1},... | collective-permute-start | bytes 786440 | tf_op jit(solution)/shard_map/ppermute | solution.py:240
  6.4 0.7 %copy-start.7 = (s32[4,3,6]{2,0,1:T(4,128)S(1)}, s32[4,3,6]{2,0,1:T(4,128)}, u32[]{:S(2)}) copy-start(s32[4,3,6]{2,0,1:T(4,128)} %param.12) | copy-start | bytes 868
  7.1 0.7 %copy-start.8 = (s32[4,3,6]{2,0,1:T(4,128)S(1)}, s32[4,3,6]{2,0,1:T(4,128)}, u32[]{:S(2)}) copy-start(s32[4,3,6]{2,0,1:T(4,128)} %param.13) | copy-start | bytes 868
  10.0 12.8 %copy-start = (bf16[512,512]{1,0:T(8,128)(2,1)S(1)}, bf16[512,512]{1,0:T(8,128)(2,1)}, u32[]{:S(2)}) copy-start(bf16[512,512]{1,0:T(8,128)(2,1)} %x.2) | copy-start | bytes 1572868
  12.6 11.3 %collective-permute-start.3 = (bf16[256,512]{1,0:T(8,128)(2,1)S(1)}, bf16[256,512]{1,0:T(8,128)(2,1)S(1)}, u32[]{:S(2)}, u32[]{:S(2)}) collective-permute-start(bf16[256,512]{1,0:T(8,128)(2,1)S(1)} %collective-permute-done.refs_2_), channel_id=1, source_target_pairs={{0,4},{2,14},{4,8},{6,2},{8,12},{10,6},{12,0},{14,10},{1,5},{3,15}... | collective-permute-start | bytes 786440 | tf_op jit(solution)/shard_map/ppermute | solution.py:240
  14.6 9.3 %collective-permute-start.2 = (bf16[256,512]{1,0:T(8,128)(2,1)S(1)}, bf16[256,512]{1,0:T(8,128)(2,1)S(1)}, u32[]{:S(2)}, u32[]{:S(2)}) collective-permute-start(bf16[256,512]{1,0:T(8,128)(2,1)S(1)} %collective-permute-done.refs_2_), channel_id=1, source_target_pairs={{0,1},{1,0},{2,3},{3,2},{4,5},{5,4},{6,7},{7,6},{8,9},{9,8},{10,11... | collective-permute-start | bytes 786440 | tf_op jit(solution)/shard_map/ppermute | solution.py:243
  14.6 14.6 %collective-permute-start.6 = (bf16[256,512]{1,0:T(8,128)(2,1)}, bf16[256,512]{1,0:T(8,128)(2,1)}, u32[]{:S(2)}, u32[]{:S(2)}) collective-permute-start(bf16[256,512]{1,0:T(8,128)(2,1)} %get-tuple-element.33), channel_id=1, source_target_pairs={{0,14},{2,4},{4,2},{6,8},{8,6},{10,12},{12,10},{14,0},{1,15},{3,5}... | collective-permute-start | bytes 786440 | tf_op jit(solution)/shard_map/ppermute | solution.py:240
  22.6 6.7 %collective-permute-start.7 = (bf16[1536,512]{1,0:T(8,128)(2,1)}, bf16[1536,512]{1,0:T(8,128)(2,1)S(1)}, u32[]{:S(2)}, u32[]{:S(2)}) collective-permute-start(bf16[1536,512]{1,0:T(8,128)(2,1)} %get-tuple-element.34), channel_id=1, source_target_pairs={{0,1},{1,0},{2,3},{3,2},{4,5},{5,4},{6,7},{7,6},{8,9},{9,8},{10,11... | collective-permute-start | bytes 4718600 | tf_op jit(solution)/shard_map/ppermute | solution.py:243
  23.9 7.0 %collective-permute-start.4 = (bf16[256,512]{1,0:T(8,128)(2,1)S(1)}, bf16[256,512]{1,0:T(8,128)(2,1)S(1)}, u32[]{:S(2)}, u32[]{:S(2)}) collective-permute-start(bf16[256,512]{1,0:T(8,128)(2,1)S(1)} %collective-permute-done.3.refs_4_), channel_id=1, source_target_pairs={{0,1},{1,0},{2,3},{3,2},{4,5},{5,4},{6,7},{7,6},{8,9},{9,8},{10,11... | collective-permute-start | bytes 786440 | tf_op jit(solution)/shard_map/ppermute | solution.py:243
  29.2 1.1 %copy-start.1 = (bf16[1536,512]{1,0:T(8,128)(2,1)}, bf16[1536,512]{1,0:T(8,128)(2,1)S(1)}, u32[]{:S(2)}) copy-start(bf16[1536,512]{1,0:T(8,128)(2,1)S(1)} %collective-permute-done.7.theirs) | copy-start | bytes 4718596
  30.4 2.8 %collective-permute-start.8 = (bf16[256,512]{1,0:T(8,128)(2,1)}, bf16[256,512]{1,0:T(8,128)(2,1)S(1)}, u32[]{:S(2)}, u32[]{:S(2)}) collective-permute-start(bf16[256,512]{1,0:T(8,128)(2,1)} %collective-permute-done.5.refs_6_), channel_id=1, source_target_pairs={{0,1},{1,0},{2,3},{3,2},{4,5},{5,4},{6,7},{7,6},{8,9},{9,8},{10,11... | collective-permute-start | bytes 786440 | tf_op jit(solution)/shard_map/ppermute | solution.py:243
  30.4 2.8 %collective-permute-start.9 = (bf16[256,512]{1,0:T(8,128)(2,1)}, bf16[256,512]{1,0:T(8,128)(2,1)S(1)}, u32[]{:S(2)}, u32[]{:S(2)}) collective-permute-start(bf16[256,512]{1,0:T(8,128)(2,1)} %collective-permute-done.6.refs_7_), channel_id=1, source_target_pairs={{0,1},{1,0},{2,3},{3,2},{4,5},{5,4},{6,7},{7,6},{8,9},{9,8},{10,11... | collective-permute-start | bytes 786440 | tf_op jit(solution)/shard_map/ppermute | solution.py:243
  30.9 1.8 %copy-start.5 = (bf16[512,512]{1,0:T(8,128)(2,1)S(1)}, bf16[512,512]{1,0:T(8,128)(2,1)}, u32[]{:S(2)}) copy-start(bf16[512,512]{1,0:T(8,128)(2,1)} %w_self.3) | copy-start | bytes 1572868
  32.7 1.0 %copy-start.3 = (bf16[512,512]{1,0:T(8,128)(2,1)S(1)}, bf16[512,512]{1,0:T(8,128)(2,1)}, u32[]{:S(2)}) copy-start(bf16[512,512]{1,0:T(8,128)(2,1)} %w_neigh.1) | copy-start | bytes 1572868
  32.7 1.2 %copy-start.4 = (bf16[512,512]{1,0:T(8,128)(2,1)S(1)}, bf16[512,512]{1,0:T(8,128)(2,1)}, u32[]{:S(2)}) copy-start(bf16[512,512]{1,0:T(8,128)(2,1)} %cotangent.1) | copy-start | bytes 1572868
  33.2 2.7 %copy-start.9 = (bf16[1536,512]{1,0:T(8,128)(2,1)S(1)}, bf16[1536,512]{1,0:T(8,128)(2,1)}, u32[]{:S(2)}) copy-start(bf16[1536,512]{1,0:T(8,128)(2,1)} %get-tuple-element.39.mine) | copy-start | bytes 4718596
  35.8 2.0 %collective-permute-start.10 = (bf16[512,512]{1,0:T(8,128)(2,1)S(1)}, bf16[512,512]{1,0:T(8,128)(2,1)S(1)}, u32[]{:S(2)}, u32[]{:S(2)}) collective-permute-start(bf16[512,512]{1,0:T(8,128)(2,1)S(1)} %get-tuple-element.41.g), channel_id=1, source_target_pairs={{0,1},{1,0},{2,3},{3,2},{4,5},{5,4},{6,7},{7,6},{8,9},{9,8},{10,11... | collective-permute-start | bytes 1572872 | tf_op jit(solution)/shard_map/ppermute | solution.py:243
  35.8 1.9 %copy-start.2 = (bf16[1536,512]{1,0:T(8,128)(2,1)S(1)}, bf16[1536,512]{1,0:T(8,128)(2,1)}, u32[]{:S(2)}) copy-start(bf16[1536,512]{1,0:T(8,128)(2,1)} %copy-done.1) | copy-start | bytes 4718596
  37.7 3.8 %copy-start.6 = (bf16[512,512]{1,0:T(8,128)(2,1)S(1)}, bf16[512,512]{1,0:T(8,128)(2,1)}, u32[]{:S(2)}) copy-start(bf16[512,512]{1,0:T(8,128)(2,1)} %w_self.3) | copy-start | bytes 1572868
  38.5 17.1 %collective-permute-start.13 = (bf16[256,512]{1,0:T(8,128)(2,1)S(1)}, bf16[256,512]{1,0:T(8,128)(2,1)S(1)}, u32[]{:S(2)}, u32[]{:S(2)}) collective-permute-start(bf16[256,512]{1,0:T(8,128)(2,1)S(1)} %get-tuple-element.45), channel_id=1, source_target_pairs={{0,2},{2,0},{4,6},{6,4},{8,10},{10,8},{12,14},{14,12},{1,3},{3,1},... | collective-permute-start | bytes 786440 | tf_op jit(solution)/shard_map/ppermute | solution.py:240
  39.0 9.2 %collective-permute-start.11 = (bf16[256,512]{1,0:T(8,128)(2,1)S(1)}, bf16[256,512]{1,0:T(8,128)(2,1)S(1)}, u32[]{:S(2)}, u32[]{:S(2)}) collective-permute-start(bf16[256,512]{1,0:T(8,128)(2,1)S(1)} %get-tuple-element.48), channel_id=1, source_target_pairs={{4,0},{14,2},{8,4},{2,6},{12,8},{6,10},{0,12},{10,14},{5,1},{15,3}... | collective-permute-start | bytes 786440 | tf_op jit(solution)/shard_map/ppermute | solution.py:240
  42.5 13.0 %collective-permute-start.14 = (bf16[256,512]{1,0:T(8,128)(2,1)S(1)}, bf16[256,512]{1,0:T(8,128)(2,1)S(1)}, u32[]{:S(2)}, u32[]{:S(2)}) collective-permute-start(bf16[256,512]{1,0:T(8,128)(2,1)S(1)} %get-tuple-element.51), channel_id=1, source_target_pairs={{0,14},{2,4},{4,2},{6,8},{8,6},{10,12},{12,10},{14,0},{1,15},{3,5}... | collective-permute-start | bytes 786440 | tf_op jit(solution)/shard_map/ppermute | solution.py:240
  48.3 12.5 %collective-permute-start.12 = (bf16[256,512]{1,0:T(8,128)(2,1)S(1)}, bf16[256,512]{1,0:T(8,128)(2,1)S(1)}, u32[]{:S(2)}, u32[]{:S(2)}) collective-permute-start(bf16[256,512]{1,0:T(8,128)(2,1)S(1)} %add.3), channel_id=1, source_target_pairs={{0,2},{2,0},{4,6},{6,4},{8,10},{10,8},{12,14},{14,12},{1,3},{3,1},... | collective-permute-start | bytes 786440 | tf_op jit(solution)/shard_map/ppermute | solution.py:240

commit v3 on v2

v3 whole, which is shorter than its diff:
```python
import functools

import jax
import jax.numpy as jnp
from jax import lax
from jax.experimental import pallas as pl
from jax.experimental.pallas import tpu as pltpu
from jax.sharding import PartitionSpec as P

ROWS = ("parts", "slab", "sub")
VMEM = pl.BlockSpec(memory_space=pltpu.VMEM)
ANY = pl.BlockSpec(memory_space=pl.ANY)


def dot(a, b):
    return jnp.dot(a, b, preferred_element_type=jnp.float32)


def dot_t(a, b):
    return lax.dot_general(a, b, (((1,), (1,)), ((), ())), preferred_element_type=jnp.float32)


def call(kernel, outs, *args, specs=None, out_specs=None, scratch=(), flops=1 << 34, name=None):
    single = not isinstance(outs, list)
    return pl.pallas_call(
        kernel,
        in_specs=specs or [VMEM] * len(args),
        out_specs=out_specs or (VMEM if single else [VMEM] * len(outs)),
        out_shape=outs,
        scratch_shapes=scratch,
        compiler_params=pltpu.CompilerParams(vmem_limit_bytes=12 << 20),
        cost_estimate=pl.CostEstimate(flops=flops, bytes_accessed=flops >> 8, transcendentals=0),
        name=name,
    )(*args)


OFFSET = {
    "own": lambda odd: 1,
    "pair": lambda odd: 2 - 2 * odd,
    "across": lambda odd: 2 * odd,
}


def dense_kernel(roles, known, sources_hbm, counts_hbm, tiles, *refs):
    count = len(roles)
    fwds, refs = refs[:known], refs[known:]
    outs, refs = refs[:count], refs[count:]
    last = len(refs) > 6
    if last:
        mine, send, buffer, total, in_sem, sources, counts, index_sem, turned, out_sem = refs
    else:
        buffer, total, in_sem, sources, counts, index_sem = refs
    local, slots, size = buffer.shape[1], buffer.shape[2], buffer.shape[3]
    rows = local * size
    u = lax.axis_index("sub")
    odd = lax.bitwise_and(lax.axis_index("slab"), 1)
    offsets = [OFFSET[role](odd) for role in roles]
    indices = [
        pltpu.make_async_copy(source, target, index_sem.at[n])
        for n, (source, target) in enumerate(((sources_hbm, sources), (counts_hbm, counts)))
    ]
    for copy in indices:
        copy.start()

    def load(r, i):
        return pltpu.make_async_copy(tiles.at[i, offsets[r]], buffer.at[r, i], in_sem.at[r, i])

    def place_of(b):
        at = (b % local) * size
        return b // local, slice(at, at + size)

    stores = []

    def hand_out(n):
        for h, out in enumerate((mine, send)):
            part = pl.ds(n * rows, rows)
            store = pltpu.make_async_copy(turned.at[h, part], out.at[part], out_sem.at[h, n])
            store.start()
            stores.append(store)

    for r in range(count):
        for i in range(local):
            load(r, i).start()
    if last:
        for n, fwd in enumerate(fwds):
            for i in range(local):
                rows_i = slice(i * size, (i + 1) * size)
                for b in range(2 * local):
                    h, at = place_of(b)
                    block = fwd[rows_i, b * size:(b + 1) * size]
                    turned[h, n * rows + at.start:n * rows + at.stop, rows_i] = block.T
            hand_out(n)
    for copy in indices:
        copy.wait()
    for r in range(count):
        n = known + r
        for i in range(local):
            load(r, i).wait()
            total[...] = jnp.zeros_like(total)
            for k in range(slots):
                b = sources[offsets[r], i, k]
                place = jnp.bitwise_xor(b // local, u) * local + b % local
                scale = counts[offsets[r], i, k].astype(jnp.float32) * (1.0 / size)
                total[place] += buffer[r, i, k].astype(jnp.float32) * scale
            rows_i = slice(i * size, (i + 1) * size)
            for b in range(2 * local):
                block = total[b].astype(outs[r].dtype)
                outs[r][rows_i, b * size:(b + 1) * size] = block
                if last:
                    h, at = place_of(b)
                    turned[h, n * rows + at.start:n * rows + at.stop, rows_i] = block.T
        if last:
            hand_out(n)
    for store in stores:
        store.wait()


def dense(roles, built, last, sources, counts, tiles):
    local, _, slots, size, _ = tiles.shape
    rows = local * size
    count, every = len(roles), len(roles) + len(built)
    kind = tiles.dtype
    hbm = pl.BlockSpec(memory_space=pltpu.HBM)
    outs = [jax.ShapeDtypeStruct((rows, 2 * rows), kind)] * count
    out_specs = [VMEM] * count
    scratch = [
        pltpu.VMEM((count, local, slots, size, size), kind),
        pltpu.VMEM((2 * local, size, size), jnp.float32),
        pltpu.SemaphoreType.DMA((count, local)),
        pltpu.SMEM(sources.shape, jnp.int32),
        pltpu.SMEM(counts.shape, jnp.int32),
        pltpu.SemaphoreType.DMA((2,)),
    ]
    if last:
        outs += [pltpu.HBM((every * rows, rows), kind)] * 2
        out_specs += [hbm] * 2
        scratch += [
            pltpu.VMEM((2, every * rows, rows), kind),
            pltpu.SemaphoreType.DMA((2, every)),
        ]
    sources, counts = (pltpu.with_memory_space_constraint(v, pltpu.HBM) for v in (sources, counts))
    return call(
        functools.partial(dense_kernel, roles, len(built)),
        outs,
        sources, counts, tiles, *built,
        specs=[hbm] * 3 + [VMEM] * len(built),
        out_specs=out_specs,
        scratch=scratch,
        flops=count << 26,
        name="dense_" + roles[0],
    )


def split_kernel(x, low, high, sems):
    cut = low.shape[0]
    parts = [
        pltpu.make_async_copy(x.at[:cut], low, sems.at[0]),
        pltpu.make_async_copy(x.at[cut:], high, sems.at[1]),
    ]
    for part in parts:
        part.start()
    for part in parts:
        part.wait()


def local_kernel(adj, x, x_sib, w_self, messages, own):
    rows = x.shape[0]
    messages[...] = dot(adj[:, :rows], x[...]) + dot(adj[:, rows:], x_sib[...])
    own[...] = dot(x[...], w_self[...])


def gather_kernel(starts, messages, *refs):
    count = len(starts)
    adjs, feats, out = refs[:count], refs[count:2 * count], refs[2 * count]
    total = messages[...]
    for start, adj, feat in zip(starts, adjs, feats):
        total += dot(adj[:, start:start + feat.shape[0]], feat[...])
    out[...] = total


def gather(messages, starts, adjs, feats):
    out = jax.ShapeDtypeStruct(messages.shape, jnp.float32)
    return call(functools.partial(gather_kernel, starts), out, messages, *adjs, *feats, name="gather")


def middle_kernel(
    start, messages, own, adj, last, norm, w_neigh, cotangent,
    out, pre_grad, grad, out_buffer, sem,
):
    kind = out.dtype
    across = (1.0 / norm[...].astype(jnp.float32)).T
    inverse = jnp.concatenate([across[:, b:b + 1] for b in range(across.shape[1])], axis=0)
    total = messages[...] + dot(adj[:, start:], last[...])
    aggregate = (total * inverse).astype(kind)
    v = own[...] + dot(aggregate, w_neigh[...])
    q = 1.0 / (1.0 + jnp.exp(-v))
    out_buffer[...] = (v * q).astype(kind)
    store = pltpu.make_async_copy(out_buffer, out, sem)
    store.start()
    p = (cotangent[...].astype(jnp.float32) * (q * (1.0 + v * (1.0 - q)))).astype(kind)
    pre_grad[...] = p
    grad[...] = (dot_t(p, w_neigh[...]) * inverse).astype(kind)
    store.wait()


def first_kernel(mine, g, theirs, tx, tz, kept, sem):
    rows = tz.shape[0]
    fetch = pltpu.make_async_copy(theirs.at[:2 * rows], kept, sem)
    fetch.start()
    tx[...] = dot(mine[:rows, :], g[...])
    tz[...] = dot(mine[rows:2 * rows, :], g[...])
    fetch.wait()


def second_kernel(theirs, g_sib, tx, tz, px, *pz):
    rows, step = tz.shape[0], pz[0].shape[0]
    z = (tz[...] + dot(theirs[rows:2 * rows, :], g_sib[...])).astype(pz[0].dtype)
    for n, part in enumerate(pz):
        part[...] = z[n * step:(n + 1) * step]
    px[...] = tx[...] + dot(theirs[:rows, :], g_sib[...])


def add_kernel(start, px, b, out):
    part = px[start:start + b.shape[0], :]
    out[...] = (part + b[...].astype(jnp.float32)).astype(out.dtype)


def own_kernel(mine, theirs, g, g_sib, pre_grad, w_self, out):
    rows = out.shape[0]
    out[...] = (
        dot_t(pre_grad[...], w_self[...])
        + dot(mine[2 * rows:, :], g[...])
        + dot(theirs[2 * rows:, :], g_sib[...])
    )


def last_kernel(own, *refs):
    parts, (out, buffer, sem) = refs[:-3], refs[-3:]
    step = parts[0].shape[0]
    stores = []
    for n, part in enumerate(parts):
        at = pl.ds(n * step, step)
        buffer[at, :] = (own[at, :] + part[...].astype(jnp.float32)).astype(out.dtype)
        store = pltpu.make_async_copy(buffer.at[at], out.at[at], sem.at[n])
        store.start()
        stores.append(store)
    for store in stores:
        store.wait()


def after(value, *earlier):
    return lax.optimization_barrier((value, *earlier))[0]


def per_device(x, w_self, w_neigh, tiles, source_block, edge_counts, normalizer, cotangent):
    n_slab = lax.axis_size("slab")
    ring = range(n_slab)
    pair = [(i, i ^ 1) for i in ring]
    hop = [(i, (i + (-2 if i % 2 else 2)) % n_slab) for i in ring]
    back = [(b, a) for a, b in hop]
    swap = [(0, 1), (1, 0)]

    def slab(v, route):
        return lax.ppermute(v, "slab", route)

    def sub(v):
        return lax.ppermute(v, "sub", swap)

    rows, width = x.shape
    cut = rows // 2
    kind = x.dtype
    tiles = pltpu.with_memory_space_constraint(tiles, pltpu.HBM)
    block = tiles.shape[-1]
    norm = normalizer.reshape(rows // block, block)
    sources = source_block.transpose(1, 0, 2)
    counts = edge_counts.transpose(1, 0, 2)
    wide = jax.ShapeDtypeStruct((rows, width), jnp.float32)
    narrow = jax.ShapeDtypeStruct((rows, width), kind)
    half = jax.ShapeDtypeStruct((cut, width), kind)

    low, high = call(
        split_kernel, [half, half], pltpu.with_memory_space_constraint(x, pltpu.HBM),
        specs=[pl.BlockSpec(memory_space=pltpu.HBM)],
        scratch=[pltpu.SemaphoreType.DMA((2,))],
        name="split",
    )
    xa = slab(low, pair)
    x_sib = sub(x)
    (fx,) = dense(("pair",), (), False, after(sources, low, x_sib), counts, tiles)
    xb = slab(high, pair)
    fz, fo, mine, send = dense(("across", "own"), (fx,), True, after(sources, fx), counts, tiles)
    xa = after(xa, fz)
    za = slab(xa, hop)
    xa_sib = sub(xa)
    theirs = sub(send)
    messages, own = call(local_kernel, [wide, wide], fo, x, x_sib, w_self, name="local")
    xb = after(xb, messages)
    zb = slab(xb, hop)
    xb_sib = sub(xb)
    messages = gather(messages, (0, rows, cut), (fx, fx, fx), (xa, xa_sib, xb))
    za, theirs = lax.optimization_barrier((za, theirs, messages))[:2]
    za_sib = sub(za)
    messages = gather(messages, (rows + cut, 0), (fx, fz), (xb_sib, za))
    zb = after(zb, messages)
    zb_sib = sub(zb)
    messages = gather(messages, (rows, cut), (fz, fz), (za_sib, zb))
    node_out, pre_grad, g = call(
        functools.partial(middle_kernel, rows + cut),
        [narrow, narrow, narrow],
        messages, own, fz, zb_sib, norm, w_neigh, cotangent,
        out_specs=[ANY, VMEM, VMEM],
        scratch=[pltpu.VMEM((rows, width), kind), pltpu.SemaphoreType.DMA],
        name="middle",
    )
    g_sib = sub(g)

    tx, tz, theirs_near = call(
        first_kernel, [wide, wide, jax.ShapeDtypeStruct((2 * rows, width), kind)],
        mine, g, theirs,
        specs=[VMEM, VMEM, pl.BlockSpec(memory_space=pltpu.HBM)],
        scratch=[pltpu.SemaphoreType.DMA],
        name="first",
    )
    steps = range(0, rows, block)
    part = jax.ShapeDtypeStruct((block, width), kind)
    px, *pz = call(
        second_kernel, [wide] + [part for _ in steps], theirs_near, g_sib, tx, tz, name="second"
    )
    relayed = [slab(v, back) for v in pz]
    own_grad = call(own_kernel, wide, mine, theirs, g, g_sib, after(pre_grad, px), w_self, name="own")
    summed = []
    for at, v in zip(steps, relayed):
        v = call(functools.partial(add_kernel, at), part, px, after(v, own_grad), name="add")
        summed.append(slab(v, pair))
    node_grad = call(
        last_kernel, narrow, own_grad, *summed,
        out_specs=ANY,
        scratch=[pltpu.VMEM((rows, width), kind), pltpu.SemaphoreType.DMA((len(steps),))],
        name="last",
    )
    return (node_out, node_grad)


def solution(mesh):
    whole = P(None, None)
    return jax.shard_map(
        per_device,
        mesh=mesh,
        in_specs=(
            P(ROWS, None),
            whole,
            whole,
            P(ROWS, None, None, None, None),
            P(ROWS, None, None),
            P(ROWS, None, None),
            P(ROWS),
            P(ROWS, None),
        ),
        out_specs=(P(ROWS, None), P(ROWS, None)),
        check_vma=False,
    )
```

time: 62 us -> 55.4 us (0.89)
  starting transfers between devices: 18.2 us -> 23.7 us
  local copies, waits for them, and re-layouts: 5.18 us -> 0.04 us
  waiting for transfers between devices: 21.4 us -> 16.4 us
  Pallas kernels: 15.3 us -> 14.2 us
  other arithmetic: 0.76 us -> 0 us
    ppermute x8 -> x12, waiting for transfers between devices: 20.2 us -> 13.1 us  [slab(): return lax.ppermute(v, 'slab', route)]
    ppermute x8 -> x12, starting transfers between devices: 16.8 us -> 22.4 us  [slab(): return lax.ppermute(v, 'slab', route)]
    unnamed x20 -> x14, local copies, waits for them, and re-layouts: 3.27 us -> 0.04 us
    ppermute x7, waiting for transfers between devices: 1.18 us -> 3.28 us  [sub(): return lax.ppermute(v, 'sub', swap)]
    slice x1 -> x0, local copies, waits for them, and re-layouts: 1.76 us -> none  [per_device(): high = x[cut:]]
    pallas_call x12 -> x16, Pallas kernels: 15.3 us -> 14.2 us  [call(): pl.pallas_call(kernel, in_specs=specs or [VMEM] * len(args), out_specs=ou...]
    convert_element_type x1 -> x0, other arithmetic: 0.68 us -> none  [per_device(): norm = normalizer.astype(jnp.float32)[:, None]]
  transfers between devices with their start and end apart: 15 -> 19, of which waited for: 7 -> 10; matrix products, arithmetic and copies ran while one was open for 4% -> 0% of each run, Pallas kernels for 19% -> 19%
where the time goes in v3:
time: 55.4 us; the launch traced here: 55.2 us
  starting transfers between devices  23.7 us (43%)
  waiting for transfers between devices  16.4 us (30%)
  Pallas kernels  14.2 us (26%)
  between operations  0.8 us (1%)
    ppermute x12, starting transfers between devices, slab(): return lax.ppermute(v, 'slab', route)  22.4 us
    pallas_call x16, Pallas kernels, call(): pl.pallas_call(kernel, in_specs=specs or [VMEM] * len(args), out_specs=ou...  14.2 us
    ppermute x12, waiting for transfers between devices, slab(): return lax.ppermute(v, 'slab', route)  13.1 us
    ppermute x7, waiting for transfers between devices, sub(): return lax.ppermute(v, 'sub', swap)  3.28 us
    ppermute x7, starting transfers between devices, sub(): return lax.ppermute(v, 'sub', swap)  1.36 us
  transfers between devices with their start and end apart: 19, of which 10 were waited for; matrix products, arithmetic and copies ran while one was open for 0% of the time, Pallas kernels for 19%

profile of v3, /device:TPU:0, one launch (start us, length us, event | category | flops | bytes accessed | tf_op | source)
XLA Modules:
  0.0 55.2 jit_solution(18362197920094935258)
XLA Ops:
  0.6 0.5 collective-permute-start
  1.1 1.0 %split.1 = (bf16[256,512]{1,0:T(8,128)(2,1)S(1)}, bf16[256,512]{1,0:T(8,128)(2,1)S(1)}) custom-call(bf16[512,512]{1,0:T(8,128)(2,1)} %x.3), custom_call_target="tpu_custom_call" | custom-call | flops 17179869184 | bytes 67108864 | tf_op jit(solution)/shard_map/split/pallas_call | solution.py:25
  2.2 2.6 %collective-permute-start.1 = (bf16[256,512]{1,0:T(8,128)(2,1)S(1)}, bf16[256,512]{1,0:T(8,128)(2,1)S(1)}, u32[]{:S(2)}, u32[]{:S(2)}) collective-permute-start(bf16[256,512]{1,0:T(8,128)(2,1)S(1)} %get-tuple-element.33), channel_id=1, source_target_pairs={{0,2},{2,0},{4,6},{6,4},{8,10},{10,8},{12,14},{14,12},{1,3},{3,1},... | collective-permute-start | bytes 786440 | tf_op jit(solution)/shard_map/ppermute | solution.py:264
  4.8 0.1 collective-permute-start.3
  4.8 0.0 collective-permute-done.x_sib
  4.9 1.5 %dense_pair.1.refs_0_.refs_1_.refs_2_ = bf16[512,1024]{1,0:T(8,128)(2,1)S(1)} custom-call(s32[3,4,6]{2,1,0:T(4,128)} %bitcast.4, s32[3,4,6]{2,1,0:T(4,128)} %bitcast.6, bf16[4,3,6,128,128]{4,3,2,1,0:T(8,128)(2,1)} %tiles.3), custom_call_target="tpu_custom_call" | custom-call | flops 67108864 | bytes 262144 | tf_op jit(solution)/shard_map/dense_pair/pallas_call | solution.py:25
  6.4 0.0 copy-start.1
  6.4 0.0 copy-start.4
  6.4 3.9 %dense_across.1 = (bf16[512,1024]{1,0:T(8,128)(2,1)S(1)}, bf16[512,1024]{1,0:T(8,128)(2,1)S(1)}, bf16[1536,512]{1,0:T(8,128)(2,1)}, bf16[1536,512]{1,0:T(8,128)(2,1)}) custom-call(s32[3,4,6]{2,1,0:T(4,128)} %bitcast.5, s32[3,4,6]{2,1,0:T(4,128)} %bitcast.7, bf16[4,3,6,128,128]{4,3,2,1,0:T(8,128)(2,1)} %tiles.3, ...), custom_call_target="tpu_custom_call" | custom-call | flops 134217728 | bytes 524288 | tf_op jit(solution)/shard_map/dense_across/pallas_call | solution.py:25
  10.3 1.6 %collective-permute-done.1.refs_3_ = bf16[256,512]{1,0:T(8,128)(2,1)S(1)} collective-permute-done((bf16[256,512]{1,0:T(8,128)(2,1)S(1)}, bf16[256,512]{1,0:T(8,128)(2,1)S(1)}, u32[]{:S(2)}, u32[]{:S(2)}) %collective-permute-start.1) | collective-permute-done | bytes 262176 | tf_op jit(solution)/shard_map/ppermute | solution.py:264
  11.9 2.0 %collective-permute-start.5 = (bf16[256,512]{1,0:T(8,128)(2,1)S(1)}, bf16[256,512]{1,0:T(8,128)(2,1)S(1)}, u32[]{:S(2)}, u32[]{:S(2)}) collective-permute-start(bf16[256,512]{1,0:T(8,128)(2,1)S(1)} %collective-permute-done.1.refs_3_), channel_id=1, source_target_pairs={{0,4},{2,14},{4,8},{6,2},{8,12},{10,6},{12,0},{14,10},{1,5},{3,15}... | collective-permute-start | bytes 786440 | tf_op jit(solution)/shard_map/ppermute | solution.py:264
  14.0 1.0 %local.1 = (f32[512,512]{1,0:T(8,128)S(1)}, f32[512,512]{1,0:T(8,128)S(1)}) custom-call(bf16[512,1024]{1,0:T(8,128)(2,1)S(1)} %get-tuple-element.36.adj, bf16[512,512]{1,0:T(8,128)(2,1)S(1)} %copy-done.1, bf16[512,512]{1,0:T(8,128)(2,1)S(1)} %collective-permute-done.x_sib, bf16[512,512]{1,0:T(8,128)(2,1)S(1)} %copy-done.4), custom_call_target="tpu_custom_call" | custom-call | flops 17179869184 | bytes 67108864 | tf_op jit(solution)/shard_map/local/pallas_call | solution.py:25
  15.0 2.4 %collective-permute-done.3.refs_5_ = bf16[256,512]{1,0:T(8,128)(2,1)S(1)} collective-permute-done((bf16[256,512]{1,0:T(8,128)(2,1)S(1)}, bf16[256,512]{1,0:T(8,128)(2,1)S(1)}, u32[]{:S(2)}, u32[]{:S(2)}) %collective-permute-start.3) | collective-permute-done | bytes 262176 | tf_op jit(solution)/shard_map/ppermute | solution.py:264
  17.4 1.8 %collective-permute-start.8 = (bf16[256,512]{1,0:T(8,128)(2,1)S(1)}, bf16[256,512]{1,0:T(8,128)(2,1)S(1)}, u32[]{:S(2)}, u32[]{:S(2)}) collective-permute-start(bf16[256,512]{1,0:T(8,128)(2,1)S(1)} %collective-permute-done.3.refs_5_), channel_id=1, source_target_pairs={{0,4},{2,14},{4,8},{6,2},{8,12},{10,6},{12,0},{14,10},{1,5},{3,15}... | collective-permute-start | bytes 786440 | tf_op jit(solution)/shard_map/ppermute | solution.py:264
  19.2 0.0 collective-permute-start.4
  19.2 0.5 collective-permute-start.6
  19.7 0.0 collective-permute-done.2.refs_4_
  19.7 0.6 %gather.3.messages = f32[512,512]{1,0:T(8,128)S(1)} custom-call(f32[512,512]{1,0:T(8,128)S(1)} %get-tuple-element.37.messages, bf16[512,1024]{1,0:T(8,128)(2,1)S(1)} %dense_pair.1.refs_0_.refs_1_.refs_2_, bf16[512,1024]{1,0:T(8,128)(2,1)S(1)} %dense_pair.1.refs_0_.refs_1_.refs_2_, bf16[512,1024]{1,0:T(8,128)(2,1)S(1)} %dense_pair.1.refs_0_.refs_1_.refs_2_, ...), custom_call_target="tpu_custom_call" | custom-call | flops 17179869184 | bytes 67108864 | tf_op jit(solution)/shard_map/gather/pallas_call | solution.py:25
  20.3 1.5 %collective-permute-done.5.refs_3_ = bf16[256,512]{1,0:T(8,128)(2,1)S(1)} collective-permute-done((bf16[256,512]{1,0:T(8,128)(2,1)S(1)}, bf16[256,512]{1,0:T(8,128)(2,1)S(1)}, u32[]{:S(2)}, u32[]{:S(2)}) %collective-permute-start.5) | collective-permute-done | bytes 262176 | tf_op jit(solution)/shard_map/ppermute | solution.py:264
  21.8 1.2 %collective-permute-done.6.theirs = bf16[1536,512]{1,0:T(8,128)(2,1)S(1)} collective-permute-done((bf16[1536,512]{1,0:T(8,128)(2,1)S(1)}, bf16[1536,512]{1,0:T(8,128)(2,1)S(1)}, u32[]{:S(2)}, u32[]{:S(2)}) %collective-permute-start.6) | collective-permute-done | bytes 1572896 | tf_op jit(solution)/shard_map/ppermute | solution.py:267
  23.0 0.1 collective-permute-start.7
  23.1 0.4 gather.4.messages
  23.5 0.0 copy-start.2
  23.6 0.0 copy-start.3
  23.6 0.0 copy-start.5
  23.6 3.8 %collective-permute-done.8.refs_3_ = bf16[256,512]{1,0:T(8,128)(2,1)S(1)} collective-permute-done((bf16[256,512]{1,0:T(8,128)(2,1)S(1)}, bf16[256,512]{1,0:T(8,128)(2,1)S(1)}, u32[]{:S(2)}, u32[]{:S(2)}) %collective-permute-start.8) | collective-permute-done | bytes 262176 | tf_op jit(solution)/shard_map/ppermute | solution.py:264
  27.4 0.4 gather.5.messages
  27.8 1.1 %collective-permute-done.9.last = bf16[256,512]{1,0:T(8,128)(2,1)S(1)} collective-permute-done((bf16[256,512]{1,0:T(8,128)(2,1)S(1)}, bf16[256,512]{1,0:T(8,128)(2,1)S(1)}, u32[]{:S(2)}, u32[]{:S(2)}) %collective-permute-start.9) | collective-permute-done | bytes 262176 | tf_op jit(solution)/shard_map/ppermute | solution.py:267
  28.9 1.8 %middle.1 = (bf16[512,512]{1,0:T(8,128)(2,1)}, bf16[512,512]{1,0:T(8,128)(2,1)S(1)}, bf16[512,512]{1,0:T(8,128)(2,1)S(1)}) custom-call(f32[512,512]{1,0:T(8,128)S(1)} %gather.5.messages, f32[512,512]{1,0:T(8,128)S(1)} %get-tuple-element.45.own, bf16[512,1024]{1,0:T(8,128)(2,1)S(1)} %get-tuple-element.38.refs_1_.refs_0_.adj, ...), custom_call_target="tpu_custom_call" | custom-call | flops 17179869184 | bytes 67108864 | tf_op jit(solution)/shard_map/middle/pallas_call | solution.py:25
  30.8 0.2 collective-permute-start.10
  31.0 0.8 %first.1 = (f32[512,512]{1,0:T(8,128)S(1)}, f32[512,512]{1,0:T(8,128)S(1)}, bf16[1024,512]{1,0:T(8,128)(2,1)S(1)}) custom-call(bf16[1536,512]{1,0:T(8,128)(2,1)S(1)} %copy-done, bf16[512,512]{1,0:T(8,128)(2,1)S(1)} %get-tuple-element.49.g, bf16[1536,512]{1,0:T(8,128)(2,1)S(1)} %collective-permute-done.6.theirs), custom_call_target="tpu_custom_call" | custom-call | flops 17179869184 | bytes 67108864 | tf_op jit(solution)/shard_map/first/pallas_call | solution.py:25
  31.8 1.0 %collective-permute-done.10.g_sib = bf16[512,512]{1,0:T(8,128)(2,1)S(1)} collective-permute-done((bf16[512,512]{1,0:T(8,128)(2,1)S(1)}, bf16[512,512]{1,0:T(8,128)(2,1)S(1)}, u32[]{:S(2)}, u32[]{:S(2)}) %collective-permute-start.10) | collective-permute-done | bytes 524320 | tf_op jit(solution)/shard_map/ppermute | solution.py:267
  32.8 0.7 %second.1 = (f32[512,512]{1,0:T(8,128)S(1)}, bf16[128,512]{1,0:T(8,128)(2,1)S(1)}, bf16[128,512]{1,0:T(8,128)(2,1)S(1)}, bf16[128,512]{1,0:T(8,128)(2,1)S(1)}, bf16[128,512]{1,0:T(8,128)(2,1)S(1)}) custom-call(bf16[1024,512]{1,0:T(8,128)(2,1)S(1)} %get-tuple-element.51.theirs, bf16[512,512]{1,0:T(8,128)(2,1)S(1)} %collective-permute-done.10.g_sib, ...), custom_call_target="tpu_custom_call" | custom-call | flops 17179869184 | bytes 67108864 | tf_op jit(solution)/shard_map/second/pallas_call | solution.py:25
  33.5 1.8 %collective-permute-start.11 = (bf16[128,512]{1,0:T(8,128)(2,1)S(1)}, bf16[128,512]{1,0:T(8,128)(2,1)S(1)}, u32[]{:S(2)}, u32[]{:S(2)}) collective-permute-start(bf16[128,512]{1,0:T(8,128)(2,1)S(1)} %get-tuple-element.56), channel_id=1, source_target_pairs={{4,0},{14,2},{8,4},{2,6},{12,8},{6,10},{0,12},{10,14},{5,1},{15,3}... | collective-permute-start | bytes 393224 | tf_op jit(solution)/shard_map/ppermute | solution.py:264
  35.3 0.5 collective-permute-start.13
  35.7 0.4 collective-permute-start.15
  36.2 2.3 %collective-permute-start.17 = (bf16[128,512]{1,0:T(8,128)(2,1)S(1)}, bf16[128,512]{1,0:T(8,128)(2,1)S(1)}, u32[]{:S(2)}, u32[]{:S(2)}) collective-permute-start(bf16[128,512]{1,0:T(8,128)(2,1)S(1)} %get-tuple-element.62), channel_id=1, source_target_pairs={{4,0},{14,2},{8,4},{2,6},{12,8},{6,10},{0,12},{10,14},{5,1},{15,3}... | collective-permute-start | bytes 393224 | tf_op jit(solution)/shard_map/ppermute | solution.py:264
  38.5 1.0 %own.1 = f32[512,512]{1,0:T(8,128)S(1)} custom-call(bf16[1536,512]{1,0:T(8,128)(2,1)S(1)} %copy-done, bf16[1536,512]{1,0:T(8,128)(2,1)S(1)} %collective-permute-done.6.theirs, bf16[512,512]{1,0:T(8,128)(2,1)S(1)} %get-tuple-element.49.g, bf16[512,512]{1,0:T(8,128)(2,1)S(1)} %collective-permute-done.10.g_sib, ...), custom_call_target="tpu_custom_call" | custom-call | flops 17179869184 | bytes 67108864 | tf_op jit(solution)/shard_map/own/pallas_call | solution.py:25
  39.5 0.4 collective-permute-done.11.b
  39.9 3.0 %collective-permute-start.12 = (bf16[128,512]{1,0:T(8,128)(2,1)S(1)}, bf16[128,512]{1,0:T(8,128)(2,1)S(1)}, u32[]{:S(2)}, u32[]{:S(2)}) collective-permute-start(bf16[128,512]{1,0:T(8,128)(2,1)S(1)} %add.4), channel_id=1, source_target_pairs={{0,2},{2,0},{4,6},{6,4},{8,10},{10,8},{12,14},{14,12},{1,3},{3,1},... | collective-permute-start | bytes 393224 | tf_op jit(solution)/shard_map/ppermute | solution.py:264
  43.0 2.8 %collective-permute-start.14 = (bf16[128,512]{1,0:T(8,128)(2,1)S(1)}, bf16[128,512]{1,0:T(8,128)(2,1)S(1)}, u32[]{:S(2)}, u32[]{:S(2)}) collective-permute-start(bf16[128,512]{1,0:T(8,128)(2,1)S(1)} %add.5), channel_id=1, source_target_pairs={{0,2},{2,0},{4,6},{6,4},{8,10},{10,8},{12,14},{14,12},{1,3},{3,1},... | collective-permute-start | bytes 393224 | tf_op jit(solution)/shard_map/ppermute | solution.py:264
  45.8 2.8 %collective-permute-start.16 = (bf16[128,512]{1,0:T(8,128)(2,1)S(1)}, bf16[128,512]{1,0:T(8,128)(2,1)S(1)}, u32[]{:S(2)}, u32[]{:S(2)}) collective-permute-start(bf16[128,512]{1,0:T(8,128)(2,1)S(1)} %add.6), channel_id=1, source_target_pairs={{0,2},{2,0},{4,6},{6,4},{8,10},{10,8},{12,14},{14,12},{1,3},{3,1},... | collective-permute-start | bytes 393224 | tf_op jit(solution)/shard_map/ppermute | solution.py:264
  48.6 0.0 collective-permute-done.17.b
  48.6 2.3 %collective-permute-start.18 = (bf16[128,512]{1,0:T(8,128)(2,1)S(1)}, bf16[128,512]{1,0:T(8,128)(2,1)S(1)}, u32[]{:S(2)}, u32[]{:S(2)}) collective-permute-start(bf16[128,512]{1,0:T(8,128)(2,1)S(1)} %add.7), channel_id=1, source_target_pairs={{0,2},{2,0},{4,6},{6,4},{8,10},{10,8},{12,14},{14,12},{1,3},{3,1},... | collective-permute-start | bytes 393224 | tf_op jit(solution)/shard_map/ppermute | solution.py:264
  50.9 0.0 collective-permute-done.14.refs_1_
  50.9 0.7 %collective-permute-done.16.refs_2_ = bf16[128,512]{1,0:T(8,128)(2,1)S(1)} collective-permute-done((bf16[128,512]{1,0:T(8,128)(2,1)S(1)}, bf16[128,512]{1,0:T(8,128)(2,1)S(1)}, u32[]{:S(2)}, u32[]{:S(2)}) %collective-permute-start.16) | collective-permute-done | bytes 131104 | tf_op jit(solution)/shard_map/ppermute | solution.py:264
  51.6 2.7 %collective-permute-done.18.refs_3_ = bf16[128,512]{1,0:T(8,128)(2,1)S(1)} collective-permute-done((bf16[128,512]{1,0:T(8,128)(2,1)S(1)}, bf16[128,512]{1,0:T(8,128)(2,1)S(1)}, u32[]{:S(2)}, u32[]{:S(2)}) %collective-permute-start.18) | collective-permute-done | bytes 131104 | tf_op jit(solution)/shard_map/ppermute | solution.py:264
  54.3 0.8 %last.1 = bf16[512,512]{1,0:T(8,128)(2,1)} custom-call(f32[512,512]{1,0:T(8,128)S(1)} %own.1, bf16[128,512]{1,0:T(8,128)(2,1)S(1)} %collective-permute-done.12.refs_0_, bf16[128,512]{1,0:T(8,128)(2,1)S(1)} %collective-permute-done.14.refs_1_, bf16[128,512]{1,0:T(8,128)(2,1)S(1)} %collective-permute-done.16.refs_2_, ...), custom_call_target="tpu_custom_call" | custom-call | flops 17179869184 | bytes 67108864 | tf_op jit(solution)/shard_map/last/pallas_call | solution.py:25
  (20 shorter events, 0.1 us)
Async XLA Ops:
  0.6 4.2 %collective-permute-start = (bf16[512,512]{1,0:T(8,128)(2,1)}, bf16[512,512]{1,0:T(8,128)(2,1)S(1)}, u32[]{:S(2)}, u32[]{:S(2)}) collective-permute-start(bf16[512,512]{1,0:T(8,128)(2,1)} %x.3), channel_id=1, source_target_pairs={{0,1},{1,0},{2,3},{3,2},{4,5},{5,4},{6,7},{7,6},{8,9},{9,8},{10,11... | collective-permute-start | bytes 1572872 | tf_op jit(solution)/shard_map/ppermute | solution.py:267
  2.2 9.7 %collective-permute-start.1 = (bf16[256,512]{1,0:T(8,128)(2,1)S(1)}, bf16[256,512]{1,0:T(8,128)(2,1)S(1)}, u32[]{:S(2)}, u32[]{:S(2)}) collective-permute-start(bf16[256,512]{1,0:T(8,128)(2,1)S(1)} %get-tuple-element.33), channel_id=1, source_target_pairs={{0,2},{2,0},{4,6},{6,4},{8,10},{10,8},{12,14},{14,12},{1,3},{3,1},... | collective-permute-start | bytes 786440 | tf_op jit(solution)/shard_map/ppermute | solution.py:264
  4.8 12.6 %collective-permute-start.3 = (bf16[256,512]{1,0:T(8,128)(2,1)S(1)}, bf16[256,512]{1,0:T(8,128)(2,1)S(1)}, u32[]{:S(2)}, u32[]{:S(2)}) collective-permute-start(bf16[256,512]{1,0:T(8,128)(2,1)S(1)} %get-tuple-element.40), channel_id=1, source_target_pairs={{0,2},{2,0},{4,6},{6,4},{8,10},{10,8},{12,14},{14,12},{1,3},{3,1},... | collective-permute-start | bytes 786440 | tf_op jit(solution)/shard_map/ppermute | solution.py:264
  6.4 7.6 %copy-start.1 = (bf16[512,512]{1,0:T(8,128)(2,1)S(1)}, bf16[512,512]{1,0:T(8,128)(2,1)}, u32[]{:S(2)}) copy-start(bf16[512,512]{1,0:T(8,128)(2,1)} %x.3) | copy-start | bytes 1572868
  6.4 7.6 %copy-start.4 = (bf16[512,512]{1,0:T(8,128)(2,1)S(1)}, bf16[512,512]{1,0:T(8,128)(2,1)}, u32[]{:S(2)}) copy-start(bf16[512,512]{1,0:T(8,128)(2,1)} %w_self.3) | copy-start | bytes 1572868
  11.9 9.8 %collective-permute-start.5 = (bf16[256,512]{1,0:T(8,128)(2,1)S(1)}, bf16[256,512]{1,0:T(8,128)(2,1)S(1)}, u32[]{:S(2)}, u32[]{:S(2)}) collective-permute-start(bf16[256,512]{1,0:T(8,128)(2,1)S(1)} %collective-permute-done.1.refs_3_), channel_id=1, source_target_pairs={{0,4},{2,14},{4,8},{6,2},{8,12},{10,6},{12,0},{14,10},{1,5},{3,15}... | collective-permute-start | bytes 786440 | tf_op jit(solution)/shard_map/ppermute | solution.py:264
  14.0 5.7 %collective-permute-start.2 = (bf16[256,512]{1,0:T(8,128)(2,1)S(1)}, bf16[256,512]{1,0:T(8,128)(2,1)S(1)}, u32[]{:S(2)}, u32[]{:S(2)}) collective-permute-start(bf16[256,512]{1,0:T(8,128)(2,1)S(1)} %collective-permute-done.1.refs_3_), channel_id=1, source_target_pairs={{0,1},{1,0},{2,3},{3,2},{4,5},{5,4},{6,7},{7,6},{8,9},{9,8},{10,11... | collective-permute-start | bytes 786440 | tf_op jit(solution)/shard_map/ppermute | solution.py:267
  14.0 5.2 %copy-start.6 = (bf16[1536,512]{1,0:T(8,128)(2,1)S(1)}, bf16[1536,512]{1,0:T(8,128)(2,1)}, u32[]{:S(2)}) copy-start(bf16[1536,512]{1,0:T(8,128)(2,1)} %get-tuple-element.42) | copy-start | bytes 4718596
  17.4 10.0 %collective-permute-start.8 = (bf16[256,512]{1,0:T(8,128)(2,1)S(1)}, bf16[256,512]{1,0:T(8,128)(2,1)S(1)}, u32[]{:S(2)}, u32[]{:S(2)}) collective-permute-start(bf16[256,512]{1,0:T(8,128)(2,1)S(1)} %collective-permute-done.3.refs_5_), channel_id=1, source_target_pairs={{0,4},{2,14},{4,8},{6,2},{8,12},{10,6},{12,0},{14,10},{1,5},{3,15}... | collective-permute-start | bytes 786440 | tf_op jit(solution)/shard_map/ppermute | solution.py:264
  19.2 3.9 %collective-permute-start.4 = (bf16[256,512]{1,0:T(8,128)(2,1)S(1)}, bf16[256,512]{1,0:T(8,128)(2,1)S(1)}, u32[]{:S(2)}, u32[]{:S(2)}) collective-permute-start(bf16[256,512]{1,0:T(8,128)(2,1)S(1)} %collective-permute-done.3.refs_5_), channel_id=1, source_target_pairs={{0,1},{1,0},{2,3},{3,2},{4,5},{5,4},{6,7},{7,6},{8,9},{9,8},{10,11... | collective-permute-start | bytes 786440 | tf_op jit(solution)/shard_map/ppermute | solution.py:267
  19.2 3.8 %collective-permute-start.6 = (bf16[1536,512]{1,0:T(8,128)(2,1)S(1)}, bf16[1536,512]{1,0:T(8,128)(2,1)S(1)}, u32[]{:S(2)}, u32[]{:S(2)}) collective-permute-start(bf16[1536,512]{1,0:T(8,128)(2,1)S(1)} %copy-done.6), channel_id=1, source_target_pairs={{0,1},{1,0},{2,3},{3,2},{4,5},{5,4},{6,7},{7,6},{8,9},{9,8},{10,11... | collective-permute-start | bytes 4718600 | tf_op jit(solution)/shard_map/ppermute | solution.py:267
  23.0 4.4 %collective-permute-start.7 = (bf16[256,512]{1,0:T(8,128)(2,1)S(1)}, bf16[256,512]{1,0:T(8,128)(2,1)S(1)}, u32[]{:S(2)}, u32[]{:S(2)}) collective-permute-start(bf16[256,512]{1,0:T(8,128)(2,1)S(1)} %collective-permute-done.5.refs_3_), channel_id=1, source_target_pairs={{0,1},{1,0},{2,3},{3,2},{4,5},{5,4},{6,7},{7,6},{8,9},{9,8},{10,11... | collective-permute-start | bytes 786440 | tf_op jit(solution)/shard_map/ppermute | solution.py:267
  23.5 5.4 %copy-start.2 = (bf16[512,512]{1,0:T(8,128)(2,1)S(1)}, bf16[512,512]{1,0:T(8,128)(2,1)}, u32[]{:S(2)}) copy-start(bf16[512,512]{1,0:T(8,128)(2,1)} %w_neigh.1) | copy-start | bytes 1572868
  23.6 5.4 %copy-start.3 = (bf16[512,512]{1,0:T(8,128)(2,1)S(1)}, bf16[512,512]{1,0:T(8,128)(2,1)}, u32[]{:S(2)}) copy-start(bf16[512,512]{1,0:T(8,128)(2,1)} %cotangent.1) | copy-start | bytes 1572868
  23.6 5.4 %copy-start.5 = (s32[512]{0:T(512)S(1)}, s32[512]{0:T(512)}, u32[]{:S(2)}) copy-start(s32[512]{0:T(512)} %param.14) | copy-start | bytes 6148
  27.4 1.5 %collective-permute-start.9 = (bf16[256,512]{1,0:T(8,128)(2,1)S(1)}, bf16[256,512]{1,0:T(8,128)(2,1)S(1)}, u32[]{:S(2)}, u32[]{:S(2)}) collective-permute-start(bf16[256,512]{1,0:T(8,128)(2,1)S(1)} %collective-permute-done.8.refs_3_), channel_id=1, source_target_pairs={{0,1},{1,0},{2,3},{3,2},{4,5},{5,4},{6,7},{7,6},{8,9},{9,8},{10,11... | collective-permute-start | bytes 786440 | tf_op jit(solution)/shard_map/ppermute | solution.py:267
  28.9 2.1 %copy-start = (bf16[1536,512]{1,0:T(8,128)(2,1)S(1)}, bf16[1536,512]{1,0:T(8,128)(2,1)}, u32[]{:S(2)}) copy-start(bf16[1536,512]{1,0:T(8,128)(2,1)} %get-tuple-element.47.mine) | copy-start | bytes 4718596
  30.8 2.0 %collective-permute-start.10 = (bf16[512,512]{1,0:T(8,128)(2,1)S(1)}, bf16[512,512]{1,0:T(8,128)(2,1)S(1)}, u32[]{:S(2)}, u32[]{:S(2)}) collective-permute-start(bf16[512,512]{1,0:T(8,128)(2,1)S(1)} %get-tuple-element.49.g), channel_id=1, source_target_pairs={{0,1},{1,0},{2,3},{3,2},{4,5},{5,4},{6,7},{7,6},{8,9},{9,8},{10,11... | collective-permute-start | bytes 1572872 | tf_op jit(solution)/shard_map/ppermute | solution.py:267
  33.5 6.4 %collective-permute-start.11 = (bf16[128,512]{1,0:T(8,128)(2,1)S(1)}, bf16[128,512]{1,0:T(8,128)(2,1)S(1)}, u32[]{:S(2)}, u32[]{:S(2)}) collective-permute-start(bf16[128,512]{1,0:T(8,128)(2,1)S(1)} %get-tuple-element.56), channel_id=1, source_target_pairs={{4,0},{14,2},{8,4},{2,6},{12,8},{6,10},{0,12},{10,14},{5,1},{15,3}... | collective-permute-start | bytes 393224 | tf_op jit(solution)/shard_map/ppermute | solution.py:264
  35.3 7.7 %collective-permute-start.13 = (bf16[128,512]{1,0:T(8,128)(2,1)S(1)}, bf16[128,512]{1,0:T(8,128)(2,1)S(1)}, u32[]{:S(2)}, u32[]{:S(2)}) collective-permute-start(bf16[128,512]{1,0:T(8,128)(2,1)S(1)} %get-tuple-element.58), channel_id=1, source_target_pairs={{4,0},{14,2},{8,4},{2,6},{12,8},{6,10},{0,12},{10,14},{5,1},{15,3}... | collective-permute-start | bytes 393224 | tf_op jit(solution)/shard_map/ppermute | solution.py:264
  35.7 10.0 %collective-permute-start.15 = (bf16[128,512]{1,0:T(8,128)(2,1)S(1)}, bf16[128,512]{1,0:T(8,128)(2,1)S(1)}, u32[]{:S(2)}, u32[]{:S(2)}) collective-permute-start(bf16[128,512]{1,0:T(8,128)(2,1)S(1)} %get-tuple-element.60), channel_id=1, source_target_pairs={{4,0},{14,2},{8,4},{2,6},{12,8},{6,10},{0,12},{10,14},{5,1},{15,3}... | collective-permute-start | bytes 393224 | tf_op jit(solution)/shard_map/ppermute | solution.py:264
  36.2 12.4 %collective-permute-start.17 = (bf16[128,512]{1,0:T(8,128)(2,1)S(1)}, bf16[128,512]{1,0:T(8,128)(2,1)S(1)}, u32[]{:S(2)}, u32[]{:S(2)}) collective-permute-start(bf16[128,512]{1,0:T(8,128)(2,1)S(1)} %get-tuple-element.62), channel_id=1, source_target_pairs={{4,0},{14,2},{8,4},{2,6},{12,8},{6,10},{0,12},{10,14},{5,1},{15,3}... | collective-permute-start | bytes 393224 | tf_op jit(solution)/shard_map/ppermute | solution.py:264
  39.9 11.0 %collective-permute-start.12 = (bf16[128,512]{1,0:T(8,128)(2,1)S(1)}, bf16[128,512]{1,0:T(8,128)(2,1)S(1)}, u32[]{:S(2)}, u32[]{:S(2)}) collective-permute-start(bf16[128,512]{1,0:T(8,128)(2,1)S(1)} %add.4), channel_id=1, source_target_pairs={{0,2},{2,0},{4,6},{6,4},{8,10},{10,8},{12,14},{14,12},{1,3},{3,1},... | collective-permute-start | bytes 393224 | tf_op jit(solution)/shard_map/ppermute | solution.py:264
  43.0 7.9 %collective-permute-start.14 = (bf16[128,512]{1,0:T(8,128)(2,1)S(1)}, bf16[128,512]{1,0:T(8,128)(2,1)S(1)}, u32[]{:S(2)}, u32[]{:S(2)}) collective-permute-start(bf16[128,512]{1,0:T(8,128)(2,1)S(1)} %add.5), channel_id=1, source_target_pairs={{0,2},{2,0},{4,6},{6,4},{8,10},{10,8},{12,14},{14,12},{1,3},{3,1},... | collective-permute-start | bytes 393224 | tf_op jit(solution)/shard_map/ppermute | solution.py:264
  45.8 5.8 %collective-permute-start.16 = (bf16[128,512]{1,0:T(8,128)(2,1)S(1)}, bf16[128,512]{1,0:T(8,128)(2,1)S(1)}, u32[]{:S(2)}, u32[]{:S(2)}) collective-permute-start(bf16[128,512]{1,0:T(8,128)(2,1)S(1)} %add.6), channel_id=1, source_target_pairs={{0,2},{2,0},{4,6},{6,4},{8,10},{10,8},{12,14},{14,12},{1,3},{3,1},... | collective-permute-start | bytes 393224 | tf_op jit(solution)/shard_map/ppermute | solution.py:264
  48.6 5.7 %collective-permute-start.18 = (bf16[128,512]{1,0:T(8,128)(2,1)S(1)}, bf16[128,512]{1,0:T(8,128)(2,1)S(1)}, u32[]{:S(2)}, u32[]{:S(2)}) collective-permute-start(bf16[128,512]{1,0:T(8,128)(2,1)S(1)} %add.7), channel_id=1, source_target_pairs={{0,2},{2,0},{4,6},{6,4},{8,10},{10,8},{12,14},{14,12},{1,3},{3,1},... | collective-permute-start | bytes 393224 | tf_op jit(solution)/shard_map/ppermute | solution.py:264

commit v4 on v3

--- a/solution.py
+++ b/solution.py
@@ -212,12 +212,13 @@
     fetch.wait()
 
 
-def second_kernel(theirs, g_sib, tx, tz, px, *pz):
-    rows, step = tz.shape[0], pz[0].shape[0]
-    z = (tz[...] + dot(theirs[rows:2 * rows, :], g_sib[...])).astype(pz[0].dtype)
-    for n, part in enumerate(pz):
-        part[...] = z[n * step:(n + 1) * step]
-    px[...] = tx[...] + dot(theirs[:rows, :], g_sib[...])
+def across_kernel(theirs, g_sib, tz, *pz):
+    rows = tz.shape[0]
+    z = (tz[...] + dot(theirs[rows:, :], g_sib[...])).astype(pz[0].dtype)
+    at = 0
+    for part in pz:
+        part[...] = z[at:at + part.shape[0]]
+        at += part.shape[0]
 
 
 def add_kernel(start, px, b, out):
@@ -225,8 +226,9 @@
     out[...] = (part + b[...].astype(jnp.float32)).astype(out.dtype)
 
 
-def own_kernel(mine, theirs, g, g_sib, pre_grad, w_self, out):
+def own_kernel(mine, theirs, near, g, g_sib, tx, pre_grad, w_self, px, out):
     rows = out.shape[0]
+    px[...] = tx[...] + dot(near[:rows, :], g_sib[...])
     out[...] = (
         dot_t(pre_grad[...], w_self[...])
         + dot(mine[2 * rows:, :], g[...])
@@ -236,14 +238,14 @@
 
 def last_kernel(own, *refs):
     parts, (out, buffer, sem) = refs[:-3], refs[-3:]
-    step = parts[0].shape[0]
-    stores = []
+    stores, start = [], 0
     for n, part in enumerate(parts):
-        at = pl.ds(n * step, step)
+        at = pl.ds(start, part.shape[0])
         buffer[at, :] = (own[at, :] + part[...].astype(jnp.float32)).astype(out.dtype)
         store = pltpu.make_async_copy(buffer.at[at], out.at[at], sem.at[n])
         store.start()
         stores.append(store)
+        start += part.shape[0]
     for store in stores:
         store.wait()
 
@@ -321,21 +323,23 @@
         scratch=[pltpu.SemaphoreType.DMA],
         name="first",
     )
-    steps = range(0, rows, block)
-    part = jax.ShapeDtypeStruct((block, width), kind)
-    px, *pz = call(
-        second_kernel, [wide] + [part for _ in steps], theirs_near, g_sib, tx, tz, name="second"
-    )
+    sizes = [block] * (rows // block)
+    parts = [jax.ShapeDtypeStruct((n, width), kind) for n in sizes]
+    pz = call(across_kernel, parts, theirs_near, g_sib, tz, name="across")
     relayed = [slab(v, back) for v in pz]
-    own_grad = call(own_kernel, wide, mine, theirs, g, g_sib, after(pre_grad, px), w_self, name="own")
-    summed = []
-    for at, v in zip(steps, relayed):
+    px, own_grad = call(
+        own_kernel, [wide, wide],
+        mine, theirs, theirs_near, g, g_sib, tx, after(pre_grad, *pz), w_self, name="own",
+    )
+    summed, at = [], 0
+    for part, v in zip(parts, relayed):
         v = call(functools.partial(add_kernel, at), part, px, after(v, own_grad), name="add")
         summed.append(slab(v, pair))
+        at += part.shape[0]
     node_grad = call(
         last_kernel, narrow, own_grad, *summed,
         out_specs=ANY,
-        scratch=[pltpu.VMEM((rows, width), kind), pltpu.SemaphoreType.DMA((len(steps),))],
+        scratch=[pltpu.VMEM((rows, width), kind), pltpu.SemaphoreType.DMA((len(parts),))],
         name="last",
     )
     return (node_out, node_grad)

time: 55.4 us -> 55.1 us (level)
  transfers between devices with their start and end apart: 19 -> 19, of which waited for: 10 -> 10; matrix products, arithmetic and copies ran while one was open for 0% -> 0% of each run, Pallas kernels for 19% -> 20%
where the time goes in v4:
time: 55.1 us; the launch traced here: 54.9 us
  starting transfers between devices  23.8 us (43%)
  waiting for transfers between devices  16.1 us (29%)
  Pallas kernels  14.2 us (26%)
  between operations  0.8 us (1%)
    ppermute x12, starting transfers between devices, slab(): return lax.ppermute(v, 'slab', route)  22.4 us
    pallas_call x16, Pallas kernels, call(): pl.pallas_call(kernel, in_specs=specs or [VMEM] * len(args), out_specs=ou...  14.2 us
    ppermute x12, waiting for transfers between devices, slab(): return lax.ppermute(v, 'slab', route)  12.9 us
    ppermute x7, waiting for transfers between devices, sub(): return lax.ppermute(v, 'sub', swap)  3.27 us
    ppermute x7, starting transfers between devices, sub(): return lax.ppermute(v, 'sub', swap)  1.37 us
  transfers between devices with their start and end apart: 19, of which 10 were waited for; matrix products, arithmetic and copies ran while one was open for 0% of the time, Pallas kernels for 20%

profile of v4, /device:TPU:0, one launch (start us, length us, event | category | flops | bytes accessed | tf_op | source)
XLA Modules:
  0.0 54.9 jit_solution(1373744490208019692)
XLA Ops:
  0.6 0.5 collective-permute-start
  1.1 1.0 %split.1 = (bf16[256,512]{1,0:T(8,128)(2,1)S(1)}, bf16[256,512]{1,0:T(8,128)(2,1)S(1)}) custom-call(bf16[512,512]{1,0:T(8,128)(2,1)} %x.3), custom_call_target="tpu_custom_call" | custom-call | flops 17179869184 | bytes 67108864 | tf_op jit(solution)/shard_map/split/pallas_call | solution.py:25
  2.2 2.6 %collective-permute-start.1 = (bf16[256,512]{1,0:T(8,128)(2,1)S(1)}, bf16[256,512]{1,0:T(8,128)(2,1)S(1)}, u32[]{:S(2)}, u32[]{:S(2)}) collective-permute-start(bf16[256,512]{1,0:T(8,128)(2,1)S(1)} %get-tuple-element.34), channel_id=1, source_target_pairs={{0,2},{2,0},{4,6},{6,4},{8,10},{10,8},{12,14},{14,12},{1,3},{3,1},... | collective-permute-start | bytes 786440 | tf_op jit(solution)/shard_map/ppermute | solution.py:266
  4.8 0.1 collective-permute-start.3
  4.8 0.0 collective-permute-done.x_sib
  4.9 1.5 %dense_pair.1.refs_0_.refs_1_.refs_2_ = bf16[512,1024]{1,0:T(8,128)(2,1)S(1)} custom-call(s32[3,4,6]{2,1,0:T(4,128)} %bitcast.4, s32[3,4,6]{2,1,0:T(4,128)} %bitcast.6, bf16[4,3,6,128,128]{4,3,2,1,0:T(8,128)(2,1)} %tiles.3), custom_call_target="tpu_custom_call" | custom-call | flops 67108864 | bytes 262144 | tf_op jit(solution)/shard_map/dense_pair/pallas_call | solution.py:25
  6.4 0.0 copy-start.1
  6.4 0.0 copy-start.4
  6.4 3.9 %dense_across.1 = (bf16[512,1024]{1,0:T(8,128)(2,1)S(1)}, bf16[512,1024]{1,0:T(8,128)(2,1)S(1)}, bf16[1536,512]{1,0:T(8,128)(2,1)}, bf16[1536,512]{1,0:T(8,128)(2,1)}) custom-call(s32[3,4,6]{2,1,0:T(4,128)} %bitcast.5, s32[3,4,6]{2,1,0:T(4,128)} %bitcast.7, bf16[4,3,6,128,128]{4,3,2,1,0:T(8,128)(2,1)} %tiles.3, ...), custom_call_target="tpu_custom_call" | custom-call | flops 134217728 | bytes 524288 | tf_op jit(solution)/shard_map/dense_across/pallas_call | solution.py:25
  10.3 1.6 %collective-permute-done.1.refs_3_ = bf16[256,512]{1,0:T(8,128)(2,1)S(1)} collective-permute-done((bf16[256,512]{1,0:T(8,128)(2,1)S(1)}, bf16[256,512]{1,0:T(8,128)(2,1)S(1)}, u32[]{:S(2)}, u32[]{:S(2)}) %collective-permute-start.1) | collective-permute-done | bytes 262176 | tf_op jit(solution)/shard_map/ppermute | solution.py:266
  11.9 2.0 %collective-permute-start.5 = (bf16[256,512]{1,0:T(8,128)(2,1)S(1)}, bf16[256,512]{1,0:T(8,128)(2,1)S(1)}, u32[]{:S(2)}, u32[]{:S(2)}) collective-permute-start(bf16[256,512]{1,0:T(8,128)(2,1)S(1)} %collective-permute-done.1.refs_3_), channel_id=1, source_target_pairs={{0,4},{2,14},{4,8},{6,2},{8,12},{10,6},{12,0},{14,10},{1,5},{3,15}... | collective-permute-start | bytes 786440 | tf_op jit(solution)/shard_map/ppermute | solution.py:266
  14.0 0.0 collective-permute-start.2
  14.0 1.0 %local.1 = (f32[512,512]{1,0:T(8,128)S(1)}, f32[512,512]{1,0:T(8,128)S(1)}) custom-call(bf16[512,1024]{1,0:T(8,128)(2,1)S(1)} %get-tuple-element.37.adj, bf16[512,512]{1,0:T(8,128)(2,1)S(1)} %copy-done.1, bf16[512,512]{1,0:T(8,128)(2,1)S(1)} %collective-permute-done.x_sib, bf16[512,512]{1,0:T(8,128)(2,1)S(1)} %copy-done.4), custom_call_target="tpu_custom_call" | custom-call | flops 17179869184 | bytes 67108864 | tf_op jit(solution)/shard_map/local/pallas_call | solution.py:25
  15.0 2.4 %collective-permute-done.3.refs_5_ = bf16[256,512]{1,0:T(8,128)(2,1)S(1)} collective-permute-done((bf16[256,512]{1,0:T(8,128)(2,1)S(1)}, bf16[256,512]{1,0:T(8,128)(2,1)S(1)}, u32[]{:S(2)}, u32[]{:S(2)}) %collective-permute-start.3) | collective-permute-done | bytes 262176 | tf_op jit(solution)/shard_map/ppermute | solution.py:266
  17.4 1.8 %collective-permute-start.8 = (bf16[256,512]{1,0:T(8,128)(2,1)S(1)}, bf16[256,512]{1,0:T(8,128)(2,1)S(1)}, u32[]{:S(2)}, u32[]{:S(2)}) collective-permute-start(bf16[256,512]{1,0:T(8,128)(2,1)S(1)} %collective-permute-done.3.refs_5_), channel_id=1, source_target_pairs={{0,4},{2,14},{4,8},{6,2},{8,12},{10,6},{12,0},{14,10},{1,5},{3,15}... | collective-permute-start | bytes 786440 | tf_op jit(solution)/shard_map/ppermute | solution.py:266
  19.2 0.5 collective-permute-start.6
  19.7 0.6 %gather.3.messages = f32[512,512]{1,0:T(8,128)S(1)} custom-call(f32[512,512]{1,0:T(8,128)S(1)} %get-tuple-element.38.messages, bf16[512,1024]{1,0:T(8,128)(2,1)S(1)} %dense_pair.1.refs_0_.refs_1_.refs_2_, bf16[512,1024]{1,0:T(8,128)(2,1)S(1)} %dense_pair.1.refs_0_.refs_1_.refs_2_, bf16[512,1024]{1,0:T(8,128)(2,1)S(1)} %dense_pair.1.refs_0_.refs_1_.refs_2_, ...), custom_call_target="tpu_custom_call" | custom-call | flops 17179869184 | bytes 67108864 | tf_op jit(solution)/shard_map/gather/pallas_call | solution.py:25
  20.3 1.5 %collective-permute-done.5.refs_3_ = bf16[256,512]{1,0:T(8,128)(2,1)S(1)} collective-permute-done((bf16[256,512]{1,0:T(8,128)(2,1)S(1)}, bf16[256,512]{1,0:T(8,128)(2,1)S(1)}, u32[]{:S(2)}, u32[]{:S(2)}) %collective-permute-start.5) | collective-permute-done | bytes 262176 | tf_op jit(solution)/shard_map/ppermute | solution.py:266
  21.8 1.2 %collective-permute-done.6.theirs = bf16[1536,512]{1,0:T(8,128)(2,1)S(1)} collective-permute-done((bf16[1536,512]{1,0:T(8,128)(2,1)S(1)}, bf16[1536,512]{1,0:T(8,128)(2,1)S(1)}, u32[]{:S(2)}, u32[]{:S(2)}) %collective-permute-start.6) | collective-permute-done | bytes 1572896 | tf_op jit(solution)/shard_map/ppermute | solution.py:269
  23.0 0.1 collective-permute-start.7
  23.1 0.0 collective-permute-done.4.refs_2_
  23.1 0.4 gather.4.messages
  23.5 0.0 copy-start.2
  23.6 0.0 copy-start.3
  23.6 0.0 copy-start.5
  23.6 3.8 %collective-permute-done.8.refs_3_ = bf16[256,512]{1,0:T(8,128)(2,1)S(1)} collective-permute-done((bf16[256,512]{1,0:T(8,128)(2,1)S(1)}, bf16[256,512]{1,0:T(8,128)(2,1)S(1)}, u32[]{:S(2)}, u32[]{:S(2)}) %collective-permute-start.8) | collective-permute-done | bytes 262176 | tf_op jit(solution)/shard_map/ppermute | solution.py:266
  27.4 0.0 collective-permute-done.7.refs_2_
  27.4 0.4 gather.5.messages
  27.8 1.1 %collective-permute-done.9.last = bf16[256,512]{1,0:T(8,128)(2,1)S(1)} collective-permute-done((bf16[256,512]{1,0:T(8,128)(2,1)S(1)}, bf16[256,512]{1,0:T(8,128)(2,1)S(1)}, u32[]{:S(2)}, u32[]{:S(2)}) %collective-permute-start.9) | collective-permute-done | bytes 262176 | tf_op jit(solution)/shard_map/ppermute | solution.py:269
  28.9 1.8 %middle.1 = (bf16[512,512]{1,0:T(8,128)(2,1)}, bf16[512,512]{1,0:T(8,128)(2,1)S(1)}, bf16[512,512]{1,0:T(8,128)(2,1)S(1)}) custom-call(f32[512,512]{1,0:T(8,128)S(1)} %gather.5.messages, f32[512,512]{1,0:T(8,128)S(1)} %get-tuple-element.46.own, bf16[512,1024]{1,0:T(8,128)(2,1)S(1)} %get-tuple-element.39.refs_1_.refs_0_.adj, ...), custom_call_target="tpu_custom_call" | custom-call | flops 17179869184 | bytes 67108864 | tf_op jit(solution)/shard_map/middle/pallas_call | solution.py:25
  30.8 0.2 collective-permute-start.10
  31.0 0.8 %first.1 = (f32[512,512]{1,0:T(8,128)S(1)}, f32[512,512]{1,0:T(8,128)S(1)}, bf16[1024,512]{1,0:T(8,128)(2,1)S(1)}) custom-call(bf16[1536,512]{1,0:T(8,128)(2,1)S(1)} %copy-done, bf16[512,512]{1,0:T(8,128)(2,1)S(1)} %get-tuple-element.50.g, bf16[1536,512]{1,0:T(8,128)(2,1)S(1)} %collective-permute-done.6.theirs), custom_call_target="tpu_custom_call" | custom-call | flops 17179869184 | bytes 67108864 | tf_op jit(solution)/shard_map/first/pallas_call | solution.py:25
  31.8 1.0 %collective-permute-done.10.g_sib = bf16[512,512]{1,0:T(8,128)(2,1)S(1)} collective-permute-done((bf16[512,512]{1,0:T(8,128)(2,1)S(1)}, bf16[512,512]{1,0:T(8,128)(2,1)S(1)}, u32[]{:S(2)}, u32[]{:S(2)}) %collective-permute-start.10) | collective-permute-done | bytes 524320 | tf_op jit(solution)/shard_map/ppermute | solution.py:269
  32.8 0.4 across.1
  33.2 1.8 %collective-permute-start.11 = (bf16[128,512]{1,0:T(8,128)(2,1)S(1)}, bf16[128,512]{1,0:T(8,128)(2,1)S(1)}, u32[]{:S(2)}, u32[]{:S(2)}) collective-permute-start(bf16[128,512]{1,0:T(8,128)(2,1)S(1)} %get-tuple-element.55), channel_id=1, source_target_pairs={{4,0},{14,2},{8,4},{2,6},{12,8},{6,10},{0,12},{10,14},{5,1},{15,3}... | collective-permute-start | bytes 393224 | tf_op jit(solution)/shard_map/ppermute | solution.py:266
  35.0 0.4 collective-permute-start.13
  35.4 0.5 collective-permute-start.15
  35.9 2.3 %collective-permute-start.17 = (bf16[128,512]{1,0:T(8,128)(2,1)S(1)}, bf16[128,512]{1,0:T(8,128)(2,1)S(1)}, u32[]{:S(2)}, u32[]{:S(2)}) collective-permute-start(bf16[128,512]{1,0:T(8,128)(2,1)S(1)} %get-tuple-element.58), channel_id=1, source_target_pairs={{4,0},{14,2},{8,4},{2,6},{12,8},{6,10},{0,12},{10,14},{5,1},{15,3}... | collective-permute-start | bytes 393224 | tf_op jit(solution)/shard_map/ppermute | solution.py:266
  38.2 1.2 %own.1 = (f32[512,512]{1,0:T(8,128)S(1)}, f32[512,512]{1,0:T(8,128)S(1)}) custom-call(bf16[1536,512]{1,0:T(8,128)(2,1)S(1)} %copy-done, bf16[1536,512]{1,0:T(8,128)(2,1)S(1)} %collective-permute-done.6.theirs, bf16[1024,512]{1,0:T(8,128)(2,1)S(1)} %get-tuple-element.51.theirs.near, bf16[512,512]{1,0:T(8,128)(2,1)S(1)} %get-tuple-element.50.g, ...), custom_call_target="tpu_custom_call" | custom-call | flops 17179869184 | bytes 67108864 | tf_op jit(solution)/shard_map/own/pallas_call | solution.py:25
  39.5 0.1 collective-permute-done.11.b
  39.6 3.0 %collective-permute-start.12 = (bf16[128,512]{1,0:T(8,128)(2,1)S(1)}, bf16[128,512]{1,0:T(8,128)(2,1)S(1)}, u32[]{:S(2)}, u32[]{:S(2)}) collective-permute-start(bf16[128,512]{1,0:T(8,128)(2,1)S(1)} %add.4), channel_id=1, source_target_pairs={{0,2},{2,0},{4,6},{6,4},{8,10},{10,8},{12,14},{14,12},{1,3},{3,1},... | collective-permute-start | bytes 393224 | tf_op jit(solution)/shard_map/ppermute | solution.py:266
  42.7 0.0 collective-permute-done.13.b
  42.7 2.8 %collective-permute-start.14 = (bf16[128,512]{1,0:T(8,128)(2,1)S(1)}, bf16[128,512]{1,0:T(8,128)(2,1)S(1)}, u32[]{:S(2)}, u32[]{:S(2)}) collective-permute-start(bf16[128,512]{1,0:T(8,128)(2,1)S(1)} %add.5), channel_id=1, source_target_pairs={{0,2},{2,0},{4,6},{6,4},{8,10},{10,8},{12,14},{14,12},{1,3},{3,1},... | collective-permute-start | bytes 393224 | tf_op jit(solution)/shard_map/ppermute | solution.py:266
  45.5 2.8 %collective-permute-start.16 = (bf16[128,512]{1,0:T(8,128)(2,1)S(1)}, bf16[128,512]{1,0:T(8,128)(2,1)S(1)}, u32[]{:S(2)}, u32[]{:S(2)}) collective-permute-start(bf16[128,512]{1,0:T(8,128)(2,1)S(1)} %add.6), channel_id=1, source_target_pairs={{0,2},{2,0},{4,6},{6,4},{8,10},{10,8},{12,14},{14,12},{1,3},{3,1},... | collective-permute-start | bytes 393224 | tf_op jit(solution)/shard_map/ppermute | solution.py:266
  48.3 2.3 %collective-permute-start.18 = (bf16[128,512]{1,0:T(8,128)(2,1)S(1)}, bf16[128,512]{1,0:T(8,128)(2,1)S(1)}, u32[]{:S(2)}, u32[]{:S(2)}) collective-permute-start(bf16[128,512]{1,0:T(8,128)(2,1)S(1)} %add.7), channel_id=1, source_target_pairs={{0,2},{2,0},{4,6},{6,4},{8,10},{10,8},{12,14},{14,12},{1,3},{3,1},... | collective-permute-start | bytes 393224 | tf_op jit(solution)/shard_map/ppermute | solution.py:266
  50.6 0.7 %collective-permute-done.16.refs_2_ = bf16[128,512]{1,0:T(8,128)(2,1)S(1)} collective-permute-done((bf16[128,512]{1,0:T(8,128)(2,1)S(1)}, bf16[128,512]{1,0:T(8,128)(2,1)S(1)}, u32[]{:S(2)}, u32[]{:S(2)}) %collective-permute-start.16) | collective-permute-done | bytes 131104 | tf_op jit(solution)/shard_map/ppermute | solution.py:266
  51.3 2.7 %collective-permute-done.18.refs_3_ = bf16[128,512]{1,0:T(8,128)(2,1)S(1)} collective-permute-done((bf16[128,512]{1,0:T(8,128)(2,1)S(1)}, bf16[128,512]{1,0:T(8,128)(2,1)S(1)}, u32[]{:S(2)}, u32[]{:S(2)}) %collective-permute-start.18) | collective-permute-done | bytes 131104 | tf_op jit(solution)/shard_map/ppermute | solution.py:266
  54.0 0.8 %last.1 = bf16[512,512]{1,0:T(8,128)(2,1)} custom-call(f32[512,512]{1,0:T(8,128)S(1)} %get-tuple-element.60.own, bf16[128,512]{1,0:T(8,128)(2,1)S(1)} %collective-permute-done.12.refs_0_, bf16[128,512]{1,0:T(8,128)(2,1)S(1)} %collective-permute-done.14.refs_1_, bf16[128,512]{1,0:T(8,128)(2,1)S(1)} %collective-permute-done.16.refs_2_, ...), custom_call_target="tpu_custom_call" | custom-call | flops 17179869184 | bytes 67108864 | tf_op jit(solution)/shard_map/last/pallas_call | solution.py:25
  (20 shorter events, 0.1 us)
Async XLA Ops:
  0.6 4.2 %collective-permute-start = (bf16[512,512]{1,0:T(8,128)(2,1)}, bf16[512,512]{1,0:T(8,128)(2,1)S(1)}, u32[]{:S(2)}, u32[]{:S(2)}) collective-permute-start(bf16[512,512]{1,0:T(8,128)(2,1)} %x.3), channel_id=1, source_target_pairs={{0,1},{1,0},{2,3},{3,2},{4,5},{5,4},{6,7},{7,6},{8,9},{9,8},{10,11... | collective-permute-start | bytes 1572872 | tf_op jit(solution)/shard_map/ppermute | solution.py:269
  2.2 9.7 %collective-permute-start.1 = (bf16[256,512]{1,0:T(8,128)(2,1)S(1)}, bf16[256,512]{1,0:T(8,128)(2,1)S(1)}, u32[]{:S(2)}, u32[]{:S(2)}) collective-permute-start(bf16[256,512]{1,0:T(8,128)(2,1)S(1)} %get-tuple-element.34), channel_id=1, source_target_pairs={{0,2},{2,0},{4,6},{6,4},{8,10},{10,8},{12,14},{14,12},{1,3},{3,1},... | collective-permute-start | bytes 786440 | tf_op jit(solution)/shard_map/ppermute | solution.py:266
  4.8 12.6 %collective-permute-start.3 = (bf16[256,512]{1,0:T(8,128)(2,1)S(1)}, bf16[256,512]{1,0:T(8,128)(2,1)S(1)}, u32[]{:S(2)}, u32[]{:S(2)}) collective-permute-start(bf16[256,512]{1,0:T(8,128)(2,1)S(1)} %get-tuple-element.41), channel_id=1, source_target_pairs={{0,2},{2,0},{4,6},{6,4},{8,10},{10,8},{12,14},{14,12},{1,3},{3,1},... | collective-permute-start | bytes 786440 | tf_op jit(solution)/shard_map/ppermute | solution.py:266
  6.4 7.6 %copy-start.1 = (bf16[512,512]{1,0:T(8,128)(2,1)S(1)}, bf16[512,512]{1,0:T(8,128)(2,1)}, u32[]{:S(2)}) copy-start(bf16[512,512]{1,0:T(8,128)(2,1)} %x.3) | copy-start | bytes 1572868
  6.4 7.6 %copy-start.4 = (bf16[512,512]{1,0:T(8,128)(2,1)S(1)}, bf16[512,512]{1,0:T(8,128)(2,1)}, u32[]{:S(2)}) copy-start(bf16[512,512]{1,0:T(8,128)(2,1)} %w_self.3) | copy-start | bytes 1572868
  11.9 9.8 %collective-permute-start.5 = (bf16[256,512]{1,0:T(8,128)(2,1)S(1)}, bf16[256,512]{1,0:T(8,128)(2,1)S(1)}, u32[]{:S(2)}, u32[]{:S(2)}) collective-permute-start(bf16[256,512]{1,0:T(8,128)(2,1)S(1)} %collective-permute-done.1.refs_3_), channel_id=1, source_target_pairs={{0,4},{2,14},{4,8},{6,2},{8,12},{10,6},{12,0},{14,10},{1,5},{3,15}... | collective-permute-start | bytes 786440 | tf_op jit(solution)/shard_map/ppermute | solution.py:266
  14.0 5.7 %collective-permute-start.2 = (bf16[256,512]{1,0:T(8,128)(2,1)S(1)}, bf16[256,512]{1,0:T(8,128)(2,1)S(1)}, u32[]{:S(2)}, u32[]{:S(2)}) collective-permute-start(bf16[256,512]{1,0:T(8,128)(2,1)S(1)} %collective-permute-done.1.refs_3_), channel_id=1, source_target_pairs={{0,1},{1,0},{2,3},{3,2},{4,5},{5,4},{6,7},{7,6},{8,9},{9,8},{10,11... | collective-permute-start | bytes 786440 | tf_op jit(solution)/shard_map/ppermute | solution.py:269
  14.0 5.2 %copy-start.6 = (bf16[1536,512]{1,0:T(8,128)(2,1)S(1)}, bf16[1536,512]{1,0:T(8,128)(2,1)}, u32[]{:S(2)}) copy-start(bf16[1536,512]{1,0:T(8,128)(2,1)} %get-tuple-element.43) | copy-start | bytes 4718596
  17.4 10.0 %collective-permute-start.8 = (bf16[256,512]{1,0:T(8,128)(2,1)S(1)}, bf16[256,512]{1,0:T(8,128)(2,1)S(1)}, u32[]{:S(2)}, u32[]{:S(2)}) collective-permute-start(bf16[256,512]{1,0:T(8,128)(2,1)S(1)} %collective-permute-done.3.refs_5_), channel_id=1, source_target_pairs={{0,4},{2,14},{4,8},{6,2},{8,12},{10,6},{12,0},{14,10},{1,5},{3,15}... | collective-permute-start | bytes 786440 | tf_op jit(solution)/shard_map/ppermute | solution.py:266
  19.2 3.9 %collective-permute-start.4 = (bf16[256,512]{1,0:T(8,128)(2,1)S(1)}, bf16[256,512]{1,0:T(8,128)(2,1)S(1)}, u32[]{:S(2)}, u32[]{:S(2)}) collective-permute-start(bf16[256,512]{1,0:T(8,128)(2,1)S(1)} %collective-permute-done.3.refs_5_), channel_id=1, source_target_pairs={{0,1},{1,0},{2,3},{3,2},{4,5},{5,4},{6,7},{7,6},{8,9},{9,8},{10,11... | collective-permute-start | bytes 786440 | tf_op jit(solution)/shard_map/ppermute | solution.py:269
  19.2 3.8 %collective-permute-start.6 = (bf16[1536,512]{1,0:T(8,128)(2,1)S(1)}, bf16[1536,512]{1,0:T(8,128)(2,1)S(1)}, u32[]{:S(2)}, u32[]{:S(2)}) collective-permute-start(bf16[1536,512]{1,0:T(8,128)(2,1)S(1)} %copy-done.6), channel_id=1, source_target_pairs={{0,1},{1,0},{2,3},{3,2},{4,5},{5,4},{6,7},{7,6},{8,9},{9,8},{10,11... | collective-permute-start | bytes 4718600 | tf_op jit(solution)/shard_map/ppermute | solution.py:269
  23.0 4.4 %collective-permute-start.7 = (bf16[256,512]{1,0:T(8,128)(2,1)S(1)}, bf16[256,512]{1,0:T(8,128)(2,1)S(1)}, u32[]{:S(2)}, u32[]{:S(2)}) collective-permute-start(bf16[256,512]{1,0:T(8,128)(2,1)S(1)} %collective-permute-done.5.refs_3_), channel_id=1, source_target_pairs={{0,1},{1,0},{2,3},{3,2},{4,5},{5,4},{6,7},{7,6},{8,9},{9,8},{10,11... | collective-permute-start | bytes 786440 | tf_op jit(solution)/shard_map/ppermute | solution.py:269
  23.5 5.4 %copy-start.2 = (bf16[512,512]{1,0:T(8,128)(2,1)S(1)}, bf16[512,512]{1,0:T(8,128)(2,1)}, u32[]{:S(2)}) copy-start(bf16[512,512]{1,0:T(8,128)(2,1)} %w_neigh.1) | copy-start | bytes 1572868
  23.6 5.4 %copy-start.3 = (bf16[512,512]{1,0:T(8,128)(2,1)S(1)}, bf16[512,512]{1,0:T(8,128)(2,1)}, u32[]{:S(2)}) copy-start(bf16[512,512]{1,0:T(8,128)(2,1)} %cotangent.1) | copy-start | bytes 1572868
  23.6 5.4 %copy-start.5 = (s32[512]{0:T(512)S(1)}, s32[512]{0:T(512)}, u32[]{:S(2)}) copy-start(s32[512]{0:T(512)} %param.14) | copy-start | bytes 6148
  27.4 1.5 %collective-permute-start.9 = (bf16[256,512]{1,0:T(8,128)(2,1)S(1)}, bf16[256,512]{1,0:T(8,128)(2,1)S(1)}, u32[]{:S(2)}, u32[]{:S(2)}) collective-permute-start(bf16[256,512]{1,0:T(8,128)(2,1)S(1)} %collective-permute-done.8.refs_3_), channel_id=1, source_target_pairs={{0,1},{1,0},{2,3},{3,2},{4,5},{5,4},{6,7},{7,6},{8,9},{9,8},{10,11... | collective-permute-start | bytes 786440 | tf_op jit(solution)/shard_map/ppermute | solution.py:269
  28.9 2.1 %copy-start = (bf16[1536,512]{1,0:T(8,128)(2,1)S(1)}, bf16[1536,512]{1,0:T(8,128)(2,1)}, u32[]{:S(2)}) copy-start(bf16[1536,512]{1,0:T(8,128)(2,1)} %get-tuple-element.48.mine) | copy-start | bytes 4718596
  30.8 2.0 %collective-permute-start.10 = (bf16[512,512]{1,0:T(8,128)(2,1)S(1)}, bf16[512,512]{1,0:T(8,128)(2,1)S(1)}, u32[]{:S(2)}, u32[]{:S(2)}) collective-permute-start(bf16[512,512]{1,0:T(8,128)(2,1)S(1)} %get-tuple-element.50.g), channel_id=1, source_target_pairs={{0,1},{1,0},{2,3},{3,2},{4,5},{5,4},{6,7},{7,6},{8,9},{9,8},{10,11... | collective-permute-start | bytes 1572872 | tf_op jit(solution)/shard_map/ppermute | solution.py:269
  33.2 6.4 %collective-permute-start.11 = (bf16[128,512]{1,0:T(8,128)(2,1)S(1)}, bf16[128,512]{1,0:T(8,128)(2,1)S(1)}, u32[]{:S(2)}, u32[]{:S(2)}) collective-permute-start(bf16[128,512]{1,0:T(8,128)(2,1)S(1)} %get-tuple-element.55), channel_id=1, source_target_pairs={{4,0},{14,2},{8,4},{2,6},{12,8},{6,10},{0,12},{10,14},{5,1},{15,3}... | collective-permute-start | bytes 393224 | tf_op jit(solution)/shard_map/ppermute | solution.py:266
  35.0 7.7 %collective-permute-start.13 = (bf16[128,512]{1,0:T(8,128)(2,1)S(1)}, bf16[128,512]{1,0:T(8,128)(2,1)S(1)}, u32[]{:S(2)}, u32[]{:S(2)}) collective-permute-start(bf16[128,512]{1,0:T(8,128)(2,1)S(1)} %get-tuple-element.56), channel_id=1, source_target_pairs={{4,0},{14,2},{8,4},{2,6},{12,8},{6,10},{0,12},{10,14},{5,1},{15,3}... | collective-permute-start | bytes 393224 | tf_op jit(solution)/shard_map/ppermute | solution.py:266
  35.4 10.0 %collective-permute-start.15 = (bf16[128,512]{1,0:T(8,128)(2,1)S(1)}, bf16[128,512]{1,0:T(8,128)(2,1)S(1)}, u32[]{:S(2)}, u32[]{:S(2)}) collective-permute-start(bf16[128,512]{1,0:T(8,128)(2,1)S(1)} %get-tuple-element.57), channel_id=1, source_target_pairs={{4,0},{14,2},{8,4},{2,6},{12,8},{6,10},{0,12},{10,14},{5,1},{15,3}... | collective-permute-start | bytes 393224 | tf_op jit(solution)/shard_map/ppermute | solution.py:266
  35.9 12.4 %collective-permute-start.17 = (bf16[128,512]{1,0:T(8,128)(2,1)S(1)}, bf16[128,512]{1,0:T(8,128)(2,1)S(1)}, u32[]{:S(2)}, u32[]{:S(2)}) collective-permute-start(bf16[128,512]{1,0:T(8,128)(2,1)S(1)} %get-tuple-element.58), channel_id=1, source_target_pairs={{4,0},{14,2},{8,4},{2,6},{12,8},{6,10},{0,12},{10,14},{5,1},{15,3}... | collective-permute-start | bytes 393224 | tf_op jit(solution)/shard_map/ppermute | solution.py:266
  39.6 11.0 %collective-permute-start.12 = (bf16[128,512]{1,0:T(8,128)(2,1)S(1)}, bf16[128,512]{1,0:T(8,128)(2,1)S(1)}, u32[]{:S(2)}, u32[]{:S(2)}) collective-permute-start(bf16[128,512]{1,0:T(8,128)(2,1)S(1)} %add.4), channel_id=1, source_target_pairs={{0,2},{2,0},{4,6},{6,4},{8,10},{10,8},{12,14},{14,12},{1,3},{3,1},... | collective-permute-start | bytes 393224 | tf_op jit(solution)/shard_map/ppermute | solution.py:266
  42.7 7.9 %collective-permute-start.14 = (bf16[128,512]{1,0:T(8,128)(2,1)S(1)}, bf16[128,512]{1,0:T(8,128)(2,1)S(1)}, u32[]{:S(2)}, u32[]{:S(2)}) collective-permute-start(bf16[128,512]{1,0:T(8,128)(2,1)S(1)} %add.5), channel_id=1, source_target_pairs={{0,2},{2,0},{4,6},{6,4},{8,10},{10,8},{12,14},{14,12},{1,3},{3,1},... | collective-permute-start | bytes 393224 | tf_op jit(solution)/shard_map/ppermute | solution.py:266
  45.5 5.8 %collective-permute-start.16 = (bf16[128,512]{1,0:T(8,128)(2,1)S(1)}, bf16[128,512]{1,0:T(8,128)(2,1)S(1)}, u32[]{:S(2)}, u32[]{:S(2)}) collective-permute-start(bf16[128,512]{1,0:T(8,128)(2,1)S(1)} %add.6), channel_id=1, source_target_pairs={{0,2},{2,0},{4,6},{6,4},{8,10},{10,8},{12,14},{14,12},{1,3},{3,1},... | collective-permute-start | bytes 393224 | tf_op jit(solution)/shard_map/ppermute | solution.py:266
  48.3 5.7 %collective-permute-start.18 = (bf16[128,512]{1,0:T(8,128)(2,1)S(1)}, bf16[128,512]{1,0:T(8,128)(2,1)S(1)}, u32[]{:S(2)}, u32[]{:S(2)}) collective-permute-start(bf16[128,512]{1,0:T(8,128)(2,1)S(1)} %add.7), channel_id=1, source_target_pairs={{0,2},{2,0},{4,6},{6,4},{8,10},{10,8},{12,14},{14,12},{1,3},{3,1},... | collective-permute-start | bytes 393224 | tf_op jit(solution)/shard_map/ppermute | solution.py:266

commit v5 on v4

--- a/solution.py
+++ b/solution.py
@@ -185,7 +185,7 @@
 
 def middle_kernel(
     start, messages, own, adj, last, norm, w_neigh, cotangent,
-    out, pre_grad, grad, out_buffer, sem,
+    out, pre_grad, grad,
 ):
     kind = out.dtype
     across = (1.0 / norm[...].astype(jnp.float32)).T
@@ -194,22 +194,22 @@
     aggregate = (total * inverse).astype(kind)
     v = own[...] + dot(aggregate, w_neigh[...])
     q = 1.0 / (1.0 + jnp.exp(-v))
-    out_buffer[...] = (v * q).astype(kind)
-    store = pltpu.make_async_copy(out_buffer, out, sem)
-    store.start()
+    out[...] = (v * q).astype(kind)
     p = (cotangent[...].astype(jnp.float32) * (q * (1.0 + v * (1.0 - q)))).astype(kind)
     pre_grad[...] = p
     grad[...] = (dot_t(p, w_neigh[...]) * inverse).astype(kind)
-    store.wait()
-
-
-def first_kernel(mine, g, theirs, tx, tz, kept, sem):
+
+
+def first_kernel(mine, g, theirs, near, tx, tz, kept, out, sems):
     rows = tz.shape[0]
-    fetch = pltpu.make_async_copy(theirs.at[:2 * rows], kept, sem)
+    fetch = pltpu.make_async_copy(theirs.at[:2 * rows], kept, sems.at[0])
+    store = pltpu.make_async_copy(near, out, sems.at[1])
     fetch.start()
+    store.start()
     tx[...] = dot(mine[:rows, :], g[...])
     tz[...] = dot(mine[rows:2 * rows, :], g[...])
     fetch.wait()
+    store.wait()
 
 
 def across_kernel(theirs, g_sib, tz, *pz):
@@ -310,17 +310,17 @@
         functools.partial(middle_kernel, rows + cut),
         [narrow, narrow, narrow],
         messages, own, fz, zb_sib, norm, w_neigh, cotangent,
-        out_specs=[ANY, VMEM, VMEM],
-        scratch=[pltpu.VMEM((rows, width), kind), pltpu.SemaphoreType.DMA],
         name="middle",
     )
     g_sib = sub(g)
 
-    tx, tz, theirs_near = call(
-        first_kernel, [wide, wide, jax.ShapeDtypeStruct((2 * rows, width), kind)],
-        mine, g, theirs,
-        specs=[VMEM, VMEM, pl.BlockSpec(memory_space=pltpu.HBM)],
-        scratch=[pltpu.SemaphoreType.DMA],
+    tx, tz, theirs_near, node_out = call(
+        first_kernel,
+        [wide, wide, jax.ShapeDtypeStruct((2 * rows, width), kind), narrow],
+        mine, g, theirs, node_out,
+        specs=[VMEM, VMEM, pl.BlockSpec(memory_space=pltpu.HBM), VMEM],
+        out_specs=[VMEM, VMEM, VMEM, ANY],
+        scratch=[pltpu.SemaphoreType.DMA((2,))],
         name="first",
     )
     sizes = [block] * (rows // block)

time: 55.1 us -> 54.5 us (0.989)
  transfers between devices with their start and end apart: 19 -> 19, of which waited for: 10 -> 10; matrix products, arithmetic and copies ran while one was open for 0% -> 0% of each run, Pallas kernels for 20% -> 21%
where the time goes in v5:
time: 54.5 us; the launch traced here: 54.4 us
  starting transfers between devices  23.8 us (44%)
  waiting for transfers between devices  15.8 us (29%)
  Pallas kernels  13.9 us (26%)
  between operations  0.8 us (1%)
    ppermute x12, starting transfers between devices, slab(): return lax.ppermute(v, 'slab', route)  22.4 us
    pallas_call x16, Pallas kernels, call(): pl.pallas_call(kernel, in_specs=specs or [VMEM] * len(args), out_specs=ou...  13.9 us
    ppermute x12, waiting for transfers between devices, slab(): return lax.ppermute(v, 'slab', route)  12.8 us
    ppermute x7, waiting for transfers between devices, sub(): return lax.ppermute(v, 'sub', swap)  3 us
    ppermute x7, starting transfers between devices, sub(): return lax.ppermute(v, 'sub', swap)  1.38 us
  transfers between devices with their start and end apart: 19, of which 10 were waited for; matrix products, arithmetic and copies ran while one was open for 0% of the time, Pallas kernels for 21%

profile of v5, /device:TPU:0, one launch (start us, length us, event | category | flops | bytes accessed | tf_op | source)
XLA Modules:
  0.0 54.4 jit_solution(3927558518115177721)
XLA Ops:
  0.6 0.5 collective-permute-start
  1.1 1.0 %split.1 = (bf16[256,512]{1,0:T(8,128)(2,1)S(1)}, bf16[256,512]{1,0:T(8,128)(2,1)S(1)}) custom-call(bf16[512,512]{1,0:T(8,128)(2,1)} %x.3), custom_call_target="tpu_custom_call" | custom-call | flops 17179869184 | bytes 67108864 | tf_op jit(solution)/shard_map/split/pallas_call | solution.py:25
  2.2 2.6 %collective-permute-start.1 = (bf16[256,512]{1,0:T(8,128)(2,1)S(1)}, bf16[256,512]{1,0:T(8,128)(2,1)S(1)}, u32[]{:S(2)}, u32[]{:S(2)}) collective-permute-start(bf16[256,512]{1,0:T(8,128)(2,1)S(1)} %get-tuple-element.35), channel_id=1, source_target_pairs={{0,2},{2,0},{4,6},{6,4},{8,10},{10,8},{12,14},{14,12},{1,3},{3,1},... | collective-permute-start | bytes 786440 | tf_op jit(solution)/shard_map/ppermute | solution.py:266
  4.8 0.1 collective-permute-start.3
  4.8 0.0 collective-permute-done.x_sib
  4.9 1.5 %dense_pair.1.refs_0_.refs_1_.refs_2_ = bf16[512,1024]{1,0:T(8,128)(2,1)S(1)} custom-call(s32[3,4,6]{2,1,0:T(4,128)} %bitcast.4, s32[3,4,6]{2,1,0:T(4,128)} %bitcast.6, bf16[4,3,6,128,128]{4,3,2,1,0:T(8,128)(2,1)} %tiles.3), custom_call_target="tpu_custom_call" | custom-call | flops 67108864 | bytes 262144 | tf_op jit(solution)/shard_map/dense_pair/pallas_call | solution.py:25
  6.4 0.0 copy-start.1
  6.4 0.0 copy-start.4
  6.4 3.9 %dense_across.1 = (bf16[512,1024]{1,0:T(8,128)(2,1)S(1)}, bf16[512,1024]{1,0:T(8,128)(2,1)S(1)}, bf16[1536,512]{1,0:T(8,128)(2,1)}, bf16[1536,512]{1,0:T(8,128)(2,1)}) custom-call(s32[3,4,6]{2,1,0:T(4,128)} %bitcast.5, s32[3,4,6]{2,1,0:T(4,128)} %bitcast.7, bf16[4,3,6,128,128]{4,3,2,1,0:T(8,128)(2,1)} %tiles.3, ...), custom_call_target="tpu_custom_call" | custom-call | flops 134217728 | bytes 524288 | tf_op jit(solution)/shard_map/dense_across/pallas_call | solution.py:25
  10.3 1.6 %collective-permute-done.1.refs_3_ = bf16[256,512]{1,0:T(8,128)(2,1)S(1)} collective-permute-done((bf16[256,512]{1,0:T(8,128)(2,1)S(1)}, bf16[256,512]{1,0:T(8,128)(2,1)S(1)}, u32[]{:S(2)}, u32[]{:S(2)}) %collective-permute-start.1) | collective-permute-done | bytes 262176 | tf_op jit(solution)/shard_map/ppermute | solution.py:266
  11.9 2.0 %collective-permute-start.5 = (bf16[256,512]{1,0:T(8,128)(2,1)S(1)}, bf16[256,512]{1,0:T(8,128)(2,1)S(1)}, u32[]{:S(2)}, u32[]{:S(2)}) collective-permute-start(bf16[256,512]{1,0:T(8,128)(2,1)S(1)} %collective-permute-done.1.refs_3_), channel_id=1, source_target_pairs={{0,4},{2,14},{4,8},{6,2},{8,12},{10,6},{12,0},{14,10},{1,5},{3,15}... | collective-permute-start | bytes 786440 | tf_op jit(solution)/shard_map/ppermute | solution.py:266
  14.0 0.0 collective-permute-start.2
  14.0 1.0 %local.1 = (f32[512,512]{1,0:T(8,128)S(1)}, f32[512,512]{1,0:T(8,128)S(1)}) custom-call(bf16[512,1024]{1,0:T(8,128)(2,1)S(1)} %get-tuple-element.39.adj, bf16[512,512]{1,0:T(8,128)(2,1)S(1)} %copy-done.1, bf16[512,512]{1,0:T(8,128)(2,1)S(1)} %collective-permute-done.x_sib, bf16[512,512]{1,0:T(8,128)(2,1)S(1)} %copy-done.4), custom_call_target="tpu_custom_call" | custom-call | flops 17179869184 | bytes 67108864 | tf_op jit(solution)/shard_map/local/pallas_call | solution.py:25
  15.0 2.4 %collective-permute-done.3.refs_5_ = bf16[256,512]{1,0:T(8,128)(2,1)S(1)} collective-permute-done((bf16[256,512]{1,0:T(8,128)(2,1)S(1)}, bf16[256,512]{1,0:T(8,128)(2,1)S(1)}, u32[]{:S(2)}, u32[]{:S(2)}) %collective-permute-start.3) | collective-permute-done | bytes 262176 | tf_op jit(solution)/shard_map/ppermute | solution.py:266
  17.4 1.8 %collective-permute-start.8 = (bf16[256,512]{1,0:T(8,128)(2,1)S(1)}, bf16[256,512]{1,0:T(8,128)(2,1)S(1)}, u32[]{:S(2)}, u32[]{:S(2)}) collective-permute-start(bf16[256,512]{1,0:T(8,128)(2,1)S(1)} %collective-permute-done.3.refs_5_), channel_id=1, source_target_pairs={{0,4},{2,14},{4,8},{6,2},{8,12},{10,6},{12,0},{14,10},{1,5},{3,15}... | collective-permute-start | bytes 786440 | tf_op jit(solution)/shard_map/ppermute | solution.py:266
  19.2 0.0 collective-permute-start.4
  19.2 0.5 collective-permute-start.6
  19.7 0.0 collective-permute-done.2.refs_4_
  19.7 0.6 %gather.3.messages = f32[512,512]{1,0:T(8,128)S(1)} custom-call(f32[512,512]{1,0:T(8,128)S(1)} %get-tuple-element.40.messages, bf16[512,1024]{1,0:T(8,128)(2,1)S(1)} %dense_pair.1.refs_0_.refs_1_.refs_2_, bf16[512,1024]{1,0:T(8,128)(2,1)S(1)} %dense_pair.1.refs_0_.refs_1_.refs_2_, bf16[512,1024]{1,0:T(8,128)(2,1)S(1)} %dense_pair.1.refs_0_.refs_1_.refs_2_, ...), custom_call_target="tpu_custom_call" | custom-call | flops 17179869184 | bytes 67108864 | tf_op jit(solution)/shard_map/gather/pallas_call | solution.py:25
  20.3 1.5 %collective-permute-done.5.refs_3_ = bf16[256,512]{1,0:T(8,128)(2,1)S(1)} collective-permute-done((bf16[256,512]{1,0:T(8,128)(2,1)S(1)}, bf16[256,512]{1,0:T(8,128)(2,1)S(1)}, u32[]{:S(2)}, u32[]{:S(2)}) %collective-permute-start.5) | collective-permute-done | bytes 262176 | tf_op jit(solution)/shard_map/ppermute | solution.py:266
  21.8 1.2 %collective-permute-done.6.theirs = bf16[1536,512]{1,0:T(8,128)(2,1)S(1)} collective-permute-done((bf16[1536,512]{1,0:T(8,128)(2,1)S(1)}, bf16[1536,512]{1,0:T(8,128)(2,1)S(1)}, u32[]{:S(2)}, u32[]{:S(2)}) %collective-permute-start.6) | collective-permute-done | bytes 1572896 | tf_op jit(solution)/shard_map/ppermute | solution.py:269
  23.0 0.1 collective-permute-start.7
  23.1 0.4 gather.4.messages
  23.5 0.0 copy-start.2
  23.6 0.0 copy-start.3
  23.6 0.0 copy-start.5
  23.6 3.8 %collective-permute-done.8.refs_3_ = bf16[256,512]{1,0:T(8,128)(2,1)S(1)} collective-permute-done((bf16[256,512]{1,0:T(8,128)(2,1)S(1)}, bf16[256,512]{1,0:T(8,128)(2,1)S(1)}, u32[]{:S(2)}, u32[]{:S(2)}) %collective-permute-start.8) | collective-permute-done | bytes 262176 | tf_op jit(solution)/shard_map/ppermute | solution.py:266
  27.4 0.4 gather.5.messages
  27.8 1.1 %collective-permute-done.9.last = bf16[256,512]{1,0:T(8,128)(2,1)S(1)} collective-permute-done((bf16[256,512]{1,0:T(8,128)(2,1)S(1)}, bf16[256,512]{1,0:T(8,128)(2,1)S(1)}, u32[]{:S(2)}, u32[]{:S(2)}) %collective-permute-start.9) | collective-permute-done | bytes 262176 | tf_op jit(solution)/shard_map/ppermute | solution.py:269
  28.9 1.3 %middle.1 = (bf16[512,512]{1,0:T(8,128)(2,1)S(1)}, bf16[512,512]{1,0:T(8,128)(2,1)S(1)}, bf16[512,512]{1,0:T(8,128)(2,1)S(1)}) custom-call(f32[512,512]{1,0:T(8,128)S(1)} %gather.5.messages, f32[512,512]{1,0:T(8,128)S(1)} %get-tuple-element.48.own, bf16[512,1024]{1,0:T(8,128)(2,1)S(1)} %get-tuple-element.41.refs_1_.refs_0_.adj, ...), custom_call_target="tpu_custom_call" | custom-call | flops 17179869184 | bytes 67108864 | tf_op jit(solution)/shard_map/middle/pallas_call | solution.py:25
  30.3 0.2 collective-permute-start.10
  30.5 1.0 %first.1 = (f32[512,512]{1,0:T(8,128)S(1)}, f32[512,512]{1,0:T(8,128)S(1)}, bf16[1024,512]{1,0:T(8,128)(2,1)S(1)}, bf16[512,512]{1,0:T(8,128)(2,1)}) custom-call(bf16[1536,512]{1,0:T(8,128)(2,1)S(1)} %copy-done, bf16[512,512]{1,0:T(8,128)(2,1)S(1)} %get-tuple-element.49.g, bf16[1536,512]{1,0:T(8,128)(2,1)S(1)} %collective-permute-done.6.theirs, ...), custom_call_target="tpu_custom_call" | custom-call | flops 17179869184 | bytes 67108864 | tf_op jit(solution)/shard_map/first/pallas_call | solution.py:25
  31.5 0.7 %collective-permute-done.10.g_sib = bf16[512,512]{1,0:T(8,128)(2,1)S(1)} collective-permute-done((bf16[512,512]{1,0:T(8,128)(2,1)S(1)}, bf16[512,512]{1,0:T(8,128)(2,1)S(1)}, u32[]{:S(2)}, u32[]{:S(2)}) %collective-permute-start.10) | collective-permute-done | bytes 524320 | tf_op jit(solution)/shard_map/ppermute | solution.py:269
  32.2 0.4 across.1
  32.7 1.8 %collective-permute-start.11 = (bf16[128,512]{1,0:T(8,128)(2,1)S(1)}, bf16[128,512]{1,0:T(8,128)(2,1)S(1)}, u32[]{:S(2)}, u32[]{:S(2)}) collective-permute-start(bf16[128,512]{1,0:T(8,128)(2,1)S(1)} %get-tuple-element.57), channel_id=1, source_target_pairs={{4,0},{14,2},{8,4},{2,6},{12,8},{6,10},{0,12},{10,14},{5,1},{15,3}... | collective-permute-start | bytes 393224 | tf_op jit(solution)/shard_map/ppermute | solution.py:266
  34.5 0.4 collective-permute-start.13
  34.9 0.5 collective-permute-start.15
  35.4 2.3 %collective-permute-start.17 = (bf16[128,512]{1,0:T(8,128)(2,1)S(1)}, bf16[128,512]{1,0:T(8,128)(2,1)S(1)}, u32[]{:S(2)}, u32[]{:S(2)}) collective-permute-start(bf16[128,512]{1,0:T(8,128)(2,1)S(1)} %get-tuple-element.60), channel_id=1, source_target_pairs={{4,0},{14,2},{8,4},{2,6},{12,8},{6,10},{0,12},{10,14},{5,1},{15,3}... | collective-permute-start | bytes 393224 | tf_op jit(solution)/shard_map/ppermute | solution.py:266
  37.7 1.2 %own.1 = (f32[512,512]{1,0:T(8,128)S(1)}, f32[512,512]{1,0:T(8,128)S(1)}) custom-call(bf16[1536,512]{1,0:T(8,128)(2,1)S(1)} %copy-done, bf16[1536,512]{1,0:T(8,128)(2,1)S(1)} %collective-permute-done.6.theirs, bf16[1024,512]{1,0:T(8,128)(2,1)S(1)} %get-tuple-element.53.theirs.near, bf16[512,512]{1,0:T(8,128)(2,1)S(1)} %get-tuple-element.49.g, ...), custom_call_target="tpu_custom_call" | custom-call | flops 17179869184 | bytes 67108864 | tf_op jit(solution)/shard_map/own/pallas_call | solution.py:25
  38.9 0.1 collective-permute-done.11.b
  39.1 3.0 %collective-permute-start.12 = (bf16[128,512]{1,0:T(8,128)(2,1)S(1)}, bf16[128,512]{1,0:T(8,128)(2,1)S(1)}, u32[]{:S(2)}, u32[]{:S(2)}) collective-permute-start(bf16[128,512]{1,0:T(8,128)(2,1)S(1)} %add.4), channel_id=1, source_target_pairs={{0,2},{2,0},{4,6},{6,4},{8,10},{10,8},{12,14},{14,12},{1,3},{3,1},... | collective-permute-start | bytes 393224 | tf_op jit(solution)/shard_map/ppermute | solution.py:266
  42.1 0.0 collective-permute-done.13.b
  42.2 2.8 %collective-permute-start.14 = (bf16[128,512]{1,0:T(8,128)(2,1)S(1)}, bf16[128,512]{1,0:T(8,128)(2,1)S(1)}, u32[]{:S(2)}, u32[]{:S(2)}) collective-permute-start(bf16[128,512]{1,0:T(8,128)(2,1)S(1)} %add.5), channel_id=1, source_target_pairs={{0,2},{2,0},{4,6},{6,4},{8,10},{10,8},{12,14},{14,12},{1,3},{3,1},... | collective-permute-start | bytes 393224 | tf_op jit(solution)/shard_map/ppermute | solution.py:266
  45.0 2.8 %collective-permute-start.16 = (bf16[128,512]{1,0:T(8,128)(2,1)S(1)}, bf16[128,512]{1,0:T(8,128)(2,1)S(1)}, u32[]{:S(2)}, u32[]{:S(2)}) collective-permute-start(bf16[128,512]{1,0:T(8,128)(2,1)S(1)} %add.6), channel_id=1, source_target_pairs={{0,2},{2,0},{4,6},{6,4},{8,10},{10,8},{12,14},{14,12},{1,3},{3,1},... | collective-permute-start | bytes 393224 | tf_op jit(solution)/shard_map/ppermute | solution.py:266
  47.8 2.3 %collective-permute-start.18 = (bf16[128,512]{1,0:T(8,128)(2,1)S(1)}, bf16[128,512]{1,0:T(8,128)(2,1)S(1)}, u32[]{:S(2)}, u32[]{:S(2)}) collective-permute-start(bf16[128,512]{1,0:T(8,128)(2,1)S(1)} %add.7), channel_id=1, source_target_pairs={{0,2},{2,0},{4,6},{6,4},{8,10},{10,8},{12,14},{14,12},{1,3},{3,1},... | collective-permute-start | bytes 393224 | tf_op jit(solution)/shard_map/ppermute | solution.py:266
  50.1 0.7 %collective-permute-done.16.refs_2_ = bf16[128,512]{1,0:T(8,128)(2,1)S(1)} collective-permute-done((bf16[128,512]{1,0:T(8,128)(2,1)S(1)}, bf16[128,512]{1,0:T(8,128)(2,1)S(1)}, u32[]{:S(2)}, u32[]{:S(2)}) %collective-permute-start.16) | collective-permute-done | bytes 131104 | tf_op jit(solution)/shard_map/ppermute | solution.py:266
  50.8 2.7 %collective-permute-done.18.refs_3_ = bf16[128,512]{1,0:T(8,128)(2,1)S(1)} collective-permute-done((bf16[128,512]{1,0:T(8,128)(2,1)S(1)}, bf16[128,512]{1,0:T(8,128)(2,1)S(1)}, u32[]{:S(2)}, u32[]{:S(2)}) %collective-permute-start.18) | collective-permute-done | bytes 131104 | tf_op jit(solution)/shard_map/ppermute | solution.py:266
  53.5 0.8 %last.1 = bf16[512,512]{1,0:T(8,128)(2,1)} custom-call(f32[512,512]{1,0:T(8,128)S(1)} %get-tuple-element.62.own, bf16[128,512]{1,0:T(8,128)(2,1)S(1)} %collective-permute-done.12.refs_0_, bf16[128,512]{1,0:T(8,128)(2,1)S(1)} %collective-permute-done.14.refs_1_, bf16[128,512]{1,0:T(8,128)(2,1)S(1)} %collective-permute-done.16.refs_2_, ...), custom_call_target="tpu_custom_call" | custom-call | flops 17179869184 | bytes 67108864 | tf_op jit(solution)/shard_map/last/pallas_call | solution.py:25
  (20 shorter events, 0.1 us)
Async XLA Ops:
  0.6 4.2 %collective-permute-start = (bf16[512,512]{1,0:T(8,128)(2,1)}, bf16[512,512]{1,0:T(8,128)(2,1)S(1)}, u32[]{:S(2)}, u32[]{:S(2)}) collective-permute-start(bf16[512,512]{1,0:T(8,128)(2,1)} %x.3), channel_id=1, source_target_pairs={{0,1},{1,0},{2,3},{3,2},{4,5},{5,4},{6,7},{7,6},{8,9},{9,8},{10,11... | collective-permute-start | bytes 1572872 | tf_op jit(solution)/shard_map/ppermute | solution.py:269
  2.2 9.7 %collective-permute-start.1 = (bf16[256,512]{1,0:T(8,128)(2,1)S(1)}, bf16[256,512]{1,0:T(8,128)(2,1)S(1)}, u32[]{:S(2)}, u32[]{:S(2)}) collective-permute-start(bf16[256,512]{1,0:T(8,128)(2,1)S(1)} %get-tuple-element.35), channel_id=1, source_target_pairs={{0,2},{2,0},{4,6},{6,4},{8,10},{10,8},{12,14},{14,12},{1,3},{3,1},... | collective-permute-start | bytes 786440 | tf_op jit(solution)/shard_map/ppermute | solution.py:266
  4.8 12.6 %collective-permute-start.3 = (bf16[256,512]{1,0:T(8,128)(2,1)S(1)}, bf16[256,512]{1,0:T(8,128)(2,1)S(1)}, u32[]{:S(2)}, u32[]{:S(2)}) collective-permute-start(bf16[256,512]{1,0:T(8,128)(2,1)S(1)} %get-tuple-element.43), channel_id=1, source_target_pairs={{0,2},{2,0},{4,6},{6,4},{8,10},{10,8},{12,14},{14,12},{1,3},{3,1},... | collective-permute-start | bytes 786440 | tf_op jit(solution)/shard_map/ppermute | solution.py:266
  6.4 7.6 %copy-start.1 = (bf16[512,512]{1,0:T(8,128)(2,1)S(1)}, bf16[512,512]{1,0:T(8,128)(2,1)}, u32[]{:S(2)}) copy-start(bf16[512,512]{1,0:T(8,128)(2,1)} %x.3) | copy-start | bytes 1572868
  6.4 7.6 %copy-start.4 = (bf16[512,512]{1,0:T(8,128)(2,1)S(1)}, bf16[512,512]{1,0:T(8,128)(2,1)}, u32[]{:S(2)}) copy-start(bf16[512,512]{1,0:T(8,128)(2,1)} %w_self.3) | copy-start | bytes 1572868
  11.9 9.8 %collective-permute-start.5 = (bf16[256,512]{1,0:T(8,128)(2,1)S(1)}, bf16[256,512]{1,0:T(8,128)(2,1)S(1)}, u32[]{:S(2)}, u32[]{:S(2)}) collective-permute-start(bf16[256,512]{1,0:T(8,128)(2,1)S(1)} %collective-permute-done.1.refs_3_), channel_id=1, source_target_pairs={{0,4},{2,14},{4,8},{6,2},{8,12},{10,6},{12,0},{14,10},{1,5},{3,15}... | collective-permute-start | bytes 786440 | tf_op jit(solution)/shard_map/ppermute | solution.py:266
  14.0 5.7 %collective-permute-start.2 = (bf16[256,512]{1,0:T(8,128)(2,1)S(1)}, bf16[256,512]{1,0:T(8,128)(2,1)S(1)}, u32[]{:S(2)}, u32[]{:S(2)}) collective-permute-start(bf16[256,512]{1,0:T(8,128)(2,1)S(1)} %collective-permute-done.1.refs_3_), channel_id=1, source_target_pairs={{0,1},{1,0},{2,3},{3,2},{4,5},{5,4},{6,7},{7,6},{8,9},{9,8},{10,11... | collective-permute-start | bytes 786440 | tf_op jit(solution)/shard_map/ppermute | solution.py:269
  14.0 5.2 %copy-start.6 = (bf16[1536,512]{1,0:T(8,128)(2,1)S(1)}, bf16[1536,512]{1,0:T(8,128)(2,1)}, u32[]{:S(2)}) copy-start(bf16[1536,512]{1,0:T(8,128)(2,1)} %get-tuple-element.45) | copy-start | bytes 4718596
  17.4 10.0 %collective-permute-start.8 = (bf16[256,512]{1,0:T(8,128)(2,1)S(1)}, bf16[256,512]{1,0:T(8,128)(2,1)S(1)}, u32[]{:S(2)}, u32[]{:S(2)}) collective-permute-start(bf16[256,512]{1,0:T(8,128)(2,1)S(1)} %collective-permute-done.3.refs_5_), channel_id=1, source_target_pairs={{0,4},{2,14},{4,8},{6,2},{8,12},{10,6},{12,0},{14,10},{1,5},{3,15}... | collective-permute-start | bytes 786440 | tf_op jit(solution)/shard_map/ppermute | solution.py:266
  19.2 3.9 %collective-permute-start.4 = (bf16[256,512]{1,0:T(8,128)(2,1)S(1)}, bf16[256,512]{1,0:T(8,128)(2,1)S(1)}, u32[]{:S(2)}, u32[]{:S(2)}) collective-permute-start(bf16[256,512]{1,0:T(8,128)(2,1)S(1)} %collective-permute-done.3.refs_5_), channel_id=1, source_target_pairs={{0,1},{1,0},{2,3},{3,2},{4,5},{5,4},{6,7},{7,6},{8,9},{9,8},{10,11... | collective-permute-start | bytes 786440 | tf_op jit(solution)/shard_map/ppermute | solution.py:269
  19.2 3.8 %collective-permute-start.6 = (bf16[1536,512]{1,0:T(8,128)(2,1)S(1)}, bf16[1536,512]{1,0:T(8,128)(2,1)S(1)}, u32[]{:S(2)}, u32[]{:S(2)}) collective-permute-start(bf16[1536,512]{1,0:T(8,128)(2,1)S(1)} %copy-done.6), channel_id=1, source_target_pairs={{0,1},{1,0},{2,3},{3,2},{4,5},{5,4},{6,7},{7,6},{8,9},{9,8},{10,11... | collective-permute-start | bytes 4718600 | tf_op jit(solution)/shard_map/ppermute | solution.py:269
  23.0 4.4 %collective-permute-start.7 = (bf16[256,512]{1,0:T(8,128)(2,1)S(1)}, bf16[256,512]{1,0:T(8,128)(2,1)S(1)}, u32[]{:S(2)}, u32[]{:S(2)}) collective-permute-start(bf16[256,512]{1,0:T(8,128)(2,1)S(1)} %collective-permute-done.5.refs_3_), channel_id=1, source_target_pairs={{0,1},{1,0},{2,3},{3,2},{4,5},{5,4},{6,7},{7,6},{8,9},{9,8},{10,11... | collective-permute-start | bytes 786440 | tf_op jit(solution)/shard_map/ppermute | solution.py:269
  23.5 5.4 %copy-start.2 = (bf16[512,512]{1,0:T(8,128)(2,1)S(1)}, bf16[512,512]{1,0:T(8,128)(2,1)}, u32[]{:S(2)}) copy-start(bf16[512,512]{1,0:T(8,128)(2,1)} %w_neigh.1) | copy-start | bytes 1572868
  23.6 5.4 %copy-start.3 = (bf16[512,512]{1,0:T(8,128)(2,1)S(1)}, bf16[512,512]{1,0:T(8,128)(2,1)}, u32[]{:S(2)}) copy-start(bf16[512,512]{1,0:T(8,128)(2,1)} %cotangent.1) | copy-start | bytes 1572868
  23.6 5.4 %copy-start.5 = (s32[512]{0:T(512)S(1)}, s32[512]{0:T(512)}, u32[]{:S(2)}) copy-start(s32[512]{0:T(512)} %param.14) | copy-start | bytes 6148
  27.4 1.5 %collective-permute-start.9 = (bf16[256,512]{1,0:T(8,128)(2,1)S(1)}, bf16[256,512]{1,0:T(8,128)(2,1)S(1)}, u32[]{:S(2)}, u32[]{:S(2)}) collective-permute-start(bf16[256,512]{1,0:T(8,128)(2,1)S(1)} %collective-permute-done.8.refs_3_), channel_id=1, source_target_pairs={{0,1},{1,0},{2,3},{3,2},{4,5},{5,4},{6,7},{7,6},{8,9},{9,8},{10,11... | collective-permute-start | bytes 786440 | tf_op jit(solution)/shard_map/ppermute | solution.py:269
  28.9 1.5 %copy-start = (bf16[1536,512]{1,0:T(8,128)(2,1)S(1)}, bf16[1536,512]{1,0:T(8,128)(2,1)}, u32[]{:S(2)}) copy-start(bf16[1536,512]{1,0:T(8,128)(2,1)} %get-tuple-element.38.mine) | copy-start | bytes 4718596
  30.3 2.0 %collective-permute-start.10 = (bf16[512,512]{1,0:T(8,128)(2,1)S(1)}, bf16[512,512]{1,0:T(8,128)(2,1)S(1)}, u32[]{:S(2)}, u32[]{:S(2)}) collective-permute-start(bf16[512,512]{1,0:T(8,128)(2,1)S(1)} %get-tuple-element.49.g), channel_id=1, source_target_pairs={{0,1},{1,0},{2,3},{3,2},{4,5},{5,4},{6,7},{7,6},{8,9},{9,8},{10,11... | collective-permute-start | bytes 1572872 | tf_op jit(solution)/shard_map/ppermute | solution.py:269
  32.7 6.4 %collective-permute-start.11 = (bf16[128,512]{1,0:T(8,128)(2,1)S(1)}, bf16[128,512]{1,0:T(8,128)(2,1)S(1)}, u32[]{:S(2)}, u32[]{:S(2)}) collective-permute-start(bf16[128,512]{1,0:T(8,128)(2,1)S(1)} %get-tuple-element.57), channel_id=1, source_target_pairs={{4,0},{14,2},{8,4},{2,6},{12,8},{6,10},{0,12},{10,14},{5,1},{15,3}... | collective-permute-start | bytes 393224 | tf_op jit(solution)/shard_map/ppermute | solution.py:266
  34.5 7.7 %collective-permute-start.13 = (bf16[128,512]{1,0:T(8,128)(2,1)S(1)}, bf16[128,512]{1,0:T(8,128)(2,1)S(1)}, u32[]{:S(2)}, u32[]{:S(2)}) collective-permute-start(bf16[128,512]{1,0:T(8,128)(2,1)S(1)} %get-tuple-element.58), channel_id=1, source_target_pairs={{4,0},{14,2},{8,4},{2,6},{12,8},{6,10},{0,12},{10,14},{5,1},{15,3}... | collective-permute-start | bytes 393224 | tf_op jit(solution)/shard_map/ppermute | solution.py:266
  34.9 10.0 %collective-permute-start.15 = (bf16[128,512]{1,0:T(8,128)(2,1)S(1)}, bf16[128,512]{1,0:T(8,128)(2,1)S(1)}, u32[]{:S(2)}, u32[]{:S(2)}) collective-permute-start(bf16[128,512]{1,0:T(8,128)(2,1)S(1)} %get-tuple-element.59), channel_id=1, source_target_pairs={{4,0},{14,2},{8,4},{2,6},{12,8},{6,10},{0,12},{10,14},{5,1},{15,3}... | collective-permute-start | bytes 393224 | tf_op jit(solution)/shard_map/ppermute | solution.py:266
  35.4 12.4 %collective-permute-start.17 = (bf16[128,512]{1,0:T(8,128)(2,1)S(1)}, bf16[128,512]{1,0:T(8,128)(2,1)S(1)}, u32[]{:S(2)}, u32[]{:S(2)}) collective-permute-start(bf16[128,512]{1,0:T(8,128)(2,1)S(1)} %get-tuple-element.60), channel_id=1, source_target_pairs={{4,0},{14,2},{8,4},{2,6},{12,8},{6,10},{0,12},{10,14},{5,1},{15,3}... | collective-permute-start | bytes 393224 | tf_op jit(solution)/shard_map/ppermute | solution.py:266
  39.1 11.0 %collective-permute-start.12 = (bf16[128,512]{1,0:T(8,128)(2,1)S(1)}, bf16[128,512]{1,0:T(8,128)(2,1)S(1)}, u32[]{:S(2)}, u32[]{:S(2)}) collective-permute-start(bf16[128,512]{1,0:T(8,128)(2,1)S(1)} %add.4), channel_id=1, source_target_pairs={{0,2},{2,0},{4,6},{6,4},{8,10},{10,8},{12,14},{14,12},{1,3},{3,1},... | collective-permute-start | bytes 393224 | tf_op jit(solution)/shard_map/ppermute | solution.py:266
  42.2 7.9 %collective-permute-start.14 = (bf16[128,512]{1,0:T(8,128)(2,1)S(1)}, bf16[128,512]{1,0:T(8,128)(2,1)S(1)}, u32[]{:S(2)}, u32[]{:S(2)}) collective-permute-start(bf16[128,512]{1,0:T(8,128)(2,1)S(1)} %add.5), channel_id=1, source_target_pairs={{0,2},{2,0},{4,6},{6,4},{8,10},{10,8},{12,14},{14,12},{1,3},{3,1},... | collective-permute-start | bytes 393224 | tf_op jit(solution)/shard_map/ppermute | solution.py:266
  45.0 5.8 %collective-permute-start.16 = (bf16[128,512]{1,0:T(8,128)(2,1)S(1)}, bf16[128,512]{1,0:T(8,128)(2,1)S(1)}, u32[]{:S(2)}, u32[]{:S(2)}) collective-permute-start(bf16[128,512]{1,0:T(8,128)(2,1)S(1)} %add.6), channel_id=1, source_target_pairs={{0,2},{2,0},{4,6},{6,4},{8,10},{10,8},{12,14},{14,12},{1,3},{3,1},... | collective-permute-start | bytes 393224 | tf_op jit(solution)/shard_map/ppermute | solution.py:266
  47.8 5.7 %collective-permute-start.18 = (bf16[128,512]{1,0:T(8,128)(2,1)S(1)}, bf16[128,512]{1,0:T(8,128)(2,1)S(1)}, u32[]{:S(2)}, u32[]{:S(2)}) collective-permute-start(bf16[128,512]{1,0:T(8,128)(2,1)S(1)} %add.7), channel_id=1, source_target_pairs={{0,2},{2,0},{4,6},{6,4},{8,10},{10,8},{12,14},{14,12},{1,3},{3,1},... | collective-permute-start | bytes 393224 | tf_op jit(solution)/shard_map/ppermute | solution.py:266

commit v6 on v5

--- a/solution.py
+++ b/solution.py
@@ -20,7 +20,7 @@
     return lax.dot_general(a, b, (((1,), (1,)), ((), ())), preferred_element_type=jnp.float32)
 
 
-def call(kernel, outs, *args, specs=None, out_specs=None, scratch=(), flops=1 << 34, name=None):
+def call(kernel, outs, *args, specs=None, out_specs=None, scratch=(), flops=1 << 34, aliases={}, name=None):
     single = not isinstance(outs, list)
     return pl.pallas_call(
         kernel,
@@ -28,6 +28,7 @@
         out_specs=out_specs or (VMEM if single else [VMEM] * len(outs)),
         out_shape=outs,
         scratch_shapes=scratch,
+        input_output_aliases=aliases,
         compiler_params=pltpu.CompilerParams(vmem_limit_bytes=12 << 20),
         cost_estimate=pl.CostEstimate(flops=flops, bytes_accessed=flops >> 8, transcendentals=0),
         name=name,
@@ -236,10 +237,10 @@
     )
 
 
-def last_kernel(own, *refs):
+def last_kernel(start, own, *refs):
     parts, (out, buffer, sem) = refs[:-3], refs[-3:]
-    stores, start = [], 0
-    for n, part in enumerate(parts):
+    stores = []
+    for n, part in enumerate(p for p in parts if p.shape[0] != out.shape[0]):
         at = pl.ds(start, part.shape[0])
         buffer[at, :] = (own[at, :] + part[...].astype(jnp.float32)).astype(out.dtype)
         store = pltpu.make_async_copy(buffer.at[at], out.at[at], sem.at[n])
@@ -336,11 +337,19 @@
         v = call(functools.partial(add_kernel, at), part, px, after(v, own_grad), name="add")
         summed.append(slab(v, pair))
         at += part.shape[0]
+    scratch = [pltpu.VMEM((rows, width), kind), pltpu.SemaphoreType.DMA((len(parts),))]
+    far = pl.BlockSpec(memory_space=pltpu.HBM)
+    most = rows - parts[-1].shape[0]
     node_grad = call(
-        last_kernel, narrow, own_grad, *summed,
-        out_specs=ANY,
-        scratch=[pltpu.VMEM((rows, width), kind), pltpu.SemaphoreType.DMA((len(parts),))],
-        name="last",
+        functools.partial(last_kernel, 0), pltpu.HBM((rows, width), kind),
+        own_grad, *summed[:-1],
+        out_specs=far, scratch=scratch, name="most",
+    )
+    node_grad = call(
+        functools.partial(last_kernel, most), pltpu.HBM((rows, width), kind),
+        own_grad, summed[-1], node_grad,
+        specs=[VMEM, VMEM, far], out_specs=far, scratch=scratch,
+        aliases={2: 0}, name="last",
     )
     return (node_out, node_grad)
 

time: 54.5 us -> 54.4 us (level)
  waiting for transfers between devices: 15.8 us -> 15 us
  Pallas kernels: 13.9 us -> 14.6 us
    ppermute x12, waiting for transfers between devices: 12.8 us -> 12 us  [slab(): return lax.ppermute(v, 'slab', route)]
    pallas_call x16 -> x17, Pallas kernels: 13.9 us -> 14.6 us  [call(): pl.pallas_call(kernel, in_specs=specs or [VMEM] * len(args), out_specs=ou...]
  transfers between devices with their start and end apart: 19 -> 19, of which waited for: 10 -> 10; matrix products, arithmetic and copies ran while one was open for 0% -> 0% of each run, Pallas kernels for 21% -> 22%
where the time goes in v6:
time: 54.4 us; the launch traced here: 54.2 us
  starting transfers between devices  23.8 us (44%)
  waiting for transfers between devices  15 us (28%)
  Pallas kernels  14.6 us (27%)
  between operations  0.81 us (1%)
    ppermute x12, starting transfers between devices, slab(): return lax.ppermute(v, 'slab', route)  22.4 us
    pallas_call x17, Pallas kernels, call(): pl.pallas_call(kernel, in_specs=specs or [VMEM] * len(args), out_specs=ou...  14.6 us
    ppermute x12, waiting for transfers between devices, slab(): return lax.ppermute(v, 'slab', route)  12 us
    ppermute x7, waiting for transfers between devices, sub(): return lax.ppermute(v, 'sub', swap)  3 us
    ppermute x7, starting transfers between devices, sub(): return lax.ppermute(v, 'sub', swap)  1.38 us
  transfers between devices with their start and end apart: 19, of which 10 were waited for; matrix products, arithmetic and copies ran while one was open for 0% of the time, Pallas kernels for 22%

profile of v6, /device:TPU:0, one launch (start us, length us, event | category | flops | bytes accessed | tf_op | source)
XLA Modules:
  0.0 54.2 jit_solution(18006413711867502255)
XLA Ops:
  0.6 0.5 collective-permute-start
  1.1 1.0 %split.1 = (bf16[256,512]{1,0:T(8,128)(2,1)S(1)}, bf16[256,512]{1,0:T(8,128)(2,1)S(1)}) custom-call(bf16[512,512]{1,0:T(8,128)(2,1)} %x.3), custom_call_target="tpu_custom_call" | custom-call | flops 17179869184 | bytes 67108864 | tf_op jit(solution)/shard_map/split/pallas_call | solution.py:25
  2.2 2.6 %collective-permute-start.1 = (bf16[256,512]{1,0:T(8,128)(2,1)S(1)}, bf16[256,512]{1,0:T(8,128)(2,1)S(1)}, u32[]{:S(2)}, u32[]{:S(2)}) collective-permute-start(bf16[256,512]{1,0:T(8,128)(2,1)S(1)} %get-tuple-element.35), channel_id=1, source_target_pairs={{0,2},{2,0},{4,6},{6,4},{8,10},{10,8},{12,14},{14,12},{1,3},{3,1},... | collective-permute-start | bytes 786440 | tf_op jit(solution)/shard_map/ppermute | solution.py:267
  4.8 0.1 collective-permute-start.3
  4.8 0.0 collective-permute-done.x_sib
  4.9 1.5 %dense_pair.1.refs_0_.refs_1_.refs_2_ = bf16[512,1024]{1,0:T(8,128)(2,1)S(1)} custom-call(s32[3,4,6]{2,1,0:T(4,128)} %bitcast.4, s32[3,4,6]{2,1,0:T(4,128)} %bitcast.6, bf16[4,3,6,128,128]{4,3,2,1,0:T(8,128)(2,1)} %tiles.3), custom_call_target="tpu_custom_call" | custom-call | flops 67108864 | bytes 262144 | tf_op jit(solution)/shard_map/dense_pair/pallas_call | solution.py:25
  6.4 0.0 copy-start.1
  6.4 0.0 copy-start.4
  6.4 3.9 %dense_across.1 = (bf16[512,1024]{1,0:T(8,128)(2,1)S(1)}, bf16[512,1024]{1,0:T(8,128)(2,1)S(1)}, bf16[1536,512]{1,0:T(8,128)(2,1)}, bf16[1536,512]{1,0:T(8,128)(2,1)}) custom-call(s32[3,4,6]{2,1,0:T(4,128)} %bitcast.5, s32[3,4,6]{2,1,0:T(4,128)} %bitcast.7, bf16[4,3,6,128,128]{4,3,2,1,0:T(8,128)(2,1)} %tiles.3, ...), custom_call_target="tpu_custom_call" | custom-call | flops 134217728 | bytes 524288 | tf_op jit(solution)/shard_map/dense_across/pallas_call | solution.py:25
  10.3 1.6 %collective-permute-done.1.refs_3_ = bf16[256,512]{1,0:T(8,128)(2,1)S(1)} collective-permute-done((bf16[256,512]{1,0:T(8,128)(2,1)S(1)}, bf16[256,512]{1,0:T(8,128)(2,1)S(1)}, u32[]{:S(2)}, u32[]{:S(2)}) %collective-permute-start.1) | collective-permute-done | bytes 262176 | tf_op jit(solution)/shard_map/ppermute | solution.py:267
  11.9 2.0 %collective-permute-start.5 = (bf16[256,512]{1,0:T(8,128)(2,1)S(1)}, bf16[256,512]{1,0:T(8,128)(2,1)S(1)}, u32[]{:S(2)}, u32[]{:S(2)}) collective-permute-start(bf16[256,512]{1,0:T(8,128)(2,1)S(1)} %collective-permute-done.1.refs_3_), channel_id=1, source_target_pairs={{0,4},{2,14},{4,8},{6,2},{8,12},{10,6},{12,0},{14,10},{1,5},{3,15}... | collective-permute-start | bytes 786440 | tf_op jit(solution)/shard_map/ppermute | solution.py:267
  14.0 0.0 collective-permute-start.2
  14.0 1.0 %local.1 = (f32[512,512]{1,0:T(8,128)S(1)}, f32[512,512]{1,0:T(8,128)S(1)}) custom-call(bf16[512,1024]{1,0:T(8,128)(2,1)S(1)} %get-tuple-element.39.adj, bf16[512,512]{1,0:T(8,128)(2,1)S(1)} %copy-done.1, bf16[512,512]{1,0:T(8,128)(2,1)S(1)} %collective-permute-done.x_sib, bf16[512,512]{1,0:T(8,128)(2,1)S(1)} %copy-done.4), custom_call_target="tpu_custom_call" | custom-call | flops 17179869184 | bytes 67108864 | tf_op jit(solution)/shard_map/local/pallas_call | solution.py:25
  15.0 2.4 %collective-permute-done.3.refs_5_ = bf16[256,512]{1,0:T(8,128)(2,1)S(1)} collective-permute-done((bf16[256,512]{1,0:T(8,128)(2,1)S(1)}, bf16[256,512]{1,0:T(8,128)(2,1)S(1)}, u32[]{:S(2)}, u32[]{:S(2)}) %collective-permute-start.3) | collective-permute-done | bytes 262176 | tf_op jit(solution)/shard_map/ppermute | solution.py:267
  17.4 1.8 %collective-permute-start.8 = (bf16[256,512]{1,0:T(8,128)(2,1)S(1)}, bf16[256,512]{1,0:T(8,128)(2,1)S(1)}, u32[]{:S(2)}, u32[]{:S(2)}) collective-permute-start(bf16[256,512]{1,0:T(8,128)(2,1)S(1)} %collective-permute-done.3.refs_5_), channel_id=1, source_target_pairs={{0,4},{2,14},{4,8},{6,2},{8,12},{10,6},{12,0},{14,10},{1,5},{3,15}... | collective-permute-start | bytes 786440 | tf_op jit(solution)/shard_map/ppermute | solution.py:267
  19.2 0.5 collective-permute-start.6
  19.7 0.0 collective-permute-done.2.refs_4_
  19.7 0.6 %gather.3.messages = f32[512,512]{1,0:T(8,128)S(1)} custom-call(f32[512,512]{1,0:T(8,128)S(1)} %get-tuple-element.40.messages, bf16[512,1024]{1,0:T(8,128)(2,1)S(1)} %dense_pair.1.refs_0_.refs_1_.refs_2_, bf16[512,1024]{1,0:T(8,128)(2,1)S(1)} %dense_pair.1.refs_0_.refs_1_.refs_2_, bf16[512,1024]{1,0:T(8,128)(2,1)S(1)} %dense_pair.1.refs_0_.refs_1_.refs_2_, ...), custom_call_target="tpu_custom_call" | custom-call | flops 17179869184 | bytes 67108864 | tf_op jit(solution)/shard_map/gather/pallas_call | solution.py:25
  20.3 1.5 %collective-permute-done.5.refs_3_ = bf16[256,512]{1,0:T(8,128)(2,1)S(1)} collective-permute-done((bf16[256,512]{1,0:T(8,128)(2,1)S(1)}, bf16[256,512]{1,0:T(8,128)(2,1)S(1)}, u32[]{:S(2)}, u32[]{:S(2)}) %collective-permute-start.5) | collective-permute-done | bytes 262176 | tf_op jit(solution)/shard_map/ppermute | solution.py:267
  21.8 1.2 %collective-permute-done.6.theirs = bf16[1536,512]{1,0:T(8,128)(2,1)S(1)} collective-permute-done((bf16[1536,512]{1,0:T(8,128)(2,1)S(1)}, bf16[1536,512]{1,0:T(8,128)(2,1)S(1)}, u32[]{:S(2)}, u32[]{:S(2)}) %collective-permute-start.6) | collective-permute-done | bytes 1572896 | tf_op jit(solution)/shard_map/ppermute | solution.py:270
  23.0 0.1 collective-permute-start.7
  23.1 0.4 gather.4.messages
  23.5 0.0 copy-start.2
  23.6 0.0 copy-start.3
  23.6 0.0 copy-start.5
  23.6 3.8 %collective-permute-done.8.refs_3_ = bf16[256,512]{1,0:T(8,128)(2,1)S(1)} collective-permute-done((bf16[256,512]{1,0:T(8,128)(2,1)S(1)}, bf16[256,512]{1,0:T(8,128)(2,1)S(1)}, u32[]{:S(2)}, u32[]{:S(2)}) %collective-permute-start.8) | collective-permute-done | bytes 262176 | tf_op jit(solution)/shard_map/ppermute | solution.py:267
  27.4 0.4 gather.5.messages
  27.8 1.1 %collective-permute-done.9.last = bf16[256,512]{1,0:T(8,128)(2,1)S(1)} collective-permute-done((bf16[256,512]{1,0:T(8,128)(2,1)S(1)}, bf16[256,512]{1,0:T(8,128)(2,1)S(1)}, u32[]{:S(2)}, u32[]{:S(2)}) %collective-permute-start.9) | collective-permute-done | bytes 262176 | tf_op jit(solution)/shard_map/ppermute | solution.py:270
  28.9 1.3 %middle.1 = (bf16[512,512]{1,0:T(8,128)(2,1)S(1)}, bf16[512,512]{1,0:T(8,128)(2,1)S(1)}, bf16[512,512]{1,0:T(8,128)(2,1)S(1)}) custom-call(f32[512,512]{1,0:T(8,128)S(1)} %gather.5.messages, f32[512,512]{1,0:T(8,128)S(1)} %get-tuple-element.48.own, bf16[512,1024]{1,0:T(8,128)(2,1)S(1)} %get-tuple-element.41.refs_1_.refs_0_.adj, ...), custom_call_target="tpu_custom_call" | custom-call | flops 17179869184 | bytes 67108864 | tf_op jit(solution)/shard_map/middle/pallas_call | solution.py:25
  30.3 0.2 collective-permute-start.10
  30.5 1.0 %first.1 = (f32[512,512]{1,0:T(8,128)S(1)}, f32[512,512]{1,0:T(8,128)S(1)}, bf16[1024,512]{1,0:T(8,128)(2,1)S(1)}, bf16[512,512]{1,0:T(8,128)(2,1)}) custom-call(bf16[1536,512]{1,0:T(8,128)(2,1)S(1)} %copy-done, bf16[512,512]{1,0:T(8,128)(2,1)S(1)} %get-tuple-element.49.g, bf16[1536,512]{1,0:T(8,128)(2,1)S(1)} %collective-permute-done.6.theirs, ...), custom_call_target="tpu_custom_call" | custom-call | flops 17179869184 | bytes 67108864 | tf_op jit(solution)/shard_map/first/pallas_call | solution.py:25
  31.5 0.7 %collective-permute-done.10.g_sib = bf16[512,512]{1,0:T(8,128)(2,1)S(1)} collective-permute-done((bf16[512,512]{1,0:T(8,128)(2,1)S(1)}, bf16[512,512]{1,0:T(8,128)(2,1)S(1)}, u32[]{:S(2)}, u32[]{:S(2)}) %collective-permute-start.10) | collective-permute-done | bytes 524320 | tf_op jit(solution)/shard_map/ppermute | solution.py:270
  32.2 0.4 across.1
  32.7 1.8 %collective-permute-start.13 = (bf16[128,512]{1,0:T(8,128)(2,1)S(1)}, bf16[128,512]{1,0:T(8,128)(2,1)S(1)}, u32[]{:S(2)}, u32[]{:S(2)}) collective-permute-start(bf16[128,512]{1,0:T(8,128)(2,1)S(1)} %get-tuple-element.57), channel_id=1, source_target_pairs={{4,0},{14,2},{8,4},{2,6},{12,8},{6,10},{0,12},{10,14},{5,1},{15,3}... | collective-permute-start | bytes 393224 | tf_op jit(solution)/shard_map/ppermute | solution.py:267
  34.5 0.4 collective-permute-start.15
  34.9 0.5 collective-permute-start.17
  35.4 2.3 %collective-permute-start.11 = (bf16[128,512]{1,0:T(8,128)(2,1)S(1)}, bf16[128,512]{1,0:T(8,128)(2,1)S(1)}, u32[]{:S(2)}, u32[]{:S(2)}) collective-permute-start(bf16[128,512]{1,0:T(8,128)(2,1)S(1)} %get-tuple-element.60), channel_id=1, source_target_pairs={{4,0},{14,2},{8,4},{2,6},{12,8},{6,10},{0,12},{10,14},{5,1},{15,3}... | collective-permute-start | bytes 393224 | tf_op jit(solution)/shard_map/ppermute | solution.py:267
  37.7 1.3 %own.1 = (f32[512,512]{1,0:T(8,128)S(1)}, f32[512,512]{1,0:T(8,128)S(1)}) custom-call(bf16[1536,512]{1,0:T(8,128)(2,1)S(1)} %copy-done, bf16[1536,512]{1,0:T(8,128)(2,1)S(1)} %collective-permute-done.6.theirs, bf16[1024,512]{1,0:T(8,128)(2,1)S(1)} %get-tuple-element.53.theirs.near, bf16[512,512]{1,0:T(8,128)(2,1)S(1)} %get-tuple-element.49.g, ...), custom_call_target="tpu_custom_call" | custom-call | flops 17179869184 | bytes 67108864 | tf_op jit(solution)/shard_map/own/pallas_call | solution.py:25
  38.9 0.1 collective-permute-done.13.b
  39.1 3.0 %collective-permute-start.14 = (bf16[128,512]{1,0:T(8,128)(2,1)S(1)}, bf16[128,512]{1,0:T(8,128)(2,1)S(1)}, u32[]{:S(2)}, u32[]{:S(2)}) collective-permute-start(bf16[128,512]{1,0:T(8,128)(2,1)S(1)} %add.5), channel_id=1, source_target_pairs={{0,2},{2,0},{4,6},{6,4},{8,10},{10,8},{12,14},{14,12},{1,3},{3,1},... | collective-permute-start | bytes 393224 | tf_op jit(solution)/shard_map/ppermute | solution.py:267
  42.1 0.0 collective-permute-done.15.b
  42.2 2.8 %collective-permute-start.16 = (bf16[128,512]{1,0:T(8,128)(2,1)S(1)}, bf16[128,512]{1,0:T(8,128)(2,1)S(1)}, u32[]{:S(2)}, u32[]{:S(2)}) collective-permute-start(bf16[128,512]{1,0:T(8,128)(2,1)S(1)} %add.6), channel_id=1, source_target_pairs={{0,2},{2,0},{4,6},{6,4},{8,10},{10,8},{12,14},{14,12},{1,3},{3,1},... | collective-permute-start | bytes 393224 | tf_op jit(solution)/shard_map/ppermute | solution.py:267
  45.0 2.8 %collective-permute-start.18 = (bf16[128,512]{1,0:T(8,128)(2,1)S(1)}, bf16[128,512]{1,0:T(8,128)(2,1)S(1)}, u32[]{:S(2)}, u32[]{:S(2)}) collective-permute-start(bf16[128,512]{1,0:T(8,128)(2,1)S(1)} %add.7), channel_id=1, source_target_pairs={{0,2},{2,0},{4,6},{6,4},{8,10},{10,8},{12,14},{14,12},{1,3},{3,1},... | collective-permute-start | bytes 393224 | tf_op jit(solution)/shard_map/ppermute | solution.py:267
  47.8 2.3 %collective-permute-start.12 = (bf16[128,512]{1,0:T(8,128)(2,1)S(1)}, bf16[128,512]{1,0:T(8,128)(2,1)S(1)}, u32[]{:S(2)}, u32[]{:S(2)}) collective-permute-start(bf16[128,512]{1,0:T(8,128)(2,1)S(1)} %add.4), channel_id=1, source_target_pairs={{0,2},{2,0},{4,6},{6,4},{8,10},{10,8},{12,14},{14,12},{1,3},{3,1},... | collective-permute-start | bytes 393224 | tf_op jit(solution)/shard_map/ppermute | solution.py:267
  50.1 0.7 %collective-permute-done.18.refs_2_ = bf16[128,512]{1,0:T(8,128)(2,1)S(1)} collective-permute-done((bf16[128,512]{1,0:T(8,128)(2,1)S(1)}, bf16[128,512]{1,0:T(8,128)(2,1)S(1)}, u32[]{:S(2)}, u32[]{:S(2)}) %collective-permute-start.18) | collective-permute-done | bytes 131104 | tf_op jit(solution)/shard_map/ppermute | solution.py:267
  50.8 0.8 %most.1.refs_1_ = bf16[512,512]{1,0:T(8,128)(2,1)} custom-call(f32[512,512]{1,0:T(8,128)S(1)} %get-tuple-element.62.own, bf16[128,512]{1,0:T(8,128)(2,1)S(1)} %collective-permute-done.14.refs_0_, bf16[128,512]{1,0:T(8,128)(2,1)S(1)} %collective-permute-done.16.refs_1_, bf16[128,512]{1,0:T(8,128)(2,1)S(1)} %collective-permute-done.18.refs_2_), custom_call_target="tpu_custom_call" | custom-call | flops 17179869184 | bytes 67108864 | tf_op jit(solution)/shard_map/most/pallas_call | solution.py:25
  51.6 1.9 %collective-permute-done.12.refs_0_ = bf16[128,512]{1,0:T(8,128)(2,1)S(1)} collective-permute-done((bf16[128,512]{1,0:T(8,128)(2,1)S(1)}, bf16[128,512]{1,0:T(8,128)(2,1)S(1)}, u32[]{:S(2)}, u32[]{:S(2)}) %collective-permute-start.12) | collective-permute-done | bytes 131104 | tf_op jit(solution)/shard_map/ppermute | solution.py:267
  53.5 0.7 %last.1 = bf16[512,512]{1,0:T(8,128)(2,1)} custom-call(f32[512,512]{1,0:T(8,128)S(1)} %get-tuple-element.62.own, bf16[128,512]{1,0:T(8,128)(2,1)S(1)} %collective-permute-done.12.refs_0_, bf16[512,512]{1,0:T(8,128)(2,1)} %most.1.refs_1_), custom_call_target="tpu_custom_call", output_to_operand_aliasing={{}: (2, {})} | custom-call | flops 17179869184 | bytes 67108864 | tf_op jit(solution)/shard_map/last/pallas_call | solution.py:25
  (21 shorter events, 0.1 us)
Async XLA Ops:
  0.6 4.2 %collective-permute-start = (bf16[512,512]{1,0:T(8,128)(2,1)}, bf16[512,512]{1,0:T(8,128)(2,1)S(1)}, u32[]{:S(2)}, u32[]{:S(2)}) collective-permute-start(bf16[512,512]{1,0:T(8,128)(2,1)} %x.3), channel_id=1, source_target_pairs={{0,1},{1,0},{2,3},{3,2},{4,5},{5,4},{6,7},{7,6},{8,9},{9,8},{10,11... | collective-permute-start | bytes 1572872 | tf_op jit(solution)/shard_map/ppermute | solution.py:270
  2.2 9.7 %collective-permute-start.1 = (bf16[256,512]{1,0:T(8,128)(2,1)S(1)}, bf16[256,512]{1,0:T(8,128)(2,1)S(1)}, u32[]{:S(2)}, u32[]{:S(2)}) collective-permute-start(bf16[256,512]{1,0:T(8,128)(2,1)S(1)} %get-tuple-element.35), channel_id=1, source_target_pairs={{0,2},{2,0},{4,6},{6,4},{8,10},{10,8},{12,14},{14,12},{1,3},{3,1},... | collective-permute-start | bytes 786440 | tf_op jit(solution)/shard_map/ppermute | solution.py:267
  4.8 12.6 %collective-permute-start.3 = (bf16[256,512]{1,0:T(8,128)(2,1)S(1)}, bf16[256,512]{1,0:T(8,128)(2,1)S(1)}, u32[]{:S(2)}, u32[]{:S(2)}) collective-permute-start(bf16[256,512]{1,0:T(8,128)(2,1)S(1)} %get-tuple-element.43), channel_id=1, source_target_pairs={{0,2},{2,0},{4,6},{6,4},{8,10},{10,8},{12,14},{14,12},{1,3},{3,1},... | collective-permute-start | bytes 786440 | tf_op jit(solution)/shard_map/ppermute | solution.py:267
  6.4 7.6 %copy-start.1 = (bf16[512,512]{1,0:T(8,128)(2,1)S(1)}, bf16[512,512]{1,0:T(8,128)(2,1)}, u32[]{:S(2)}) copy-start(bf16[512,512]{1,0:T(8,128)(2,1)} %x.3) | copy-start | bytes 1572868
  6.4 7.6 %copy-start.4 = (bf16[512,512]{1,0:T(8,128)(2,1)S(1)}, bf16[512,512]{1,0:T(8,128)(2,1)}, u32[]{:S(2)}) copy-start(bf16[512,512]{1,0:T(8,128)(2,1)} %w_self.3) | copy-start | bytes 1572868
  11.9 9.8 %collective-permute-start.5 = (bf16[256,512]{1,0:T(8,128)(2,1)S(1)}, bf16[256,512]{1,0:T(8,128)(2,1)S(1)}, u32[]{:S(2)}, u32[]{:S(2)}) collective-permute-start(bf16[256,512]{1,0:T(8,128)(2,1)S(1)} %collective-permute-done.1.refs_3_), channel_id=1, source_target_pairs={{0,4},{2,14},{4,8},{6,2},{8,12},{10,6},{12,0},{14,10},{1,5},{3,15}... | collective-permute-start | bytes 786440 | tf_op jit(solution)/shard_map/ppermute | solution.py:267
  14.0 5.7 %collective-permute-start.2 = (bf16[256,512]{1,0:T(8,128)(2,1)S(1)}, bf16[256,512]{1,0:T(8,128)(2,1)S(1)}, u32[]{:S(2)}, u32[]{:S(2)}) collective-permute-start(bf16[256,512]{1,0:T(8,128)(2,1)S(1)} %collective-permute-done.1.refs_3_), channel_id=1, source_target_pairs={{0,1},{1,0},{2,3},{3,2},{4,5},{5,4},{6,7},{7,6},{8,9},{9,8},{10,11... | collective-permute-start | bytes 786440 | tf_op jit(solution)/shard_map/ppermute | solution.py:270
  14.0 5.2 %copy-start.6 = (bf16[1536,512]{1,0:T(8,128)(2,1)S(1)}, bf16[1536,512]{1,0:T(8,128)(2,1)}, u32[]{:S(2)}) copy-start(bf16[1536,512]{1,0:T(8,128)(2,1)} %get-tuple-element.45) | copy-start | bytes 4718596
  17.4 10.0 %collective-permute-start.8 = (bf16[256,512]{1,0:T(8,128)(2,1)S(1)}, bf16[256,512]{1,0:T(8,128)(2,1)S(1)}, u32[]{:S(2)}, u32[]{:S(2)}) collective-permute-start(bf16[256,512]{1,0:T(8,128)(2,1)S(1)} %collective-permute-done.3.refs_5_), channel_id=1, source_target_pairs={{0,4},{2,14},{4,8},{6,2},{8,12},{10,6},{12,0},{14,10},{1,5},{3,15}... | collective-permute-start | bytes 786440 | tf_op jit(solution)/shard_map/ppermute | solution.py:267
  19.2 3.9 %collective-permute-start.4 = (bf16[256,512]{1,0:T(8,128)(2,1)S(1)}, bf16[256,512]{1,0:T(8,128)(2,1)S(1)}, u32[]{:S(2)}, u32[]{:S(2)}) collective-permute-start(bf16[256,512]{1,0:T(8,128)(2,1)S(1)} %collective-permute-done.3.refs_5_), channel_id=1, source_target_pairs={{0,1},{1,0},{2,3},{3,2},{4,5},{5,4},{6,7},{7,6},{8,9},{9,8},{10,11... | collective-permute-start | bytes 786440 | tf_op jit(solution)/shard_map/ppermute | solution.py:270
  19.2 3.8 %collective-permute-start.6 = (bf16[1536,512]{1,0:T(8,128)(2,1)S(1)}, bf16[1536,512]{1,0:T(8,128)(2,1)S(1)}, u32[]{:S(2)}, u32[]{:S(2)}) collective-permute-start(bf16[1536,512]{1,0:T(8,128)(2,1)S(1)} %copy-done.6), channel_id=1, source_target_pairs={{0,1},{1,0},{2,3},{3,2},{4,5},{5,4},{6,7},{7,6},{8,9},{9,8},{10,11... | collective-permute-start | bytes 4718600 | tf_op jit(solution)/shard_map/ppermute | solution.py:270
  23.0 4.4 %collective-permute-start.7 = (bf16[256,512]{1,0:T(8,128)(2,1)S(1)}, bf16[256,512]{1,0:T(8,128)(2,1)S(1)}, u32[]{:S(2)}, u32[]{:S(2)}) collective-permute-start(bf16[256,512]{1,0:T(8,128)(2,1)S(1)} %collective-permute-done.5.refs_3_), channel_id=1, source_target_pairs={{0,1},{1,0},{2,3},{3,2},{4,5},{5,4},{6,7},{7,6},{8,9},{9,8},{10,11... | collective-permute-start | bytes 786440 | tf_op jit(solution)/shard_map/ppermute | solution.py:270
  23.5 5.4 %copy-start.2 = (bf16[512,512]{1,0:T(8,128)(2,1)S(1)}, bf16[512,512]{1,0:T(8,128)(2,1)}, u32[]{:S(2)}) copy-start(bf16[512,512]{1,0:T(8,128)(2,1)} %w_neigh.1) | copy-start | bytes 1572868
  23.6 5.4 %copy-start.3 = (bf16[512,512]{1,0:T(8,128)(2,1)S(1)}, bf16[512,512]{1,0:T(8,128)(2,1)}, u32[]{:S(2)}) copy-start(bf16[512,512]{1,0:T(8,128)(2,1)} %cotangent.1) | copy-start | bytes 1572868
  23.6 5.4 %copy-start.5 = (s32[512]{0:T(512)S(1)}, s32[512]{0:T(512)}, u32[]{:S(2)}) copy-start(s32[512]{0:T(512)} %param.14) | copy-start | bytes 6148
  27.4 1.5 %collective-permute-start.9 = (bf16[256,512]{1,0:T(8,128)(2,1)S(1)}, bf16[256,512]{1,0:T(8,128)(2,1)S(1)}, u32[]{:S(2)}, u32[]{:S(2)}) collective-permute-start(bf16[256,512]{1,0:T(8,128)(2,1)S(1)} %collective-permute-done.8.refs_3_), channel_id=1, source_target_pairs={{0,1},{1,0},{2,3},{3,2},{4,5},{5,4},{6,7},{7,6},{8,9},{9,8},{10,11... | collective-permute-start | bytes 786440 | tf_op jit(solution)/shard_map/ppermute | solution.py:270
  28.9 1.5 %copy-start = (bf16[1536,512]{1,0:T(8,128)(2,1)S(1)}, bf16[1536,512]{1,0:T(8,128)(2,1)}, u32[]{:S(2)}) copy-start(bf16[1536,512]{1,0:T(8,128)(2,1)} %get-tuple-element.38.mine) | copy-start | bytes 4718596
  30.3 2.0 %collective-permute-start.10 = (bf16[512,512]{1,0:T(8,128)(2,1)S(1)}, bf16[512,512]{1,0:T(8,128)(2,1)S(1)}, u32[]{:S(2)}, u32[]{:S(2)}) collective-permute-start(bf16[512,512]{1,0:T(8,128)(2,1)S(1)} %get-tuple-element.49.g), channel_id=1, source_target_pairs={{0,1},{1,0},{2,3},{3,2},{4,5},{5,4},{6,7},{7,6},{8,9},{9,8},{10,11... | collective-permute-start | bytes 1572872 | tf_op jit(solution)/shard_map/ppermute | solution.py:270
  32.7 6.4 %collective-permute-start.13 = (bf16[128,512]{1,0:T(8,128)(2,1)S(1)}, bf16[128,512]{1,0:T(8,128)(2,1)S(1)}, u32[]{:S(2)}, u32[]{:S(2)}) collective-permute-start(bf16[128,512]{1,0:T(8,128)(2,1)S(1)} %get-tuple-element.57), channel_id=1, source_target_pairs={{4,0},{14,2},{8,4},{2,6},{12,8},{6,10},{0,12},{10,14},{5,1},{15,3}... | collective-permute-start | bytes 393224 | tf_op jit(solution)/shard_map/ppermute | solution.py:267
  34.5 7.7 %collective-permute-start.15 = (bf16[128,512]{1,0:T(8,128)(2,1)S(1)}, bf16[128,512]{1,0:T(8,128)(2,1)S(1)}, u32[]{:S(2)}, u32[]{:S(2)}) collective-permute-start(bf16[128,512]{1,0:T(8,128)(2,1)S(1)} %get-tuple-element.58), channel_id=1, source_target_pairs={{4,0},{14,2},{8,4},{2,6},{12,8},{6,10},{0,12},{10,14},{5,1},{15,3}... | collective-permute-start | bytes 393224 | tf_op jit(solution)/shard_map/ppermute | solution.py:267
  34.9 10.0 %collective-permute-start.17 = (bf16[128,512]{1,0:T(8,128)(2,1)S(1)}, bf16[128,512]{1,0:T(8,128)(2,1)S(1)}, u32[]{:S(2)}, u32[]{:S(2)}) collective-permute-start(bf16[128,512]{1,0:T(8,128)(2,1)S(1)} %get-tuple-element.59), channel_id=1, source_target_pairs={{4,0},{14,2},{8,4},{2,6},{12,8},{6,10},{0,12},{10,14},{5,1},{15,3}... | collective-permute-start | bytes 393224 | tf_op jit(solution)/shard_map/ppermute | solution.py:267
  35.4 12.4 %collective-permute-start.11 = (bf16[128,512]{1,0:T(8,128)(2,1)S(1)}, bf16[128,512]{1,0:T(8,128)(2,1)S(1)}, u32[]{:S(2)}, u32[]{:S(2)}) collective-permute-start(bf16[128,512]{1,0:T(8,128)(2,1)S(1)} %get-tuple-element.60), channel_id=1, source_target_pairs={{4,0},{14,2},{8,4},{2,6},{12,8},{6,10},{0,12},{10,14},{5,1},{15,3}... | collective-permute-start | bytes 393224 | tf_op jit(solution)/shard_map/ppermute | solution.py:267
  39.1 11.0 %collective-permute-start.14 = (bf16[128,512]{1,0:T(8,128)(2,1)S(1)}, bf16[128,512]{1,0:T(8,128)(2,1)S(1)}, u32[]{:S(2)}, u32[]{:S(2)}) collective-permute-start(bf16[128,512]{1,0:T(8,128)(2,1)S(1)} %add.5), channel_id=1, source_target_pairs={{0,2},{2,0},{4,6},{6,4},{8,10},{10,8},{12,14},{14,12},{1,3},{3,1},... | collective-permute-start | bytes 393224 | tf_op jit(solution)/shard_map/ppermute | solution.py:267
  42.2 7.9 %collective-permute-start.16 = (bf16[128,512]{1,0:T(8,128)(2,1)S(1)}, bf16[128,512]{1,0:T(8,128)(2,1)S(1)}, u32[]{:S(2)}, u32[]{:S(2)}) collective-permute-start(bf16[128,512]{1,0:T(8,128)(2,1)S(1)} %add.6), channel_id=1, source_target_pairs={{0,2},{2,0},{4,6},{6,4},{8,10},{10,8},{12,14},{14,12},{1,3},{3,1},... | collective-permute-start | bytes 393224 | tf_op jit(solution)/shard_map/ppermute | solution.py:267
  45.0 5.8 %collective-permute-start.18 = (bf16[128,512]{1,0:T(8,128)(2,1)S(1)}, bf16[128,512]{1,0:T(8,128)(2,1)S(1)}, u32[]{:S(2)}, u32[]{:S(2)}) collective-permute-start(bf16[128,512]{1,0:T(8,128)(2,1)S(1)} %add.7), channel_id=1, source_target_pairs={{0,2},{2,0},{4,6},{6,4},{8,10},{10,8},{12,14},{14,12},{1,3},{3,1},... | collective-permute-start | bytes 393224 | tf_op jit(solution)/shard_map/ppermute | solution.py:267
  47.8 5.7 %collective-permute-start.12 = (bf16[128,512]{1,0:T(8,128)(2,1)S(1)}, bf16[128,512]{1,0:T(8,128)(2,1)S(1)}, u32[]{:S(2)}, u32[]{:S(2)}) collective-permute-start(bf16[128,512]{1,0:T(8,128)(2,1)S(1)} %add.4), channel_id=1, source_target_pairs={{0,2},{2,0},{4,6},{6,4},{8,10},{10,8},{12,14},{14,12},{1,3},{3,1},... | collective-permute-start | bytes 393224 | tf_op jit(solution)/shard_map/ppermute | solution.py:267
